TPU v7x, 128 devices: a whole 4x4x4 slice. The times are simulated.
128 devices in a mesh: gy: 8 (over z, x_hi), gx: 16 (over y, x_lo, core).
Axes of the slice: x: 4 (x_hi: 2, x_lo: 2; x = x_hi * 2 + x_lo), y: 4, z: 4, core: 2. Of those that a mesh axis runs over, the one named last changes fastest.
Arguments:
- tiles: bfloat16 [16384, 128, 128], P(('gy', 'gx')), may hold values from 0.19921875 to 5
- tile_dest: int32 [16384, 1], P(('gy', 'gx')), may hold values from 0 to 127, as said below
- tile_slot: int32 [16384], P(('gy', 'gx')), may hold values from 0 to 191
- psf: float32 [6, 3, 31], replicated, may hold values from 0.05 to 1
- estimate: float32 [32, 1024, 2048], P(None, 'gy', 'gx'), may hold values from 0.5 to 2
Outputs:
- restored: float32 [32, 1024, 2048], P(None, 'gy', 'gx')
Inputs may be any that keep to these rules, and one draw needn't show every extreme that they name: `tile_dest`: among the 128 tiles held by one device no brick is named more than 2 times; in every draw some brick is named exactly 2 times by the tiles of every device.
All inputs are finite; a program needn't handle non-finite values.
Results may differ from a plain program's by a relative error of at most 0.00069.
Values may be sent and summed in bfloat16 or wider, within the bound.
No kernel may reach another device: no remote copies, remote signals or barrier semaphores. Data moves between devices by JAX's collectives and lax.ppermute only.
A program may use at most 192 MiB of HBM per device.

v0:
```python
import jax
import jax.numpy as jnp
from jax import lax
from jax.experimental import pallas as pl
from jax.experimental.pallas import tpu as pltpu
from jax.sharding import PartitionSpec as P

ITERS = 2
DAMPING = 0.05
VIEWS = 6
TAPS = 31
REACH = 15
CZ = 32
SIDE = 128
RIM = 16
EXT = SIDE + 2 * RIM
GROUPS = SIDE // RIM
ZPER = CZ // GROUPS
SLOTS = 2
HALF_TILE = 8
UX, UY, UZ, UB, UE = 2, 16, 8, 16, 2
VMEM_LIMIT = 56 * 1024 * 1024


def shift(values, axis, step):
    count = lax.axis_size(axis)
    pairs = [(i, i + step) for i in range(count) if 0 <= i + step < count]
    return lax.ppermute(values, axis, pairs)


def lanes(shape):
    return lax.broadcasted_iota(jnp.int32, shape, len(shape) - 1)


def pack_body(dest_ref, tiles_ref, labels_ref, out_ref, seen_ref, tile_sem, label_sem):
    count = tiles_ref.shape[0]
    devices = out_ref.shape[0]
    named = pltpu.make_async_copy(
        labels_ref, out_ref.at[:, pl.ds(SLOTS * SIDE, HALF_TILE)], label_sem
    )
    named.start()

    @pl.loop(0, devices)
    def _(i):
        seen_ref[i] = 0

    @pl.loop(0, count)
    def _(i):
        target = dest_ref[i]
        rank = seen_ref[target]
        seen_ref[target] = rank + 1
        pltpu.make_async_copy(
            tiles_ref.at[i], out_ref.at[target, pl.ds(rank * SIDE, SIDE)], tile_sem
        ).start()

    every = out_ref.at[pl.ds(0, count // SLOTS), pl.ds(0, SLOTS * SIDE)]
    pltpu.make_async_copy(every, every, tile_sem).wait()
    named.wait()


def pack(tile_dest, tiles, labels):
    devices = labels.shape[0]
    return pl.pallas_call(
        pack_body,
        out_shape=jax.ShapeDtypeStruct((devices, SLOTS * SIDE + HALF_TILE, SIDE), tiles.dtype),
        in_specs=[
            pl.BlockSpec(memory_space=pltpu.SMEM),
            pl.BlockSpec(memory_space=pltpu.VMEM),
            pl.BlockSpec(memory_space=pltpu.VMEM),
        ],
        out_specs=pl.BlockSpec(memory_space=pl.ANY),
        scratch_shapes=[
            pltpu.SMEM((devices,), jnp.int32),
            pltpu.SemaphoreType.DMA(()),
            pltpu.SemaphoreType.DMA(()),
        ],
        compiler_params=pltpu.CompilerParams(vmem_limit_bytes=VMEM_LIMIT),
        name="pack",
    )(tile_dest, tiles, labels)


def side_by_side(pair):
    return jnp.concatenate([pair[:, :HALF_TILE], pair[:, HALF_TILE:]], axis=2).reshape(
        -1, 2 * SIDE
    )


def interleave(wide):
    wide = wide.reshape(-1, HALF_TILE, 2 * SIDE)
    return jnp.concatenate([wide[:, :, :SIDE], wide[:, :, SIDE:]], axis=1)


def filter_x(est_ref, top_ref, bot_ref, left_ref, right_ref, wx_ref, wide_ref, ax_ref):
    @pl.loop(0, GROUPS, unroll=UX)
    def _(g):
        z0 = g * ZPER
        slot = g % UX
        wide_ref[slot, :, RIM : RIM + SIDE, 0:SIDE] = est_ref[pl.ds(z0, ZPER)].astype(
            jnp.bfloat16
        )
        wide_ref[slot, :, 0:RIM, 0:SIDE] = top_ref[pl.ds(z0, ZPER)]
        wide_ref[slot, :, RIM + SIDE : EXT, 0:SIDE] = bot_ref[pl.ds(z0, ZPER)]
        for q in range(ZPER):
            lane = lanes((EXT, SIDE))
            lo = pltpu.roll(left_ref[q].astype(jnp.float32), (SIDE - RIM * g) % SIDE, 1)
            hi = pltpu.roll(right_ref[q].astype(jnp.float32), (SIDE + RIM - RIM * g) % SIDE, 1)
            both = jnp.where(lane < RIM, lo, jnp.where(lane < 2 * RIM, hi, 0.0))
            wide_ref[slot, q, :, SIDE : 2 * SIDE] = both.astype(jnp.bfloat16)
        for q in range(ZPER):
            got = jnp.dot(
                wide_ref[slot, q], wx_ref[...], preferred_element_type=jnp.float32
            ).astype(jnp.bfloat16)
            for w in range(VIEWS):
                ax_ref[w, z0 + q] = got[:, w * SIDE : (w + 1) * SIDE]


def filter_y(v, wy_ref, ax_ref, ay_ref):
    @pl.loop(0, CZ // 2, unroll=UY)
    def _(i):
        pair = jnp.concatenate([ax_ref[v, 2 * i], ax_ref[v, 2 * i + 1]], axis=1)
        got = jnp.dot(wy_ref[0], pair, preferred_element_type=jnp.float32)
        ay_ref[:, i] = interleave(got).astype(jnp.bfloat16)


def filter_z(i, wz_ref, ay_ref):
    one = ay_ref[2 * i].reshape(CZ * HALF_TILE, SIDE)
    two = ay_ref[2 * i + 1].reshape(CZ * HALF_TILE, SIDE)
    return jnp.dot(
        wz_ref[0], jnp.concatenate([one, two], axis=1), preferred_element_type=jnp.float32
    )


def compare(i, blur, seen, count_ref, bz_ref, rz_ref):
    rows = pl.ds(pl.multiple_of(i * RIM, RIM), RIM)
    seen = side_by_side(seen.astype(jnp.float32))
    times = jnp.concatenate([count_ref[0], count_ref[0]], axis=1)
    ratio = ((seen + DAMPING) / (times * blur + DAMPING)).astype(jnp.bfloat16)
    back = jnp.dot(bz_ref[0], ratio, preferred_element_type=jnp.float32)
    rz_ref[:, rows, :] = interleave(back).astype(jnp.bfloat16)


def spread_y(v, by_ref, rz_ref, ry_ref):
    at = pl.ds(pl.multiple_of(v * SIDE, SIDE), SIDE)

    @pl.loop(0, CZ // 2, unroll=UB)
    def _(i):
        pair = jnp.concatenate([rz_ref[2 * i], rz_ref[2 * i + 1]], axis=1)
        got = jnp.dot(by_ref[0], pair, preferred_element_type=jnp.float32).astype(jnp.bfloat16)
        ry_ref[2 * i, :, at] = got[:, :SIDE]
        ry_ref[2 * i + 1, :, at] = got[:, SIDE:]


def spread_x(bx_ref, ry_ref, mid_ref, up_ref, down_ref, goleft_ref, goright_ref):
    @pl.loop(0, ZPER, unroll=UE)
    def _(q):
        goleft = jnp.zeros((EXT, SIDE), jnp.float32)
        goright = jnp.zeros((EXT, SIDE), jnp.float32)
        for g in range(GROUPS):
            z = g * ZPER + q
            got = jnp.dot(ry_ref[z], bx_ref[...], preferred_element_type=jnp.float32)
            up_ref[z] = got[:RIM, :SIDE]
            mid_ref[z] = got[RIM : RIM + SIDE, :SIDE]
            down_ref[z] = got[RIM + SIDE :, :SIDE]
            strip = got[:, SIDE:]
            mine = lanes((EXT, SIDE)) // RIM == g
            goleft = jnp.where(mine, pltpu.roll(strip, RIM * g, 1), goleft)
            goright = jnp.where(mine, pltpu.roll(strip, (SIDE + RIM * g - RIM) % SIDE, 1), goright)
        goleft_ref[q] = goleft
        goright_ref[q] = goright


def forward_body(
    est_ref, top_ref, bot_ref, left_ref, right_ref, wx_ref, wy_ref, wz_ref,
    blur_ref, wide_ref, ax_ref, ay_ref,
):
    v = pl.program_id(0)

    @pl.when(v == 0)
    def _():
        filter_x(est_ref, top_ref, bot_ref, left_ref, right_ref, wx_ref, wide_ref, ax_ref)

    filter_y(v, wy_ref, ax_ref, ay_ref)

    @pl.loop(0, SIDE // RIM, unroll=UZ)
    def _(i):
        blur_ref[0, i] = filter_z(i, wz_ref, ay_ref)


def backward_body(
    label_ref, got_ref, blur_ref, bx_ref, by_ref, bz_ref,
    mid_ref, up_ref, down_ref, goleft_ref, goright_ref, obs_ref, count_ref,
    rz_ref, ry_ref, head_ref, next_ref, times_ref,
):
    v = pl.program_id(0)

    @pl.when(v == 0)
    def _():
        @pl.loop(0, VIEWS * CZ)
        def _(i):
            head_ref[i] = -1
            times_ref[i] = 0

        @pl.loop(0, label_ref.shape[0])
        def _(i):
            label = label_ref[i]

            @pl.when(label >= 0)
            def _():
                next_ref[i] = head_ref[label]
                head_ref[label] = i
                times_ref[label] = times_ref[label] + 1

    def tile(i):
        return got_ref[i // SLOTS, pl.ds(pl.multiple_of(i % SLOTS * SIDE, SIDE), SIDE)]

    @pl.loop(0, CZ)
    def _(z):
        first = head_ref[v * CZ + z]
        times = times_ref[v * CZ + z]
        count_ref[0, pl.ds(pl.multiple_of(z * HALF_TILE, HALF_TILE), HALF_TILE)] = jnp.full(
            (HALF_TILE, SIDE), times.astype(jnp.float32)
        )

        @pl.when(times == 0)
        def _():
            obs_ref[0, z] = jnp.zeros((SIDE, SIDE), jnp.bfloat16)

        @pl.when(times == 1)
        def _():
            obs_ref[0, z] = tile(first)

        @pl.when(times > 1)
        def _():
            def add(_, carry):
                at, total = carry
                return next_ref[at], total + tile(at).astype(jnp.float32)

            total = jnp.zeros((SIDE, SIDE), jnp.float32)
            obs_ref[0, z] = lax.fori_loop(0, times, add, (first, total))[1].astype(jnp.bfloat16)

    @pl.loop(0, SIDE // RIM, unroll=UZ)
    def _(i):
        rows = pl.ds(pl.multiple_of(i * RIM, RIM), RIM)
        compare(i, blur_ref[0, i], obs_ref[0, :, rows, :], count_ref, bz_ref, rz_ref)

    spread_y(v, by_ref, rz_ref, ry_ref)

    @pl.when(v == VIEWS - 1)
    def _():
        spread_x(bx_ref, ry_ref, mid_ref, up_ref, down_ref, goleft_ref, goright_ref)


def step_body(
    est_ref, top_ref, bot_ref, left_ref, right_ref, obs_ref, count_ref,
    wx_ref, wy_ref, wz_ref, bx_ref, by_ref, bz_ref,
    mid_ref, up_ref, down_ref, goleft_ref, goright_ref,
    wide_ref, ax_ref, ay_ref, rz_ref, ry_ref,
):
    v = pl.program_id(0)

    @pl.when(v == 0)
    def _():
        filter_x(est_ref, top_ref, bot_ref, left_ref, right_ref, wx_ref, wide_ref, ax_ref)

    filter_y(v, wy_ref, ax_ref, ay_ref)

    @pl.loop(0, SIDE // RIM, unroll=UZ)
    def _(i):
        rows = pl.ds(pl.multiple_of(i * RIM, RIM), RIM)
        blur = filter_z(i, wz_ref, ay_ref)
        compare(i, blur, obs_ref[0, :, rows, :], count_ref, bz_ref, rz_ref)

    spread_y(v, by_ref, rz_ref, ry_ref)

    @pl.when(v == VIEWS - 1)
    def _():
        spread_x(bx_ref, ry_ref, mid_ref, up_ref, down_ref, goleft_ref, goright_ref)


def whole(*shape):
    return pl.BlockSpec(shape, lambda v, *_: (0,) * len(shape))


def once(*shape):
    return pl.BlockSpec(
        shape, lambda v, *_: (0,) * len(shape), pipeline_mode=pl.Buffered(1)
    )


def per_view(*shape):
    return pl.BlockSpec((1,) + shape, lambda v, *_: (v,) + (0,) * len(shape))


ROWS = (CZ, RIM, SIDE)
CORE = (CZ, SIDE, SIDE)
STRIP = (ZPER, EXT, SIDE)
Z_BAND = (CZ * HALF_TILE, CZ * HALF_TILE)
TIMES = (CZ * HALF_TILE, SIDE)
BLUR = (SIDE // RIM, CZ * HALF_TILE, 2 * SIDE)
HALO_SPECS = [whole(*ROWS), whole(*ROWS), whole(*STRIP), whole(*STRIP)]
FRONT_SPECS = [whole(2 * SIDE, VIEWS * SIDE), per_view(SIDE, EXT), per_view(*Z_BAND)]
BACK_SPECS = [whole(VIEWS * SIDE, 2 * SIDE), per_view(EXT, SIDE), per_view(*Z_BAND)]
PART_SPECS = [whole(*CORE), whole(*ROWS), whole(*ROWS), whole(*STRIP), whole(*STRIP)]
PARTS = tuple(
    jax.ShapeDtypeStruct(shape, jnp.float32) for shape in (CORE, ROWS, ROWS, STRIP, STRIP)
)
FRONT_SCRATCH = [
    pltpu.VMEM((UX, ZPER, EXT, 2 * SIDE), jnp.bfloat16),
    pltpu.VMEM((VIEWS, CZ, EXT, SIDE), jnp.bfloat16),
    pltpu.VMEM((SIDE // HALF_TILE, CZ // 2, RIM, SIDE), jnp.bfloat16),
]
BACK_SCRATCH = [
    pltpu.VMEM(CORE, jnp.bfloat16),
    pltpu.VMEM((CZ, EXT, VIEWS * SIDE), jnp.bfloat16),
]
ROOM = pltpu.CompilerParams(vmem_limit_bytes=VMEM_LIMIT)


def forward(est, halo, weights):
    return pl.pallas_call(
        forward_body,
        out_shape=jax.ShapeDtypeStruct((VIEWS,) + BLUR, jnp.float32),
        grid=(VIEWS,),
        in_specs=[whole(*CORE)] + HALO_SPECS + FRONT_SPECS,
        out_specs=per_view(*BLUR),
        scratch_shapes=FRONT_SCRATCH,
        compiler_params=ROOM,
        name="forward",
    )(est, *halo, *weights[:3])


def backward(labels, got, blur, weights):
    slots = labels.shape[0]
    return pl.pallas_call(
        backward_body,
        out_shape=PARTS
        + (
            jax.ShapeDtypeStruct((VIEWS,) + CORE, jnp.bfloat16),
            jax.ShapeDtypeStruct((VIEWS,) + TIMES, jnp.float32),
        ),
        grid_spec=pltpu.PrefetchScalarGridSpec(
            num_scalar_prefetch=1,
            grid=(VIEWS,),
            in_specs=[once(*got.shape), per_view(*BLUR)] + BACK_SPECS,
            out_specs=PART_SPECS + [per_view(*CORE), per_view(*TIMES)],
            scratch_shapes=BACK_SCRATCH
            + [
                pltpu.SMEM((VIEWS * CZ,), jnp.int32),
                pltpu.SMEM((slots,), jnp.int32),
                pltpu.SMEM((VIEWS * CZ,), jnp.int32),
            ],
        ),
        compiler_params=ROOM,
        name="backward",
    )(labels, got, blur, *weights[3:])


def iterate(counted, est, halo, observed, weights):
    return pl.pallas_call(
        step_body,
        out_shape=PARTS,
        grid=(VIEWS,),
        in_specs=[whole(*CORE)]
        + HALO_SPECS
        + [per_view(*CORE), per_view(*TIMES)]
        + FRONT_SPECS
        + BACK_SPECS,
        out_specs=PART_SPECS,
        scratch_shapes=FRONT_SCRATCH + BACK_SCRATCH,
        compiler_params=ROOM,
        name="iterate",
    )(est, *halo, observed, counted, *weights)


def beside(q, g, rows, left_ref, right_ref):
    low = pltpu.roll(left_ref[q, rows], (SIDE - RIM * g) % SIDE, 1)
    high = pltpu.roll(right_ref[q, rows], (2 * SIDE - RIM - RIM * g) % SIDE, 1)
    lane = lanes(low.shape)
    return jnp.where(lane < RIM, low, jnp.where(lane >= SIDE - RIM, high, 0.0))


def in_two(values):
    high = values.astype(jnp.bfloat16)
    return high, (values - high.astype(jnp.float32)).astype(jnp.bfloat16)


def join_x_body(first_ref, last_ref, up_ref, down_ref, left_ref, right_ref, *outs):
    @pl.loop(0, ZPER, unroll=True)
    def _(q):
        for g in range(GROUPS):
            z = g * ZPER + q
            head = up_ref[z] + beside(q, g, slice(0, RIM), left_ref, right_ref)
            tail = down_ref[z] + beside(q, g, slice(SIDE + RIM, EXT), left_ref, right_ref)
            outs[0][z], outs[1][z] = head, tail
            if len(outs) > 2:
                own = first_ref[z] + beside(q, g, slice(RIM, 2 * RIM), left_ref, right_ref)
                outs[2][z], outs[2][CZ + z] = in_two(head)
                outs[2][2 * CZ + z] = own.astype(jnp.bfloat16)
                own = last_ref[z] + beside(q, g, slice(SIDE, SIDE + RIM), left_ref, right_ref)
                outs[3][z], outs[3][CZ + z] = in_two(tail)
                outs[3][2 * CZ + z] = own.astype(jnp.bfloat16)


def join_x(mid, up, down, from_left, from_right, more):
    rows = jax.ShapeDtypeStruct(ROWS, jnp.float32)
    message = jax.ShapeDtypeStruct((3 * CZ, RIM, SIDE), jnp.bfloat16)
    out_shape = (rows, rows) + ((message, message) if more else ())
    return pl.pallas_call(
        join_x_body,
        out_shape=out_shape,
        grid=(1,),
        in_specs=[
            pl.BlockSpec(ROWS, lambda i: (0, 0, 0)),
            pl.BlockSpec(ROWS, lambda i: (0, SIDE // RIM - 1, 0)),
            whole(*ROWS),
            whole(*ROWS),
            whole(*STRIP),
            whole(*STRIP),
        ],
        out_specs=[whole(*shape.shape) for shape in out_shape],
        compiler_params=ROOM,
        name="join_x",
    )(mid, mid, up, down, from_left, from_right)


def joined(est_ref, mid_ref, left_ref, right_ref, q, g, head, tail):
    z = g * ZPER + q
    total = mid_ref[z] + beside(q, g, slice(RIM, RIM + SIDE), left_ref, right_ref)
    total = jnp.concatenate(
        [total[:RIM] + head, total[RIM : SIDE - RIM], total[SIDE - RIM :] + tail], axis=0
    )
    return est_ref[z] * total / VIEWS


def last_join_body(est_ref, mid_ref, left_ref, right_ref, above_ref, below_ref, out_ref):
    @pl.loop(0, ZPER, unroll=2)
    def _(q):
        for g in range(GROUPS):
            z = g * ZPER + q
            out_ref[z] = joined(
                est_ref, mid_ref, left_ref, right_ref, q, g, above_ref[z], below_ref[z]
            )


def last_join(est, mid, from_left, from_right, above, below):
    return pl.pallas_call(
        last_join_body,
        out_shape=jax.ShapeDtypeStruct(CORE, jnp.float32),
        compiler_params=ROOM,
        name="last_join",
    )(est, mid, from_left, from_right, above, below)


def cut(q, planes, left_ref, right_ref):
    low = jnp.zeros((EXT, SIDE), jnp.float32)
    high = jnp.zeros((EXT, SIDE), jnp.float32)
    for g, plane in enumerate(planes):
        mine = lanes((EXT, SIDE)) // RIM == g
        low = jnp.where(mine, pltpu.roll(plane, RIM * g, 1), low)
        high = jnp.where(mine, pltpu.roll(plane, (RIM * g + RIM) % SIDE, 1), high)
    left_ref[q] = low.astype(jnp.bfloat16)
    right_ref[q] = high.astype(jnp.bfloat16)


def next_join_body(
    est_ref, mid_ref, left_ref, right_ref, above_ref, below_ref,
    up_ref, down_ref, top_ref, bot_ref,
    out_ref, newtop_ref, newbot_ref, goleft_ref, goright_ref,
):
    def whole_of(ref, z):
        return ref[z].astype(jnp.float32) + ref[CZ + z].astype(jnp.float32)

    @pl.loop(0, ZPER, unroll=2)
    def _(q):
        planes = []
        for g in range(GROUPS):
            z = g * ZPER + q
            now = joined(
                est_ref, mid_ref, left_ref, right_ref, q, g,
                whole_of(above_ref, z), whole_of(below_ref, z),
            )
            out_ref[z] = now
            total = above_ref[2 * CZ + z].astype(jnp.float32) + up_ref[z]
            newtop = top_ref[z].astype(jnp.float32) * total / VIEWS
            newtop_ref[z] = newtop.astype(jnp.bfloat16)
            total = below_ref[2 * CZ + z].astype(jnp.float32) + down_ref[z]
            newbot = bot_ref[z].astype(jnp.float32) * total / VIEWS
            newbot_ref[z] = newbot.astype(jnp.bfloat16)
            planes.append(jnp.concatenate([newtop, now, newbot], axis=0))
        cut(q, planes, goleft_ref, goright_ref)


def next_join(est, mid, from_left, from_right, above, below, up, down, top, bot):
    rows = jax.ShapeDtypeStruct(ROWS, jnp.bfloat16)
    strip = jax.ShapeDtypeStruct(STRIP, jnp.bfloat16)
    return pl.pallas_call(
        next_join_body,
        out_shape=(jax.ShapeDtypeStruct(CORE, jnp.float32), rows, rows, strip, strip),
        compiler_params=ROOM,
        name="next_join",
    )(est, mid, from_left, from_right, above, below, up, down, top, bot)


def edges_body(est_ref, top_ref, bot_ref, left_ref, right_ref):
    @pl.loop(0, ZPER, unroll=2)
    def _(q):
        planes = []
        for g in range(GROUPS):
            z = g * ZPER + q
            rim = (top_ref[z].astype(jnp.float32), bot_ref[z].astype(jnp.float32))
            planes.append(jnp.concatenate([rim[0], est_ref[z], rim[1]], axis=0))
        cut(q, planes, left_ref, right_ref)


def edges(est, top, bot):
    strip = jax.ShapeDtypeStruct(STRIP, jnp.bfloat16)
    return pl.pallas_call(
        edges_body,
        out_shape=(strip, strip),
        compiler_params=ROOM,
        name="edges",
    )(est, top, bot)


def pick(taps, offset):
    hot = (offset[:, :, None] == jnp.arange(TAPS)[None, None, :]).astype(jnp.bfloat16)
    return jnp.einsum("rct,vt->vrc", hot, taps, preferred_element_type=jnp.float32).astype(
        jnp.bfloat16
    )


def weights_of(psf):
    kernel = (psf / jnp.sum(psf, axis=2, keepdims=True)).astype(jnp.bfloat16)
    core = jnp.arange(SIDE)
    rim = jnp.arange(RIM)
    far = jnp.full((SIDE - 2 * RIM,), 4 * SIDE)
    where_x = jnp.concatenate([core, rim - RIM, SIDE + rim, far])
    wx = pick(kernel[:, 2], where_x[:, None] - core[None, :] + REACH)
    wx = jnp.transpose(wx, (1, 0, 2)).reshape(2 * SIDE, VIEWS * SIDE)
    bx = pick(kernel[:, 2], where_x[None, :] - core[:, None] + REACH).reshape(
        VIEWS * SIDE, 2 * SIDE
    )
    where_y = jnp.arange(EXT) - RIM
    wy = pick(kernel[:, 1], where_y[None, :] - core[:, None] + REACH)
    by = pick(kernel[:, 1], where_y[:, None] - core[None, :] + REACH)
    row = jnp.arange(CZ * HALF_TILE)
    same = row[:, None] % HALF_TILE == row[None, :] % HALF_TILE
    gap = row[None, :] // HALF_TILE - row[:, None] // HALF_TILE
    wz = pick(kernel[:, 0], jnp.where(same, gap + REACH, -1))
    bz = pick(kernel[:, 0], jnp.where(same, REACH - gap, -1))
    return wx, wy, wz, bx, by, bz


def local(tiles, tile_dest, tile_slot, psf, estimate):
    axes = ("gy", "gx")
    devices = lax.axis_size("gy") * lax.axis_size("gx")
    top = shift(estimate[:, SIDE - RIM :].astype(jnp.bfloat16), "gy", 1)
    bot = shift(estimate[:, :RIM].astype(jnp.bfloat16), "gy", -1)
    dest = tile_dest[:, 0]
    count = dest.shape[0]
    order = (jnp.arange(count) * 256 + tile_slot)[None, :]
    hit = dest[None, :] == jnp.arange(devices)[:, None]
    first = jnp.min(jnp.where(hit, order, count * 256), axis=1)[:, None, None]
    last = jnp.max(jnp.where(hit, order, -1), axis=1)[:, None, None]
    one = jnp.where(first < count * 256, first % 256, -1)
    two = jnp.where(last > first, last % 256, -1)
    labels = jnp.where(lanes((devices, HALF_TILE, SIDE)) == 0, one, two).astype(jnp.bfloat16)
    low, high = edges(estimate, top, bot)
    left, right = shift(high, "gx", 1), shift(low, "gx", -1)
    packed = pack(dest, tiles, labels)
    packed, left, right = lax.optimization_barrier((packed, left, right))
    got = lax.all_to_all(packed, axes, split_axis=0, concat_axis=0, tiled=True)
    weights = weights_of(psf)
    blur = forward(estimate, (top, bot, left, right), weights)
    labels = got[:, SLOTS * SIDE, :SLOTS].astype(jnp.int32).reshape(-1)
    *parts, observed, counted = backward(labels, got, blur, weights)
    for repeat_index in range(ITERS):
        more = repeat_index + 1 < ITERS
        mid, up, down, goleft, goright = parts
        sides = shift(goright, "gx", 1), shift(goleft, "gx", -1)
        sent = join_x(mid, up, down, *sides, more)
        if not more:
            up, down = sent
            return last_join(
                estimate, mid, *sides, shift(down, "gy", 1), shift(up, "gy", -1)
            )
        up, down, goup, godown = sent
        estimate, top, bot, low, high = next_join(
            estimate, mid, *sides, shift(godown, "gy", 1), shift(goup, "gy", -1), up, down, top, bot
        )
        halo = top, bot, shift(high, "gx", 1), shift(low, "gx", -1)
        parts = iterate(counted, estimate, halo, observed, weights)


def solution(mesh):
    placed = (
        P(("gy", "gx"), None, None),
        P(("gy", "gx"), None),
        P(("gy", "gx")),
        P(),
        P(None, "gy", "gx"),
    )
    return jax.shard_map(
        local, mesh=mesh, in_specs=placed, out_specs=P(None, "gy", "gx"), check_vma=False
    )
```

profile of v0, /device:TPU:15, one launch (start us, length us, event | category | flops | bytes accessed | tf_op | source)
XLA Modules:
  0.0 291.8 jit_solution(13031108787057458466)
XLA Ops:
  0.0 1.7 convert.5
  1.8 3.0 %collective-permute-start.1 = (bf16[32,16,128]{2,1,0:T(8,128)(2,1)S(1)}, bf16[32,16,128]{2,1,0:T(8,128)(2,1)S(1)}, u32[]{:S(2)}, u32[]{:S(2)}) collective-permute-start(bf16[32,16,128]{2,1,0:T(8,128)(2,1)S(1)} %get-tuple-element.63), channel_id=1, source_target_pairs={{16,0},{32,16},{48,32},{64,48},{80,64},{96,80},{112,96},{17,1},{33... | collective-permute-start | bytes 393224 | tf_op jit(solution)/shard_map/ppermute | solution.py:28
  4.8 4.7 %collective-permute-start = (bf16[32,16,128]{2,1,0:T(8,128)(2,1)S(1)}, bf16[32,16,128]{2,1,0:T(8,128)(2,1)S(1)}, u32[]{:S(2)}, u32[]{:S(2)}) collective-permute-start(bf16[32,16,128]{2,1,0:T(8,128)(2,1)S(1)} %get-tuple-element.64), channel_id=1, source_target_pairs={{0,16},{16,32},{32,48},{48,64},{64,80},{80,96},{96,112},{1,17},{17... | collective-permute-start | bytes 393224 | tf_op jit(solution)/shard_map/ppermute | solution.py:28
  9.5 0.7 multiply_add_fusion
  10.1 0.8 select_reduce_fusion.1
  11.0 1.1 collective-permute-done.top_ref
  12.0 0.6 copy-done.5
  12.7 3.1 %edges.1 = (bf16[4,160,128]{2,1,0:T(8,128)(2,1)}, bf16[4,160,128]{2,1,0:T(8,128)(2,1)}) custom-call(f32[32,128,128]{2,1,0:T(8,128)} %est_ref.5, bf16[32,16,128]{2,1,0:T(8,128)(2,1)} %copy-done.5, bf16[32,16,128]{2,1,0:T(8,128)(2,1)} %copy-done.4), custom_call_target="tpu_custom_call" | custom-call | tf_op jit(solution)/shard_map/edges/pallas_call | solution.py:517
  15.8 4.5 %collective-permute-start.2 = (bf16[4,160,128]{2,1,0:T(8,128)(2,1)}, bf16[4,160,128]{2,1,0:T(8,128)(2,1)S(1)}, u32[]{:S(2)}, u32[]{:S(2)}) collective-permute-start(bf16[4,160,128]{2,1,0:T(8,128)(2,1)} %get-tuple-element.33), channel_id=1, source_target_pairs={{0,1},{1,2},{2,3},{3,4},{4,5},{5,6},{6,7},{7,8},{8,9},{9,10},{10,1... | collective-permute-start | bytes 491528 | tf_op jit(solution)/shard_map/ppermute | solution.py:28
  20.4 1.9 collective-permute-start.3
  22.3 1.0 select_convert_fusion.labels_ref
  23.4 5.1 %pack.1 = bf16[128,264,128]{2,1,0:T(8,128)(2,1)} custom-call(s32[128]{0:T(128)} %bitcast.24, bf16[128,128,128]{2,1,0:T(8,128)(2,1)} %tiles_ref.1, bf16[128,8,128]{2,1,0:T(8,128)(2,1)} %select_convert_fusion.labels_ref), custom_call_target="tpu_custom_call" | custom-call | tf_op jit(solution)/shard_map/pack/pallas_call | solution.py:63
  28.5 0.6 copy-done.10
  29.2 12.4 %all-to-all-start = ((bf16[128,264,128]{2,1,0:T(8,128)(2,1)}), bf16[128,264,128]{2,1,0:T(8,128)(2,1)}, u32[]{:S(2)}, u32[]{:S(2)}) async-start(bf16[128,264,128]{2,1,0:T(8,128)(2,1)} %pack.1), calls=%async_computation | async-start | bytes 17301504 | tf_op jit(solution)/shard_map/all_to_all | solution.py:572
  41.9 0.5 fusion.6
  42.5 1.0 copy.34.wy_ref
  43.6 0.5 fusion.7
  44.1 0.7 copy.49.by_ref
  44.9 0.1 subtract_add_fusion.2
  45.0 0.8 fusion.14
  45.8 0.3 copy.33
  46.1 0.9 copy.36.wx_ref
  47.1 0.8 fusion.12
  47.8 0.8 copy.37
  48.7 0.1 compare_select_fusion
  48.8 1.4 fusion.1
  50.3 1.1 copy.47.bz_ref
  51.3 1.4 fusion
  52.7 1.0 copy.48.wz_ref
  53.8 12.8 %forward.1.blur_ref = f32[6,8,256,256]{3,2,1,0:T(8,128)} custom-call(f32[32,128,128]{2,1,0:T(8,128)} %est_ref.5, bf16[32,16,128]{2,1,0:T(8,128)(2,1)} %copy-done.5, bf16[32,16,128]{2,1,0:T(8,128)(2,1)} %copy-done.4, bf16[4,160,128]{2,1,0:T(8,128)(2,1)} %copy-done.10, bf16[4,160,128]{2,1,0:T(8,128)(2,1)} %copy-done.11, bf16[256,768]{1,0:T(8,128)(2,1)} %copy.36.wx_ref, ...), custom_call_target="tpu_custom_call" | custom-call | tf_op jit(solution)/shard_map/forward/pallas_call | solution.py:320
  66.6 78.4 %all-to-all-done.got_ref = bf16[128,264,128]{2,1,0:T(8,128)(2,1)} async-done(((bf16[128,264,128]{2,1,0:T(8,128)(2,1)}), bf16[128,264,128]{2,1,0:T(8,128)(2,1)}, u32[]{:S(2)}, u32[]{:S(2)}) %all-to-all-start) | async-done | bytes 8650784 | tf_op jit(solution)/shard_map/all_to_all | solution.py:572
  145.0 1.2 fusion.15
  146.2 0.7 reshape.367.label_ref
  146.9 24.1 %backward.1 = (f32[32,128,128]{2,1,0:T(8,128)}, f32[32,16,128]{2,1,0:T(8,128)}, f32[32,16,128]{2,1,0:T(8,128)}, f32[4,160,128]{2,1,0:T(8,128)}, f32[4,160,128]{2...) custom-call(s32[256]{0:T(256)} %reshape.367.label_ref, ...), custom_call_target="tpu_custom_call" | custom-call | tf_op jit(solution)/shard_map/backward/pallas_call | solution.py:334
  171.0 13.6 %collective-permute-start.4 = (f32[4,160,128]{2,1,0:T(8,128)}, f32[4,160,128]{2,1,0:T(8,128)S(1)}, u32[]{:S(2)}, u32[]{:S(2)}) collective-permute-start(f32[4,160,128]{2,1,0:T(8,128)} %get-tuple-element.39), channel_id=1, source_target_pairs={{0,1},{1,2},{2,3},{3,4},{4,5},{5,6},{6,7},{7,8},{8,9},{9,10},{10,1... | collective-permute-start | bytes 983048 | tf_op jit(solution)/shard_map/ppermute | solution.py:28
  184.6 1.9 collective-permute-start.5
  186.5 2.4 collective-permute-done.4.left_ref
  188.9 5.2 %collective-permute-done.5.right_ref = f32[4,160,128]{2,1,0:T(8,128)S(1)} collective-permute-done((f32[4,160,128]{2,1,0:T(8,128)}, f32[4,160,128]{2,1,0:T(8,128)S(1)}, u32[]{:S(2)}, u32[]{:S(2)}) %collective-permute-start.5) | collective-permute-done | bytes 327712 | tf_op jit(solution)/shard_map/ppermute | solution.py:28
  194.1 0.8 copy-done.1
  194.8 3.0 %join_x.2 = (f32[32,16,128]{2,1,0:T(8,128)}, f32[32,16,128]{2,1,0:T(8,128)}, bf16[96,16,128]{2,1,0:T(8,128)(2,1)}, bf16[96,16,128]{2,1,0:T(8,128)(2,1)}) custom-call(f32[32,128,128]{2,1,0:T(8,128)} %get-tuple-element.38.first_ref.last_ref.mid_ref, f32[32,128,128]{2,1,0:T(8,128)} %get-tuple-element.38.first_ref.last_ref.mid_ref, ...), custom_call_target="tpu_custom_call" | custom-call | tf_op jit(solution)/shard_map/join_x/pallas_call | solution.py:408
  197.8 1.9 collective-permute-start.6
  199.7 5.1 %collective-permute-start.7 = (bf16[96,16,128]{2,1,0:T(8,128)(2,1)}, bf16[96,16,128]{2,1,0:T(8,128)(2,1)S(1)}, u32[]{:S(2)}, u32[]{:S(2)}) collective-permute-start(bf16[96,16,128]{2,1,0:T(8,128)(2,1)} %get-tuple-element.44), channel_id=1, source_target_pairs={{16,0},{32,16},{48,32},{64,48},{80,64},{96,80},{112,96},{17,1},{33... | collective-permute-start | bytes 1179656 | tf_op jit(solution)/shard_map/ppermute | solution.py:28
  204.8 4.0 %collective-permute-done.6.above_ref = bf16[96,16,128]{2,1,0:T(8,128)(2,1)S(1)} collective-permute-done((bf16[96,16,128]{2,1,0:T(8,128)(2,1)}, bf16[96,16,128]{2,1,0:T(8,128)(2,1)S(1)}, u32[]{:S(2)}, u32[]{:S(2)}) %collective-permute-start.6) | collective-permute-done | bytes 393248 | tf_op jit(solution)/shard_map/ppermute | solution.py:28
  208.8 4.2 %collective-permute-done.7.below_ref = bf16[96,16,128]{2,1,0:T(8,128)(2,1)S(1)} collective-permute-done((bf16[96,16,128]{2,1,0:T(8,128)(2,1)}, bf16[96,16,128]{2,1,0:T(8,128)(2,1)S(1)}, u32[]{:S(2)}, u32[]{:S(2)}) %collective-permute-start.7) | collective-permute-done | bytes 393248 | tf_op jit(solution)/shard_map/ppermute | solution.py:28
  213.0 0.7 copy-done.7
  213.8 5.9 %next_join.1 = (f32[32,128,128]{2,1,0:T(8,128)}, bf16[32,16,128]{2,1,0:T(8,128)(2,1)}, bf16[32,16,128]{2,1,0:T(8,128)(2,1)}, bf16[4,160,128]{2,1,0:T(8,128)(2,1)}, bf16[4,160,128]{2,1,0:T(8,128)(2,1)}) custom-call(f32[32,128,128]{2,1,0:T(8,128)} %est_ref.5, f32[32,128,128]{2,1,0:T(8,128)} %get-tuple-element.38.first_ref.last_ref.mid_ref, ...), custom_call_target="tpu_custom_call" | custom-call | tf_op jit(solution)/shard_map/next_join/pallas_call | solution.py:496
  219.7 5.0 %collective-permute-start.8 = (bf16[4,160,128]{2,1,0:T(8,128)(2,1)}, bf16[4,160,128]{2,1,0:T(8,128)(2,1)S(1)}, u32[]{:S(2)}, u32[]{:S(2)}) collective-permute-start(bf16[4,160,128]{2,1,0:T(8,128)(2,1)} %get-tuple-element.50), channel_id=1, source_target_pairs={{0,1},{1,2},{2,3},{3,4},{4,5},{5,6},{6,7},{7,8},{8,9},{9,10},{10,1... | collective-permute-start | bytes 491528 | tf_op jit(solution)/shard_map/ppermute | solution.py:28
  224.7 1.9 collective-permute-start.9
  226.7 1.9 collective-permute-done.8.left_ref
  228.6 3.9 %collective-permute-done.9.right_ref = bf16[4,160,128]{2,1,0:T(8,128)(2,1)S(1)} collective-permute-done((bf16[4,160,128]{2,1,0:T(8,128)(2,1)}, bf16[4,160,128]{2,1,0:T(8,128)(2,1)S(1)}, u32[]{:S(2)}, u32[]{:S(2)}) %collective-permute-start.9) | collective-permute-done | bytes 163872 | tf_op jit(solution)/shard_map/ppermute | solution.py:28
  232.5 0.7 copy-done.13
  233.1 20.5 %iterate.1 = (f32[32,128,128]{2,1,0:T(8,128)}, f32[32,16,128]{2,1,0:T(8,128)}, f32[32,16,128]{2,1,0:T(8,128)}, f32[4,160,128]{2,1,0:T(8,128)}, f32[4,160,128]{2,1,0:T(8,128)}) custom-call(f32[32,128,128]{2,1,0:T(8,128)} %get-tuple-element.47.est_ref, bf16[32,16,128]{2,1,0:T(8,128)(2,1)} %get-tuple-element.48.top_ref, ...), custom_call_target="tpu_custom_call" | custom-call | tf_op jit(solution)/shard_map/iterate/pallas_call | solution.py:359
  253.7 1.9 collective-permute-start.10
  255.6 2.4 collective-permute-start.11
  258.0 2.7 collective-permute-done.10.left_ref
  260.7 4.3 %collective-permute-done.11.right_ref = f32[4,160,128]{2,1,0:T(8,128)S(1)} collective-permute-done((f32[4,160,128]{2,1,0:T(8,128)}, f32[4,160,128]{2,1,0:T(8,128)S(1)}, u32[]{:S(2)}, u32[]{:S(2)}) %collective-permute-start.11) | collective-permute-done | bytes 327712 | tf_op jit(solution)/shard_map/ppermute | solution.py:28
  265.1 0.7 copy-done.3
  265.8 2.5 join_x.3
  268.3 4.5 %collective-permute-start.12 = (f32[32,16,128]{2,1,0:T(8,128)}, f32[32,16,128]{2,1,0:T(8,128)S(1)}, u32[]{:S(2)}, u32[]{:S(2)}) collective-permute-start(f32[32,16,128]{2,1,0:T(8,128)} %get-tuple-element.59), channel_id=1, source_target_pairs={{0,16},{16,32},{32,48},{48,64},{64,80},{80,96},{96,112},{1,17},{17... | collective-permute-start | bytes 786440 | tf_op jit(solution)/shard_map/ppermute | solution.py:28
  272.8 2.9 %collective-permute-start.13 = (f32[32,16,128]{2,1,0:T(8,128)}, f32[32,16,128]{2,1,0:T(8,128)S(1)}, u32[]{:S(2)}, u32[]{:S(2)}) collective-permute-start(f32[32,16,128]{2,1,0:T(8,128)} %get-tuple-element.60), channel_id=1, source_target_pairs={{16,0},{32,16},{48,32},{64,48},{80,64},{96,80},{112,96},{17,1},{33... | collective-permute-start | bytes 786440 | tf_op jit(solution)/shard_map/ppermute | solution.py:28
  275.7 3.7 %collective-permute-done.12.above_ref = f32[32,16,128]{2,1,0:T(8,128)S(1)} collective-permute-done((f32[32,16,128]{2,1,0:T(8,128)}, f32[32,16,128]{2,1,0:T(8,128)S(1)}, u32[]{:S(2)}, u32[]{:S(2)}) %collective-permute-start.12) | collective-permute-done | bytes 262176 | tf_op jit(solution)/shard_map/ppermute | solution.py:28
  279.4 6.8 %collective-permute-done.13.below_ref = f32[32,16,128]{2,1,0:T(8,128)S(1)} collective-permute-done((f32[32,16,128]{2,1,0:T(8,128)}, f32[32,16,128]{2,1,0:T(8,128)S(1)}, u32[]{:S(2)}, u32[]{:S(2)}) %collective-permute-start.13) | collective-permute-done | bytes 262176 | tf_op jit(solution)/shard_map/ppermute | solution.py:28
  286.2 0.7 copy-done.9
  286.9 4.9 %last_join.1 = f32[32,128,128]{2,1,0:T(8,128)} custom-call(f32[32,128,128]{2,1,0:T(8,128)} %get-tuple-element.47.est_ref, f32[32,128,128]{2,1,0:T(8,128)} %get-tuple-element.54.first_ref.last_ref.mid_ref, f32[4,160,128]{2,1,0:T(8,128)} %copy-done.2, f32[4,160,128]{2,1,0:T(8,128)} %copy-done.3, f32[32,16,128]{2,1,0:T(8,128)} %copy-done.8, ...), custom_call_target="tpu_custom_call" | custom-call | tf_op jit(solution)/shard_map/last_join/pallas_call | solution.py:446
  (41 shorter events, 0.7 us)
Async XLA Ops:
  1.8 9.2 %collective-permute-start.1 = (bf16[32,16,128]{2,1,0:T(8,128)(2,1)S(1)}, bf16[32,16,128]{2,1,0:T(8,128)(2,1)S(1)}, u32[]{:S(2)}, u32[]{:S(2)}) collective-permute-start(bf16[32,16,128]{2,1,0:T(8,128)(2,1)S(1)} %get-tuple-element.63), channel_id=1, source_target_pairs={{16,0},{32,16},{48,32},{64,48},{80,64},{96,80},{112,96},{17,1},{33... | collective-permute-start | bytes 393224 | tf_op jit(solution)/shard_map/ppermute | solution.py:28
  4.8 7.2 %collective-permute-start = (bf16[32,16,128]{2,1,0:T(8,128)(2,1)S(1)}, bf16[32,16,128]{2,1,0:T(8,128)(2,1)S(1)}, u32[]{:S(2)}, u32[]{:S(2)}) collective-permute-start(bf16[32,16,128]{2,1,0:T(8,128)(2,1)S(1)} %get-tuple-element.64), channel_id=1, source_target_pairs={{0,16},{16,32},{32,48},{48,64},{64,80},{80,96},{96,112},{1,17},{17... | collective-permute-start | bytes 393224 | tf_op jit(solution)/shard_map/ppermute | solution.py:28
  11.0 1.1 copy-start.4
  12.0 0.7 copy-start.5
  15.8 12.6 %collective-permute-start.2 = (bf16[4,160,128]{2,1,0:T(8,128)(2,1)}, bf16[4,160,128]{2,1,0:T(8,128)(2,1)S(1)}, u32[]{:S(2)}, u32[]{:S(2)}) collective-permute-start(bf16[4,160,128]{2,1,0:T(8,128)(2,1)} %get-tuple-element.33), channel_id=1, source_target_pairs={{0,1},{1,2},{2,3},{3,4},{4,5},{5,6},{6,7},{7,8},{8,9},{9,10},{10,1... | collective-permute-start | bytes 491528 | tf_op jit(solution)/shard_map/ppermute | solution.py:28
  20.4 8.1 %collective-permute-start.3 = (bf16[4,160,128]{2,1,0:T(8,128)(2,1)}, bf16[4,160,128]{2,1,0:T(8,128)(2,1)S(1)}, u32[]{:S(2)}, u32[]{:S(2)}) collective-permute-start(bf16[4,160,128]{2,1,0:T(8,128)(2,1)} %get-tuple-element.34), channel_id=1, source_target_pairs={{1,0},{2,1},{3,2},{4,3},{5,4},{6,5},{7,6},{8,7},{9,8},{10,9},{11,1... | collective-permute-start | bytes 491528 | tf_op jit(solution)/shard_map/ppermute | solution.py:28
  28.5 13.1 %copy-start.14 = (f32[6,3,31]{2,1,0:T(4,128)S(1)}, f32[6,3,31]{2,1,0:T(4,128)}, u32[]{:S(2)}) copy-start(f32[6,3,31]{2,1,0:T(4,128)} %param.8) | copy-start | bytes 6700
  28.5 0.7 copy-start.10
  28.5 0.7 copy-start.11
  29.2 115.8 %all-to-all-start = ((bf16[128,264,128]{2,1,0:T(8,128)(2,1)}), bf16[128,264,128]{2,1,0:T(8,128)(2,1)}, u32[]{:S(2)}, u32[]{:S(2)}) async-start(bf16[128,264,128]{2,1,0:T(8,128)(2,1)} %pack.1), calls=%async_computation | async-start | bytes 17301504 | tf_op jit(solution)/shard_map/all_to_all | solution.py:572
  171.0 17.9 %collective-permute-start.4 = (f32[4,160,128]{2,1,0:T(8,128)}, f32[4,160,128]{2,1,0:T(8,128)S(1)}, u32[]{:S(2)}, u32[]{:S(2)}) collective-permute-start(f32[4,160,128]{2,1,0:T(8,128)} %get-tuple-element.39), channel_id=1, source_target_pairs={{0,1},{1,2},{2,3},{3,4},{4,5},{5,6},{6,7},{7,8},{8,9},{9,10},{10,1... | collective-permute-start | bytes 983048 | tf_op jit(solution)/shard_map/ppermute | solution.py:28
  184.6 9.5 %collective-permute-start.5 = (f32[4,160,128]{2,1,0:T(8,128)}, f32[4,160,128]{2,1,0:T(8,128)S(1)}, u32[]{:S(2)}, u32[]{:S(2)}) collective-permute-start(f32[4,160,128]{2,1,0:T(8,128)} %get-tuple-element.40), channel_id=1, source_target_pairs={{1,0},{2,1},{3,2},{4,3},{5,4},{6,5},{7,6},{8,7},{9,8},{10,9},{11,1... | collective-permute-start | bytes 983048 | tf_op jit(solution)/shard_map/ppermute | solution.py:28
  188.9 5.2 %copy-start = (f32[4,160,128]{2,1,0:T(8,128)}, f32[4,160,128]{2,1,0:T(8,128)S(1)}, u32[]{:S(2)}) copy-start(f32[4,160,128]{2,1,0:T(8,128)S(1)} %collective-permute-done.4.left_ref) | copy-start | bytes 983044
  194.1 0.8 copy-start.1
  197.8 11.0 %collective-permute-start.6 = (bf16[96,16,128]{2,1,0:T(8,128)(2,1)}, bf16[96,16,128]{2,1,0:T(8,128)(2,1)S(1)}, u32[]{:S(2)}, u32[]{:S(2)}) collective-permute-start(bf16[96,16,128]{2,1,0:T(8,128)(2,1)} %get-tuple-element.43), channel_id=1, source_target_pairs={{0,16},{16,32},{32,48},{48,64},{64,80},{80,96},{96,112},{1,17},{17... | collective-permute-start | bytes 1179656 | tf_op jit(solution)/shard_map/ppermute | solution.py:28
  199.7 13.3 %collective-permute-start.7 = (bf16[96,16,128]{2,1,0:T(8,128)(2,1)}, bf16[96,16,128]{2,1,0:T(8,128)(2,1)S(1)}, u32[]{:S(2)}, u32[]{:S(2)}) collective-permute-start(bf16[96,16,128]{2,1,0:T(8,128)(2,1)} %get-tuple-element.44), channel_id=1, source_target_pairs={{16,0},{32,16},{48,32},{64,48},{80,64},{96,80},{112,96},{17,1},{33... | collective-permute-start | bytes 1179656 | tf_op jit(solution)/shard_map/ppermute | solution.py:28
  208.8 4.2 %copy-start.6 = (bf16[96,16,128]{2,1,0:T(8,128)(2,1)}, bf16[96,16,128]{2,1,0:T(8,128)(2,1)S(1)}, u32[]{:S(2)}) copy-start(bf16[96,16,128]{2,1,0:T(8,128)(2,1)S(1)} %collective-permute-done.6.above_ref) | copy-start | bytes 1179652
  213.0 0.7 copy-start.7
  219.7 8.8 %collective-permute-start.8 = (bf16[4,160,128]{2,1,0:T(8,128)(2,1)}, bf16[4,160,128]{2,1,0:T(8,128)(2,1)S(1)}, u32[]{:S(2)}, u32[]{:S(2)}) collective-permute-start(bf16[4,160,128]{2,1,0:T(8,128)(2,1)} %get-tuple-element.50), channel_id=1, source_target_pairs={{0,1},{1,2},{2,3},{3,4},{4,5},{5,6},{6,7},{7,8},{8,9},{9,10},{10,1... | collective-permute-start | bytes 491528 | tf_op jit(solution)/shard_map/ppermute | solution.py:28
  224.7 7.7 %collective-permute-start.9 = (bf16[4,160,128]{2,1,0:T(8,128)(2,1)}, bf16[4,160,128]{2,1,0:T(8,128)(2,1)S(1)}, u32[]{:S(2)}, u32[]{:S(2)}) collective-permute-start(bf16[4,160,128]{2,1,0:T(8,128)(2,1)} %get-tuple-element.51), channel_id=1, source_target_pairs={{1,0},{2,1},{3,2},{4,3},{5,4},{6,5},{7,6},{8,7},{9,8},{10,9},{11,1... | collective-permute-start | bytes 491528 | tf_op jit(solution)/shard_map/ppermute | solution.py:28
  228.6 3.9 %copy-start.12 = (bf16[4,160,128]{2,1,0:T(8,128)(2,1)}, bf16[4,160,128]{2,1,0:T(8,128)(2,1)S(1)}, u32[]{:S(2)}) copy-start(bf16[4,160,128]{2,1,0:T(8,128)(2,1)S(1)} %collective-permute-done.8.left_ref) | copy-start | bytes 491524
  232.5 0.7 copy-start.13
  253.7 7.1 %collective-permute-start.10 = (f32[4,160,128]{2,1,0:T(8,128)}, f32[4,160,128]{2,1,0:T(8,128)S(1)}, u32[]{:S(2)}, u32[]{:S(2)}) collective-permute-start(f32[4,160,128]{2,1,0:T(8,128)} %get-tuple-element.55), channel_id=1, source_target_pairs={{0,1},{1,2},{2,3},{3,4},{4,5},{5,6},{6,7},{7,8},{8,9},{9,10},{10,1... | collective-permute-start | bytes 983048 | tf_op jit(solution)/shard_map/ppermute | solution.py:28
  255.6 9.5 %collective-permute-start.11 = (f32[4,160,128]{2,1,0:T(8,128)}, f32[4,160,128]{2,1,0:T(8,128)S(1)}, u32[]{:S(2)}, u32[]{:S(2)}) collective-permute-start(f32[4,160,128]{2,1,0:T(8,128)} %get-tuple-element.56), channel_id=1, source_target_pairs={{1,0},{2,1},{3,2},{4,3},{5,4},{6,5},{7,6},{8,7},{9,8},{10,9},{11,1... | collective-permute-start | bytes 983048 | tf_op jit(solution)/shard_map/ppermute | solution.py:28
  260.7 4.4 %copy-start.2 = (f32[4,160,128]{2,1,0:T(8,128)}, f32[4,160,128]{2,1,0:T(8,128)S(1)}, u32[]{:S(2)}) copy-start(f32[4,160,128]{2,1,0:T(8,128)S(1)} %collective-permute-done.10.left_ref) | copy-start | bytes 983044
  265.1 0.7 copy-start.3
  268.3 11.1 %collective-permute-start.12 = (f32[32,16,128]{2,1,0:T(8,128)}, f32[32,16,128]{2,1,0:T(8,128)S(1)}, u32[]{:S(2)}, u32[]{:S(2)}) collective-permute-start(f32[32,16,128]{2,1,0:T(8,128)} %get-tuple-element.59), channel_id=1, source_target_pairs={{0,16},{16,32},{32,48},{48,64},{64,80},{80,96},{96,112},{1,17},{17... | collective-permute-start | bytes 786440 | tf_op jit(solution)/shard_map/ppermute | solution.py:28
  272.8 13.4 %collective-permute-start.13 = (f32[32,16,128]{2,1,0:T(8,128)}, f32[32,16,128]{2,1,0:T(8,128)S(1)}, u32[]{:S(2)}, u32[]{:S(2)}) collective-permute-start(f32[32,16,128]{2,1,0:T(8,128)} %get-tuple-element.60), channel_id=1, source_target_pairs={{16,0},{32,16},{48,32},{64,48},{80,64},{96,80},{112,96},{17,1},{33... | collective-permute-start | bytes 786440 | tf_op jit(solution)/shard_map/ppermute | solution.py:28
  279.4 6.8 %copy-start.8 = (f32[32,16,128]{2,1,0:T(8,128)}, f32[32,16,128]{2,1,0:T(8,128)S(1)}, u32[]{:S(2)}) copy-start(f32[32,16,128]{2,1,0:T(8,128)S(1)} %collective-permute-done.12.above_ref) | copy-start | bytes 786436
  286.2 0.7 copy-start.9
where the time goes:
time: 293 us; the launch traced here: 292 us
  waiting for transfers between devices  119 us (41%)
  Pallas kernels  81.9 us (28%)
  starting transfers between devices  67.6 us (23%)
  local copies, waits for them, and re-layouts  11.7 us (4%)
  other arithmetic  6.07 us (2%)
  matrix products  5.46 us (2%)
    all_to_all x1, waiting for transfers between devices, local(): got = lax.all_to_all(packed, axes, split_axis=0, concat_axis=0, tiled=True)  78.4 us
    ppermute x14, starting transfers between devices, shift(): return lax.ppermute(values, axis, pairs)  55.2 us
    ppermute x14, waiting for transfers between devices, shift(): return lax.ppermute(values, axis, pairs)  40.3 us
    pallas_call x1, Pallas kernels, backward(): pl.pallas_call(backward_body, out_shape=PARTS + (jax.ShapeDtypeStruct((VI...  24.1 us
    pallas_call x1, Pallas kernels, iterate(): pl.pallas_call(step_body, out_shape=PARTS, grid=(VIEWS,), in_specs=[whole...  20.5 us
    pallas_call x1, Pallas kernels, forward(): pl.pallas_call(forward_body, out_shape=jax.ShapeDtypeStruct((VIEWS,) + BL...  12.8 us
    all_to_all x1, starting transfers between devices, local(): got = lax.all_to_all(packed, axes, split_axis=0, concat_axis=0, tiled=True)  12.4 us
    pallas_call x1, Pallas kernels, next_join(): pl.pallas_call(next_join_body, out_shape=(jax.ShapeDtypeStruct(CORE, jnp....  5.94 us
  transfers between devices with their start and end apart: 15, of which 12 were waited for; matrix products, arithmetic and copies ran while one was open for 5% of the time, Pallas kernels for 6%

commit v1 on v0

--- a/solution.py
+++ b/solution.py
@@ -19,7 +19,8 @@
 SLOTS = 2
 HALF_TILE = 8
 UX, UY, UZ, UB, UE = 2, 16, 8, 16, 2
-VMEM_LIMIT = 56 * 1024 * 1024
+def room(mebibytes):
+    return pltpu.CompilerParams(vmem_limit_bytes=mebibytes << 20)
 
 
 def shift(values, axis, step):
@@ -68,13 +69,13 @@
             pl.BlockSpec(memory_space=pltpu.VMEM),
             pl.BlockSpec(memory_space=pltpu.VMEM),
         ],
-        out_specs=pl.BlockSpec(memory_space=pl.ANY),
+        out_specs=pl.BlockSpec(memory_space=pltpu.HBM),
         scratch_shapes=[
             pltpu.SMEM((devices,), jnp.int32),
             pltpu.SemaphoreType.DMA(()),
             pltpu.SemaphoreType.DMA(()),
         ],
-        compiler_params=pltpu.CompilerParams(vmem_limit_bytes=VMEM_LIMIT),
+        compiler_params=room(56),
         name="pack",
     )(tile_dest, tiles, labels)
 
@@ -187,47 +188,64 @@
 
 
 def backward_body(
-    label_ref, got_ref, blur_ref, bx_ref, by_ref, bz_ref,
+    got_ref, blur_ref, bx_ref, by_ref, bz_ref,
     mid_ref, up_ref, down_ref, goleft_ref, goright_ref, obs_ref, count_ref,
-    rz_ref, ry_ref, head_ref, next_ref, times_ref,
+    rz_ref, ry_ref, tiles_ref, names_ref, wide_ref, label_ref, head_ref, next_ref, times_ref,
+    sems,
 ):
     v = pl.program_id(0)
+    sources = got_ref.shape[0]
 
     @pl.when(v == 0)
     def _():
-        @pl.loop(0, VIEWS * CZ)
+        names = pltpu.make_async_copy(
+            got_ref.at[:, pl.ds(SLOTS * SIDE, HALF_TILE)], names_ref, sems.at[0]
+        )
+        tiles = pltpu.make_async_copy(
+            got_ref.at[:, pl.ds(0, SLOTS * SIDE)], tiles_ref, sems.at[1]
+        )
+        names.start()
+        tiles.start()
+
+        @pl.loop(0, VIEWS * CZ, unroll=8)
         def _(i):
-            head_ref[i] = -1
+            head_ref[i] = 0
             times_ref[i] = 0
 
-        @pl.loop(0, label_ref.shape[0])
+        names.wait()
+        wide_ref[...] = names_ref[...].astype(jnp.float32)[:, 0, :].astype(jnp.int32)
+        labels = pltpu.make_async_copy(wide_ref, label_ref, sems.at[2])
+        labels.start()
+        labels.wait()
+
+        @pl.loop(0, sources)
         def _(i):
-            label = label_ref[i]
-
-            @pl.when(label >= 0)
-            def _():
-                next_ref[i] = head_ref[label]
-                head_ref[label] = i
-                times_ref[label] = times_ref[label] + 1
+            for r in range(SLOTS):
+                label = label_ref[i, r]
+
+                @pl.when(label >= 0)
+                def _():
+                    next_ref[i * SLOTS + r] = head_ref[label]
+                    head_ref[label] = i * SLOTS + r
+                    times_ref[label] = times_ref[label] + 1
+
+        tiles.wait()
 
     def tile(i):
-        return got_ref[i // SLOTS, pl.ds(pl.multiple_of(i % SLOTS * SIDE, SIDE), SIDE)]
-
-    @pl.loop(0, CZ)
+        return tiles_ref[i // SLOTS, pl.ds(pl.multiple_of(i % SLOTS * SIDE, SIDE), SIDE)]
+
+    @pl.loop(0, CZ, unroll=4)
     def _(z):
         first = head_ref[v * CZ + z]
         times = times_ref[v * CZ + z]
         count_ref[0, pl.ds(pl.multiple_of(z * HALF_TILE, HALF_TILE), HALF_TILE)] = jnp.full(
             (HALF_TILE, SIDE), times.astype(jnp.float32)
         )
-
-        @pl.when(times == 0)
-        def _():
-            obs_ref[0, z] = jnp.zeros((SIDE, SIDE), jnp.bfloat16)
-
-        @pl.when(times == 1)
-        def _():
-            obs_ref[0, z] = tile(first)
+        obs_ref[0, z] = jnp.where(times > 0, tile(first), jnp.zeros((), jnp.bfloat16))
+
+    @pl.loop(0, CZ)
+    def _(z):
+        times = times_ref[v * CZ + z]
 
         @pl.when(times > 1)
         def _():
@@ -235,6 +253,7 @@
                 at, total = carry
                 return next_ref[at], total + tile(at).astype(jnp.float32)
 
+            first = head_ref[v * CZ + z]
             total = jnp.zeros((SIDE, SIDE), jnp.float32)
             obs_ref[0, z] = lax.fori_loop(0, times, add, (first, total))[1].astype(jnp.bfloat16)
 
@@ -297,9 +316,9 @@
 Z_BAND = (CZ * HALF_TILE, CZ * HALF_TILE)
 TIMES = (CZ * HALF_TILE, SIDE)
 BLUR = (SIDE // RIM, CZ * HALF_TILE, 2 * SIDE)
-HALO_SPECS = [whole(*ROWS), whole(*ROWS), whole(*STRIP), whole(*STRIP)]
-FRONT_SPECS = [whole(2 * SIDE, VIEWS * SIDE), per_view(SIDE, EXT), per_view(*Z_BAND)]
-BACK_SPECS = [whole(VIEWS * SIDE, 2 * SIDE), per_view(EXT, SIDE), per_view(*Z_BAND)]
+HALO_SPECS = [once(*ROWS), once(*ROWS), once(*STRIP), once(*STRIP)]
+FRONT_SPECS = [once(2 * SIDE, VIEWS * SIDE), per_view(SIDE, EXT), per_view(*Z_BAND)]
+BACK_SPECS = [once(VIEWS * SIDE, 2 * SIDE), per_view(EXT, SIDE), per_view(*Z_BAND)]
 PART_SPECS = [whole(*CORE), whole(*ROWS), whole(*ROWS), whole(*STRIP), whole(*STRIP)]
 PARTS = tuple(
     jax.ShapeDtypeStruct(shape, jnp.float32) for shape in (CORE, ROWS, ROWS, STRIP, STRIP)
@@ -313,7 +332,6 @@
     pltpu.VMEM(CORE, jnp.bfloat16),
     pltpu.VMEM((CZ, EXT, VIEWS * SIDE), jnp.bfloat16),
 ]
-ROOM = pltpu.CompilerParams(vmem_limit_bytes=VMEM_LIMIT)
 
 
 def forward(est, halo, weights):
@@ -321,16 +339,16 @@
         forward_body,
         out_shape=jax.ShapeDtypeStruct((VIEWS,) + BLUR, jnp.float32),
         grid=(VIEWS,),
-        in_specs=[whole(*CORE)] + HALO_SPECS + FRONT_SPECS,
+        in_specs=[once(*CORE)] + HALO_SPECS + FRONT_SPECS,
         out_specs=per_view(*BLUR),
         scratch_shapes=FRONT_SCRATCH,
-        compiler_params=ROOM,
+        compiler_params=room(30),
         name="forward",
     )(est, *halo, *weights[:3])
 
 
-def backward(labels, got, blur, weights):
-    slots = labels.shape[0]
+def backward(got, blur, weights):
+    sources = got.shape[0]
     return pl.pallas_call(
         backward_body,
         out_shape=PARTS
@@ -338,21 +356,23 @@
             jax.ShapeDtypeStruct((VIEWS,) + CORE, jnp.bfloat16),
             jax.ShapeDtypeStruct((VIEWS,) + TIMES, jnp.float32),
         ),
-        grid_spec=pltpu.PrefetchScalarGridSpec(
-            num_scalar_prefetch=1,
-            grid=(VIEWS,),
-            in_specs=[once(*got.shape), per_view(*BLUR)] + BACK_SPECS,
-            out_specs=PART_SPECS + [per_view(*CORE), per_view(*TIMES)],
-            scratch_shapes=BACK_SCRATCH
-            + [
-                pltpu.SMEM((VIEWS * CZ,), jnp.int32),
-                pltpu.SMEM((slots,), jnp.int32),
-                pltpu.SMEM((VIEWS * CZ,), jnp.int32),
-            ],
-        ),
-        compiler_params=ROOM,
+        grid=(VIEWS,),
+        in_specs=[pl.BlockSpec(memory_space=pl.ANY), per_view(*BLUR)] + BACK_SPECS,
+        out_specs=PART_SPECS + [per_view(*CORE), per_view(*TIMES)],
+        scratch_shapes=BACK_SCRATCH
+        + [
+            pltpu.VMEM((sources, SLOTS * SIDE, SIDE), jnp.bfloat16),
+            pltpu.VMEM((sources, HALF_TILE, SIDE), jnp.bfloat16),
+            pltpu.VMEM((sources, SIDE), jnp.int32),
+            pltpu.SMEM((sources, SIDE), jnp.int32),
+            pltpu.SMEM((VIEWS * CZ,), jnp.int32),
+            pltpu.SMEM((sources * SLOTS,), jnp.int32),
+            pltpu.SMEM((VIEWS * CZ,), jnp.int32),
+            pltpu.SemaphoreType.DMA((3,)),
+        ],
+        compiler_params=room(38),
         name="backward",
-    )(labels, got, blur, *weights[3:])
+    )(got, blur, *weights[3:])
 
 
 def iterate(counted, est, halo, observed, weights):
@@ -360,14 +380,14 @@
         step_body,
         out_shape=PARTS,
         grid=(VIEWS,),
-        in_specs=[whole(*CORE)]
+        in_specs=[once(*CORE)]
         + HALO_SPECS
         + [per_view(*CORE), per_view(*TIMES)]
         + FRONT_SPECS
         + BACK_SPECS,
         out_specs=PART_SPECS,
         scratch_shapes=FRONT_SCRATCH + BACK_SCRATCH,
-        compiler_params=ROOM,
+        compiler_params=room(38),
         name="iterate",
     )(est, *halo, observed, counted, *weights)
 
@@ -418,7 +438,7 @@
             whole(*STRIP),
         ],
         out_specs=[whole(*shape.shape) for shape in out_shape],
-        compiler_params=ROOM,
+        compiler_params=room(12),
         name="join_x",
     )(mid, mid, up, down, from_left, from_right)
 
@@ -446,7 +466,7 @@
     return pl.pallas_call(
         last_join_body,
         out_shape=jax.ShapeDtypeStruct(CORE, jnp.float32),
-        compiler_params=ROOM,
+        compiler_params=room(20),
         name="last_join",
     )(est, mid, from_left, from_right, above, below)
 
@@ -496,9 +516,30 @@
     return pl.pallas_call(
         next_join_body,
         out_shape=(jax.ShapeDtypeStruct(CORE, jnp.float32), rows, rows, strip, strip),
-        compiler_params=ROOM,
+        compiler_params=room(24),
         name="next_join",
     )(est, mid, from_left, from_right, above, below, up, down, top, bot)
+
+
+def rims_body(first_ref, last_ref, top_ref, bot_ref):
+    top_ref[...] = first_ref[...].astype(jnp.bfloat16)
+    bot_ref[...] = last_ref[...].astype(jnp.bfloat16)
+
+
+def rims(est):
+    rows = jax.ShapeDtypeStruct(ROWS, jnp.bfloat16)
+    return pl.pallas_call(
+        rims_body,
+        out_shape=(rows, rows),
+        grid=(1,),
+        in_specs=[
+            pl.BlockSpec(ROWS, lambda i: (0, 0, 0)),
+            pl.BlockSpec(ROWS, lambda i: (0, SIDE // RIM - 1, 0)),
+        ],
+        out_specs=[whole(*ROWS), whole(*ROWS)],
+        compiler_params=room(8),
+        name="rims",
+    )(est, est)
 
 
 def edges_body(est_ref, top_ref, bot_ref, left_ref, right_ref):
@@ -517,7 +558,7 @@
     return pl.pallas_call(
         edges_body,
         out_shape=(strip, strip),
-        compiler_params=ROOM,
+        compiler_params=room(12),
         name="edges",
     )(est, top, bot)
 
@@ -554,8 +595,8 @@
 def local(tiles, tile_dest, tile_slot, psf, estimate):
     axes = ("gy", "gx")
     devices = lax.axis_size("gy") * lax.axis_size("gx")
-    top = shift(estimate[:, SIDE - RIM :].astype(jnp.bfloat16), "gy", 1)
-    bot = shift(estimate[:, :RIM].astype(jnp.bfloat16), "gy", -1)
+    first_rows, last_rows = rims(estimate)
+    top, bot = shift(last_rows, "gy", 1), shift(first_rows, "gy", -1)
     dest = tile_dest[:, 0]
     count = dest.shape[0]
     order = (jnp.arange(count) * 256 + tile_slot)[None, :]
@@ -572,8 +613,7 @@
     got = lax.all_to_all(packed, axes, split_axis=0, concat_axis=0, tiled=True)
     weights = weights_of(psf)
     blur = forward(estimate, (top, bot, left, right), weights)
-    labels = got[:, SLOTS * SIDE, :SLOTS].astype(jnp.int32).reshape(-1)
-    *parts, observed, counted = backward(labels, got, blur, weights)
+    *parts, observed, counted = backward(got, blur, weights)
     for repeat_index in range(ITERS):
         more = repeat_index + 1 < ITERS
         mid, up, down, goleft, goright = parts

time: 293 us -> 269 us (0.918)
  Pallas kernels: 81.9 us -> 57.9 us
  waiting for transfers between devices: 119 us -> 124 us
  other arithmetic: 6.07 us -> 1.84 us
    pallas_call x2 -> x3, Pallas kernels: 23.7 us -> 16.8 us  [the longest x1 16.1 us: iterate(): pl.pallas_call(step_body, out_shape=PARTS, grid=(VIEWS,), in_specs=[once(...]
    pallas_call x1, Pallas kernels: 12.8 us -> 8.11 us  [forward(): pl.pallas_call(forward_body, out_shape=jax.ShapeDtypeStruct((VIEWS,) + BL...]
    pallas_call x2, Pallas kernels: 5.46 us -> 0.84 us  [join_x(): pl.pallas_call(join_x_body, out_shape=out_shape, grid=(1,), in_specs=[pl....]
    pallas_call x1, Pallas kernels: 5.94 us -> 1.71 us  [next_join(): pl.pallas_call(next_join_body, out_shape=(jax.ShapeDtypeStruct(CORE, jnp....]
    unnamed x30 -> x44, local copies, waits for them, and re-layouts: 4.95 us -> 9.01 us
  transfers between devices with their start and end apart: 15 -> 15, of which waited for: 12 -> 13; matrix products, arithmetic and copies ran while one was open for 5% -> 4% of each run, Pallas kernels for 6% -> 5%
where the time goes in v1:
time: 269 us; the launch traced here: 268 us
  waiting for transfers between devices  124 us (46%)
  starting transfers between devices  67.3 us (25%)
  Pallas kernels  57.9 us (22%)
  local copies, waits for them, and re-layouts  11.7 us (4%)
  matrix products  5.46 us (2%)
    all_to_all x1, waiting for transfers between devices, local(): got = lax.all_to_all(packed, axes, split_axis=0, concat_axis=0, tiled=True)  80.8 us
    ppermute x14, starting transfers between devices, shift(): return lax.ppermute(values, axis, pairs)  56.1 us
    ppermute x14, waiting for transfers between devices, shift(): return lax.ppermute(values, axis, pairs)  42.7 us
    pallas_call x1, Pallas kernels, backward(): pl.pallas_call(backward_body, out_shape=PARTS + (jax.ShapeDtypeStruct((VI...  23 us
    pallas_call x1, Pallas kernels, iterate(): pl.pallas_call(step_body, out_shape=PARTS, grid=(VIEWS,), in_specs=[once(...  16.1 us
    all_to_all x1, starting transfers between devices, local(): got = lax.all_to_all(packed, axes, split_axis=0, concat_axis=0, tiled=True)  11.2 us
    unnamed x44, local copies, waits for them, and re-layouts  9.01 us
    pallas_call x1, Pallas kernels, forward(): pl.pallas_call(forward_body, out_shape=jax.ShapeDtypeStruct((VIEWS,) + BL...  8.11 us
  transfers between devices with their start and end apart: 15, of which 13 were waited for; matrix products, arithmetic and copies ran while one was open for 4% of the time, Pallas kernels for 5%

profile of v1, /device:TPU:15, one launch (start us, length us, event | category | flops | bytes accessed | tf_op | source)
XLA Modules:
  0.0 268.3 jit_solution(3900678421228690716)
XLA Ops:
  0.0 1.6 copy-done
  1.6 4.5 %collective-permute-start = (bf16[32,16,128]{2,1,0:T(8,128)(2,1)S(1)}, bf16[32,16,128]{2,1,0:T(8,128)(2,1)S(1)}, u32[]{:S(2)}, u32[]{:S(2)}) collective-permute-start(bf16[32,16,128]{2,1,0:T(8,128)(2,1)S(1)} %get-tuple-element.35), channel_id=1, source_target_pairs={{0,16},{16,32},{32,48},{48,64},{64,80},{80,96},{96,112},{1,17},{17... | collective-permute-start | bytes 393224 | tf_op jit(solution)/shard_map/ppermute | solution.py:29
  6.2 2.4 collective-permute-start.1
  8.6 0.1 select_reduce_fusion.1
  8.7 0.8 collective-permute-done.top_ref
  9.5 4.7 %collective-permute-done.1.bot_ref = bf16[32,16,128]{2,1,0:T(8,128)(2,1)S(1)} collective-permute-done((bf16[32,16,128]{2,1,0:T(8,128)(2,1)S(1)}, bf16[32,16,128]{2,1,0:T(8,128)(2,1)S(1)}, u32[]{:S(2)}, u32[]{:S(2)}) %collective-permute-start.1) | collective-permute-done | bytes 131104 | tf_op jit(solution)/shard_map/ppermute | solution.py:29
  14.3 0.7 edges.1
  15.1 0.6 copy-done.9
  15.7 4.5 %collective-permute-start.2 = (bf16[4,160,128]{2,1,0:T(8,128)(2,1)S(1)}, bf16[4,160,128]{2,1,0:T(8,128)(2,1)S(1)}, u32[]{:S(2)}, u32[]{:S(2)}) collective-permute-start(bf16[4,160,128]{2,1,0:T(8,128)(2,1)S(1)} %get-tuple-element.37), channel_id=1, source_target_pairs={{0,1},{1,2},{2,3},{3,4},{4,5},{5,6},{6,7},{7,8},{8,9},{9,10},{10,1... | collective-permute-start | bytes 491528 | tf_op jit(solution)/shard_map/ppermute | solution.py:29
  20.2 1.9 collective-permute-start.3
  22.2 1.0 select_convert_fusion.labels_ref
  23.2 5.0 %pack.1 = bf16[128,264,128]{2,1,0:T(8,128)(2,1)} custom-call(s32[128]{0:T(128)} %bitcast.23, bf16[128,128,128]{2,1,0:T(8,128)(2,1)} %tiles_ref.1, bf16[128,8,128]{2,1,0:T(8,128)(2,1)} %select_convert_fusion.labels_ref), custom_call_target="tpu_custom_call" | custom-call | tf_op jit(solution)/shard_map/pack/pallas_call | solution.py:64
  28.3 0.7 copy-done.15
  29.0 0.7 copy-done.17
  29.6 11.2 %all-to-all-start = ((bf16[128,264,128]{2,1,0:T(8,128)(2,1)}), bf16[128,264,128]{2,1,0:T(8,128)(2,1)}, u32[]{:S(2)}, u32[]{:S(2)}) async-start(bf16[128,264,128]{2,1,0:T(8,128)(2,1)} %pack.1), calls=%async_computation | async-start | bytes 17301504 | tf_op jit(solution)/shard_map/all_to_all | solution.py:613
  40.8 0.1 reduce_sum.9
  40.9 0.1 copy.31
  41.1 0.1 subtract_add_fusion.4
  41.2 0.5 fusion.6
  41.7 1.0 copy.34.wy_ref
  42.7 0.1 subtract_add_fusion.3
  42.8 0.5 fusion.7
  43.4 0.1 pad_add_fusion
  43.4 0.1 subtract_add_fusion.2
  43.6 0.8 fusion.14
  44.3 0.3 copy.33
  44.6 0.9 copy.36.wx_ref
  45.6 0.8 fusion.12
  46.3 0.1 copy.37
  46.4 0.1 compare_select_fusion
  46.6 1.4 fusion.1
  48.1 0.2 copy.47.bz_ref
  48.2 1.4 fusion
  49.7 0.2 copy.48.wz_ref
  49.9 8.1 %forward.1.blur_ref = f32[6,8,256,256]{3,2,1,0:T(8,128)S(1)} custom-call(f32[32,128,128]{2,1,0:T(8,128)S(1)} %copy-done.1, bf16[32,16,128]{2,1,0:T(8,128)(2,1)S(1)} %copy-done.10, bf16[32,16,128]{2,1,0:T(8,128)(2,1)S(1)} %copy-done.13, bf16[4,160,128]{2,1,0:T(8,128)(2,1)S(1)} %copy-done.16, bf16[4,160,128]{2,1,0:T(8,128)(2,1)S(1)} %copy-done.18, ...), custom_call_target="tpu_custom_call" | custom-call | tf_op jit(solution)/shard_map/forward/pallas_call | solution.py:338
  58.0 4.5 %copy-done.2 = f32[6,8,256,256]{3,2,1,0:T(8,128)} copy-done((f32[6,8,256,256]{3,2,1,0:T(8,128)}, f32[6,8,256,256]{3,2,1,0:T(8,128)S(1)}, u32[]{:S(2)}) %copy-start.2) | copy-done | bytes 12582936
  62.5 0.9 copy-done.3
  63.4 80.8 %all-to-all-done.got_ref = bf16[128,264,128]{2,1,0:T(8,128)(2,1)} async-done(((bf16[128,264,128]{2,1,0:T(8,128)(2,1)}), bf16[128,264,128]{2,1,0:T(8,128)(2,1)}, u32[]{:S(2)}, u32[]{:S(2)}) %all-to-all-start) | async-done | bytes 8650784 | tf_op jit(solution)/shard_map/all_to_all | solution.py:613
  144.2 23.0 %backward.1 = (f32[32,128,128]{2,1,0:T(8,128)S(1)}, f32[32,16,128]{2,1,0:T(8,128)S(1)}, f32[32,16,128]{2,1,0:T(8,128)S(1)}, f32[4,160,128]{2,1,0:T(8,128)S(1)}, ...) custom-call(bf16[128,264,128]{2,1,0:T(8,128)(2,1)} %all-to-all-done.got_ref, ...), custom_call_target="tpu_custom_call" | custom-call | tf_op jit(solution)/shard_map/backward/pallas_call | solution.py:352
  167.2 14.3 %collective-permute-start.4 = (f32[4,160,128]{2,1,0:T(8,128)S(1)}, f32[4,160,128]{2,1,0:T(8,128)S(1)}, u32[]{:S(2)}, u32[]{:S(2)}) collective-permute-start(f32[4,160,128]{2,1,0:T(8,128)S(1)} %get-tuple-element.43), channel_id=1, source_target_pairs={{0,1},{1,2},{2,3},{3,4},{4,5},{5,6},{6,7},{7,8},{8,9},{9,10},{10,1... | collective-permute-start | bytes 983048 | tf_op jit(solution)/shard_map/ppermute | solution.py:29
  181.5 1.9 collective-permute-start.5
  183.5 2.1 collective-permute-done.4.left_ref
  185.5 5.3 %collective-permute-done.5.right_ref = f32[4,160,128]{2,1,0:T(8,128)S(1)} collective-permute-done((f32[4,160,128]{2,1,0:T(8,128)S(1)}, f32[4,160,128]{2,1,0:T(8,128)S(1)}, u32[]{:S(2)}, u32[]{:S(2)}) %collective-permute-start.5) | collective-permute-done | bytes 327712 | tf_op jit(solution)/shard_map/ppermute | solution.py:29
  190.8 0.5 join_x.2
  191.4 2.1 collective-permute-start.6
  193.5 5.1 %collective-permute-start.7 = (bf16[96,16,128]{2,1,0:T(8,128)(2,1)S(1)}, bf16[96,16,128]{2,1,0:T(8,128)(2,1)S(1)}, u32[]{:S(2)}, u32[]{:S(2)}) collective-permute-start(bf16[96,16,128]{2,1,0:T(8,128)(2,1)S(1)} %get-tuple-element.48), channel_id=1, source_target_pairs={{16,0},{32,16},{48,32},{64,48},{80,64},{96,80},{112,96},{17,1},{33... | collective-permute-start | bytes 1179656 | tf_op jit(solution)/shard_map/ppermute | solution.py:29
  198.5 3.8 %collective-permute-done.6.above_ref = bf16[96,16,128]{2,1,0:T(8,128)(2,1)S(1)} collective-permute-done((bf16[96,16,128]{2,1,0:T(8,128)(2,1)S(1)}, bf16[96,16,128]{2,1,0:T(8,128)(2,1)S(1)}, u32[]{:S(2)}, u32[]{:S(2)}) %collective-permute-start.6) | collective-permute-done | bytes 393248 | tf_op jit(solution)/shard_map/ppermute | solution.py:29
  202.3 4.2 %collective-permute-done.7.below_ref = bf16[96,16,128]{2,1,0:T(8,128)(2,1)S(1)} collective-permute-done((bf16[96,16,128]{2,1,0:T(8,128)(2,1)S(1)}, bf16[96,16,128]{2,1,0:T(8,128)(2,1)S(1)}, u32[]{:S(2)}, u32[]{:S(2)}) %collective-permute-start.7) | collective-permute-done | bytes 393248 | tf_op jit(solution)/shard_map/ppermute | solution.py:29
  206.5 1.7 next_join.1
  208.2 5.1 %collective-permute-start.8 = (bf16[4,160,128]{2,1,0:T(8,128)(2,1)S(1)}, bf16[4,160,128]{2,1,0:T(8,128)(2,1)S(1)}, u32[]{:S(2)}, u32[]{:S(2)}) collective-permute-start(bf16[4,160,128]{2,1,0:T(8,128)(2,1)S(1)} %get-tuple-element.54), channel_id=1, source_target_pairs={{0,1},{1,2},{2,3},{3,4},{4,5},{5,6},{6,7},{7,8},{8,9},{9,10},{10,1... | collective-permute-start | bytes 491528 | tf_op jit(solution)/shard_map/ppermute | solution.py:29
  213.3 1.9 collective-permute-start.9
  215.2 1.5 collective-permute-done.8.left_ref
  216.7 4.1 %collective-permute-done.9.right_ref = bf16[4,160,128]{2,1,0:T(8,128)(2,1)S(1)} collective-permute-done((bf16[4,160,128]{2,1,0:T(8,128)(2,1)S(1)}, bf16[4,160,128]{2,1,0:T(8,128)(2,1)S(1)}, u32[]{:S(2)}, u32[]{:S(2)}) %collective-permute-start.9) | collective-permute-done | bytes 163872 | tf_op jit(solution)/shard_map/ppermute | solution.py:29
  220.8 16.1 %iterate.1 = (f32[32,128,128]{2,1,0:T(8,128)S(1)}, f32[32,16,128]{2,1,0:T(8,128)S(1)}, f32[32,16,128]{2,1,0:T(8,128)S(1)}, f32[4,160,128]{2,1,0:T(8,128)S(1)}, f32[4,160,128]{2,1,0:T(8,128)S(1)}) custom-call(f32[32,128,128]{2,1,0:T(8,128)S(1)} %get-tuple-element.51.est_ref, bf16[32,16,128]{2,1,0:T(8,128)(2,1)S(1)} %get-tuple-element.52.top_ref, ...), custom_call_target="tpu_custom_call" | custom-call | tf_op jit(solution)/shard_map/iterate/pallas_call | solution.py:379
  236.9 1.9 collective-permute-start.10
  238.8 2.4 collective-permute-start.11
  241.3 2.4 collective-permute-done.10.left_ref
  243.7 4.5 %collective-permute-done.11.right_ref = f32[4,160,128]{2,1,0:T(8,128)S(1)} collective-permute-done((f32[4,160,128]{2,1,0:T(8,128)S(1)}, f32[4,160,128]{2,1,0:T(8,128)S(1)}, u32[]{:S(2)}, u32[]{:S(2)}) %collective-permute-start.11) | collective-permute-done | bytes 327712 | tf_op jit(solution)/shard_map/ppermute | solution.py:29
  248.1 0.3 join_x.3
  248.4 4.6 %collective-permute-start.12 = (f32[32,16,128]{2,1,0:T(8,128)S(1)}, f32[32,16,128]{2,1,0:T(8,128)S(1)}, u32[]{:S(2)}, u32[]{:S(2)}) collective-permute-start(f32[32,16,128]{2,1,0:T(8,128)S(1)} %get-tuple-element.63), channel_id=1, source_target_pairs={{0,16},{16,32},{32,48},{48,64},{64,80},{80,96},{96,112},{1,17},{17... | collective-permute-start | bytes 786440 | tf_op jit(solution)/shard_map/ppermute | solution.py:29
  253.0 3.4 %collective-permute-start.13 = (f32[32,16,128]{2,1,0:T(8,128)S(1)}, f32[32,16,128]{2,1,0:T(8,128)S(1)}, u32[]{:S(2)}, u32[]{:S(2)}) collective-permute-start(f32[32,16,128]{2,1,0:T(8,128)S(1)} %get-tuple-element.64), channel_id=1, source_target_pairs={{16,0},{32,16},{48,32},{64,48},{80,64},{96,80},{112,96},{17,1},{33... | collective-permute-start | bytes 786440 | tf_op jit(solution)/shard_map/ppermute | solution.py:29
  256.5 3.2 %collective-permute-done.12.above_ref = f32[32,16,128]{2,1,0:T(8,128)S(1)} collective-permute-done((f32[32,16,128]{2,1,0:T(8,128)S(1)}, f32[32,16,128]{2,1,0:T(8,128)S(1)}, u32[]{:S(2)}, u32[]{:S(2)}) %collective-permute-start.12) | collective-permute-done | bytes 262176 | tf_op jit(solution)/shard_map/ppermute | solution.py:29
  259.7 6.2 %collective-permute-done.13.below_ref = f32[32,16,128]{2,1,0:T(8,128)S(1)} collective-permute-done((f32[32,16,128]{2,1,0:T(8,128)S(1)}, f32[32,16,128]{2,1,0:T(8,128)S(1)}, u32[]{:S(2)}, u32[]{:S(2)}) %collective-permute-start.13) | collective-permute-done | bytes 262176 | tf_op jit(solution)/shard_map/ppermute | solution.py:29
  265.9 2.4 last_join.1
  (52 shorter events, 0.3 us)
Async XLA Ops:
  0.0 1.6 copy-start
  1.6 7.0 %copy-start.21 = (s32[128]{0:T(128)S(1)}, s32[128]{0:T(128)}, u32[]{:S(2)}) copy-start(s32[128]{0:T(128)} %param.7) | copy-start | bytes 1540
  1.6 7.0 %copy-start.20 = (s32[128,1]{0,1:T(1,128)S(1)}, s32[128,1]{0,1:T(1,128)}, u32[]{:S(2)}) copy-start(s32[128,1]{0,1:T(1,128)} %param.6) | copy-start | bytes 1540
  1.6 12.7 %copy-start.1 = (f32[32,128,128]{2,1,0:T(8,128)S(1)}, f32[32,128,128]{2,1,0:T(8,128)}, u32[]{:S(2)}) copy-start(f32[32,128,128]{2,1,0:T(8,128)} %est_ref.5) | copy-start | bytes 6291460
  1.6 7.9 %collective-permute-start = (bf16[32,16,128]{2,1,0:T(8,128)(2,1)S(1)}, bf16[32,16,128]{2,1,0:T(8,128)(2,1)S(1)}, u32[]{:S(2)}, u32[]{:S(2)}) collective-permute-start(bf16[32,16,128]{2,1,0:T(8,128)(2,1)S(1)} %get-tuple-element.35), channel_id=1, source_target_pairs={{0,16},{16,32},{32,48},{48,64},{64,80},{80,96},{96,112},{1,17},{17... | collective-permute-start | bytes 393224 | tf_op jit(solution)/shard_map/ppermute | solution.py:29
  6.2 8.1 %collective-permute-start.1 = (bf16[32,16,128]{2,1,0:T(8,128)(2,1)S(1)}, bf16[32,16,128]{2,1,0:T(8,128)(2,1)S(1)}, u32[]{:S(2)}, u32[]{:S(2)}) collective-permute-start(bf16[32,16,128]{2,1,0:T(8,128)(2,1)S(1)} %get-tuple-element.36), channel_id=1, source_target_pairs={{16,0},{32,16},{48,32},{64,48},{80,64},{96,80},{112,96},{17,1},{33... | collective-permute-start | bytes 393224 | tf_op jit(solution)/shard_map/ppermute | solution.py:29
  14.3 0.8 copy-start.12
  15.0 0.6 copy-start.9
  15.7 12.6 %collective-permute-start.2 = (bf16[4,160,128]{2,1,0:T(8,128)(2,1)S(1)}, bf16[4,160,128]{2,1,0:T(8,128)(2,1)S(1)}, u32[]{:S(2)}, u32[]{:S(2)}) collective-permute-start(bf16[4,160,128]{2,1,0:T(8,128)(2,1)S(1)} %get-tuple-element.37), channel_id=1, source_target_pairs={{0,1},{1,2},{2,3},{3,4},{4,5},{5,6},{6,7},{7,8},{8,9},{9,10},{10,1... | collective-permute-start | bytes 491528 | tf_op jit(solution)/shard_map/ppermute | solution.py:29
  20.2 8.7 %collective-permute-start.3 = (bf16[4,160,128]{2,1,0:T(8,128)(2,1)S(1)}, bf16[4,160,128]{2,1,0:T(8,128)(2,1)S(1)}, u32[]{:S(2)}, u32[]{:S(2)}) collective-permute-start(bf16[4,160,128]{2,1,0:T(8,128)(2,1)S(1)} %get-tuple-element.38), channel_id=1, source_target_pairs={{1,0},{2,1},{3,2},{4,3},{5,4},{6,5},{7,6},{8,7},{9,8},{10,9},{11,1... | collective-permute-start | bytes 491528 | tf_op jit(solution)/shard_map/ppermute | solution.py:29
  28.3 12.5 %copy-start.19 = (f32[6,3,31]{2,1,0:T(4,128)S(1)}, f32[6,3,31]{2,1,0:T(4,128)}, u32[]{:S(2)}) copy-start(f32[6,3,31]{2,1,0:T(4,128)} %param.8) | copy-start | bytes 6700
  28.3 0.7 copy-start.15
  29.0 0.7 copy-start.17
  29.6 114.6 %all-to-all-start = ((bf16[128,264,128]{2,1,0:T(8,128)(2,1)}), bf16[128,264,128]{2,1,0:T(8,128)(2,1)}, u32[]{:S(2)}, u32[]{:S(2)}) async-start(bf16[128,264,128]{2,1,0:T(8,128)(2,1)} %pack.1), calls=%async_computation | async-start | bytes 17301504 | tf_op jit(solution)/shard_map/all_to_all | solution.py:613
  46.6 3.3 %copy-start.5 = (bf16[256,768]{1,0:T(8,128)(2,1)S(1)}, bf16[256,768]{1,0:T(8,128)(2,1)}, u32[]{:S(2)}) copy-start(bf16[256,768]{1,0:T(8,128)(2,1)} %copy.36.wx_ref) | copy-start | bytes 1179652
  46.6 3.3 %copy-start.7 = (bf16[6,128,160]{2,1,0:T(8,128)(2,1)S(1)}, bf16[6,128,160]{2,1,0:T(8,128)(2,1)}, u32[]{:S(2)}) copy-start(bf16[6,128,160]{2,1,0:T(8,128)(2,1)} %copy.34.wy_ref) | copy-start | bytes 737284
  46.6 3.3 %copy-start.10 = (bf16[32,16,128]{2,1,0:T(8,128)(2,1)S(1)}, bf16[32,16,128]{2,1,0:T(8,128)(2,1)}, u32[]{:S(2)}) copy-start(bf16[32,16,128]{2,1,0:T(8,128)(2,1)} %copy-done.9) | copy-start | bytes 393220
  46.6 3.3 %copy-start.13 = (bf16[32,16,128]{2,1,0:T(8,128)(2,1)S(1)}, bf16[32,16,128]{2,1,0:T(8,128)(2,1)}, u32[]{:S(2)}) copy-start(bf16[32,16,128]{2,1,0:T(8,128)(2,1)} %copy-done.12) | copy-start | bytes 393220
  46.6 3.3 %copy-start.16 = (bf16[4,160,128]{2,1,0:T(8,128)(2,1)S(1)}, bf16[4,160,128]{2,1,0:T(8,128)(2,1)}, u32[]{:S(2)}) copy-start(bf16[4,160,128]{2,1,0:T(8,128)(2,1)} %copy-done.15) | copy-start | bytes 491524
  46.6 3.3 %copy-start.18 = (bf16[4,160,128]{2,1,0:T(8,128)(2,1)S(1)}, bf16[4,160,128]{2,1,0:T(8,128)(2,1)}, u32[]{:S(2)}) copy-start(bf16[4,160,128]{2,1,0:T(8,128)(2,1)} %copy-done.17) | copy-start | bytes 491524
  58.0 4.5 %copy-start.2 = (f32[6,8,256,256]{3,2,1,0:T(8,128)}, f32[6,8,256,256]{3,2,1,0:T(8,128)S(1)}, u32[]{:S(2)}) copy-start(f32[6,8,256,256]{3,2,1,0:T(8,128)S(1)} %forward.1.blur_ref) | copy-start | bytes 37748740
  62.5 0.9 copy-start.3
  167.2 39.2 %copy-start.11 = (bf16[32,16,128]{2,1,0:T(8,128)(2,1)S(1)}, bf16[32,16,128]{2,1,0:T(8,128)(2,1)}, u32[]{:S(2)}) copy-start(bf16[32,16,128]{2,1,0:T(8,128)(2,1)} %copy-done.9) | copy-start | bytes 393220
  167.2 39.2 %copy-start.14 = (bf16[32,16,128]{2,1,0:T(8,128)(2,1)S(1)}, bf16[32,16,128]{2,1,0:T(8,128)(2,1)}, u32[]{:S(2)}) copy-start(bf16[32,16,128]{2,1,0:T(8,128)(2,1)} %copy-done.12) | copy-start | bytes 393220
  167.2 18.3 %collective-permute-start.4 = (f32[4,160,128]{2,1,0:T(8,128)S(1)}, f32[4,160,128]{2,1,0:T(8,128)S(1)}, u32[]{:S(2)}, u32[]{:S(2)}) collective-permute-start(f32[4,160,128]{2,1,0:T(8,128)S(1)} %get-tuple-element.43), channel_id=1, source_target_pairs={{0,1},{1,2},{2,3},{3,4},{4,5},{5,6},{6,7},{7,8},{8,9},{9,10},{10,1... | collective-permute-start | bytes 983048 | tf_op jit(solution)/shard_map/ppermute | solution.py:29
  181.5 9.3 %collective-permute-start.5 = (f32[4,160,128]{2,1,0:T(8,128)S(1)}, f32[4,160,128]{2,1,0:T(8,128)S(1)}, u32[]{:S(2)}, u32[]{:S(2)}) collective-permute-start(f32[4,160,128]{2,1,0:T(8,128)S(1)} %get-tuple-element.44), channel_id=1, source_target_pairs={{1,0},{2,1},{3,2},{4,3},{5,4},{6,5},{7,6},{8,7},{9,8},{10,9},{11,1... | collective-permute-start | bytes 983048 | tf_op jit(solution)/shard_map/ppermute | solution.py:29
  191.4 29.5 %copy-start.4 = (bf16[6,256,256]{2,1,0:T(8,128)(2,1)S(1)}, bf16[6,256,256]{2,1,0:T(8,128)(2,1)}, u32[]{:S(2)}) copy-start(bf16[6,256,256]{2,1,0:T(8,128)(2,1)} %copy-done.3) | copy-start | bytes 2359300
  191.4 29.5 %copy-start.6 = (bf16[256,768]{1,0:T(8,128)(2,1)S(1)}, bf16[256,768]{1,0:T(8,128)(2,1)}, u32[]{:S(2)}) copy-start(bf16[256,768]{1,0:T(8,128)(2,1)} %copy.36.wx_ref) | copy-start | bytes 1179652
  191.4 29.4 %copy-start.8 = (bf16[6,128,160]{2,1,0:T(8,128)(2,1)S(1)}, bf16[6,128,160]{2,1,0:T(8,128)(2,1)}, u32[]{:S(2)}) copy-start(bf16[6,128,160]{2,1,0:T(8,128)(2,1)} %copy.34.wy_ref) | copy-start | bytes 737284
  191.4 10.9 %collective-permute-start.6 = (bf16[96,16,128]{2,1,0:T(8,128)(2,1)S(1)}, bf16[96,16,128]{2,1,0:T(8,128)(2,1)S(1)}, u32[]{:S(2)}, u32[]{:S(2)}) collective-permute-start(bf16[96,16,128]{2,1,0:T(8,128)(2,1)S(1)} %get-tuple-element.47), channel_id=1, source_target_pairs={{0,16},{16,32},{32,48},{48,64},{64,80},{80,96},{96,112},{1,17},{17... | collective-permute-start | bytes 1179656 | tf_op jit(solution)/shard_map/ppermute | solution.py:29
  193.5 13.0 %collective-permute-start.7 = (bf16[96,16,128]{2,1,0:T(8,128)(2,1)S(1)}, bf16[96,16,128]{2,1,0:T(8,128)(2,1)S(1)}, u32[]{:S(2)}, u32[]{:S(2)}) collective-permute-start(bf16[96,16,128]{2,1,0:T(8,128)(2,1)S(1)} %get-tuple-element.48), channel_id=1, source_target_pairs={{16,0},{32,16},{48,32},{64,48},{80,64},{96,80},{112,96},{17,1},{33... | collective-permute-start | bytes 1179656 | tf_op jit(solution)/shard_map/ppermute | solution.py:29
  208.2 8.5 %collective-permute-start.8 = (bf16[4,160,128]{2,1,0:T(8,128)(2,1)S(1)}, bf16[4,160,128]{2,1,0:T(8,128)(2,1)S(1)}, u32[]{:S(2)}, u32[]{:S(2)}) collective-permute-start(bf16[4,160,128]{2,1,0:T(8,128)(2,1)S(1)} %get-tuple-element.54), channel_id=1, source_target_pairs={{0,1},{1,2},{2,3},{3,4},{4,5},{5,6},{6,7},{7,8},{8,9},{9,10},{10,1... | collective-permute-start | bytes 491528 | tf_op jit(solution)/shard_map/ppermute | solution.py:29
  213.3 7.5 %collective-permute-start.9 = (bf16[4,160,128]{2,1,0:T(8,128)(2,1)S(1)}, bf16[4,160,128]{2,1,0:T(8,128)(2,1)S(1)}, u32[]{:S(2)}, u32[]{:S(2)}) collective-permute-start(bf16[4,160,128]{2,1,0:T(8,128)(2,1)S(1)} %get-tuple-element.55), channel_id=1, source_target_pairs={{1,0},{2,1},{3,2},{4,3},{5,4},{6,5},{7,6},{8,7},{9,8},{10,9},{11,1... | collective-permute-start | bytes 491528 | tf_op jit(solution)/shard_map/ppermute | solution.py:29
  236.9 6.8 %collective-permute-start.10 = (f32[4,160,128]{2,1,0:T(8,128)S(1)}, f32[4,160,128]{2,1,0:T(8,128)S(1)}, u32[]{:S(2)}, u32[]{:S(2)}) collective-permute-start(f32[4,160,128]{2,1,0:T(8,128)S(1)} %get-tuple-element.59), channel_id=1, source_target_pairs={{0,1},{1,2},{2,3},{3,4},{4,5},{5,6},{6,7},{7,8},{8,9},{9,10},{10,1... | collective-permute-start | bytes 983048 | tf_op jit(solution)/shard_map/ppermute | solution.py:29
  238.8 9.3 %collective-permute-start.11 = (f32[4,160,128]{2,1,0:T(8,128)S(1)}, f32[4,160,128]{2,1,0:T(8,128)S(1)}, u32[]{:S(2)}, u32[]{:S(2)}) collective-permute-start(f32[4,160,128]{2,1,0:T(8,128)S(1)} %get-tuple-element.60), channel_id=1, source_target_pairs={{1,0},{2,1},{3,2},{4,3},{5,4},{6,5},{7,6},{8,7},{9,8},{10,9},{11,1... | collective-permute-start | bytes 983048 | tf_op jit(solution)/shard_map/ppermute | solution.py:29
  248.4 11.2 %collective-permute-start.12 = (f32[32,16,128]{2,1,0:T(8,128)S(1)}, f32[32,16,128]{2,1,0:T(8,128)S(1)}, u32[]{:S(2)}, u32[]{:S(2)}) collective-permute-start(f32[32,16,128]{2,1,0:T(8,128)S(1)} %get-tuple-element.63), channel_id=1, source_target_pairs={{0,16},{16,32},{32,48},{48,64},{64,80},{80,96},{96,112},{1,17},{17... | collective-permute-start | bytes 786440 | tf_op jit(solution)/shard_map/ppermute | solution.py:29
  253.0 12.9 %collective-permute-start.13 = (f32[32,16,128]{2,1,0:T(8,128)S(1)}, f32[32,16,128]{2,1,0:T(8,128)S(1)}, u32[]{:S(2)}, u32[]{:S(2)}) collective-permute-start(f32[32,16,128]{2,1,0:T(8,128)S(1)} %get-tuple-element.64), channel_id=1, source_target_pairs={{16,0},{32,16},{48,32},{64,48},{80,64},{96,80},{112,96},{17,1},{33... | collective-permute-start | bytes 786440 | tf_op jit(solution)/shard_map/ppermute | solution.py:29

commit v2 on v1

--- a/solution.py
+++ b/solution.py
@@ -78,6 +78,20 @@
         compiler_params=room(56),
         name="pack",
     )(tile_dest, tiles, labels)
+
+
+TOP_CODE = 32767
+KNEE = 8.0
+
+
+def encode(sums):
+    code = (sums / (sums + KNEE) * TOP_CODE + 0.5).astype(jnp.int32)
+    return jnp.minimum(code, TOP_CODE - 1).astype(jnp.int16)
+
+
+def decode(codes):
+    codes = codes.astype(jnp.int32).astype(jnp.float32)
+    return KNEE * codes / (TOP_CODE - codes)
 
 
 def side_by_side(pair):
@@ -166,8 +180,8 @@
             mine = lanes((EXT, SIDE)) // RIM == g
             goleft = jnp.where(mine, pltpu.roll(strip, RIM * g, 1), goleft)
             goright = jnp.where(mine, pltpu.roll(strip, (SIDE + RIM * g - RIM) % SIDE, 1), goright)
-        goleft_ref[q] = goleft
-        goright_ref[q] = goright
+        goleft_ref[q] = encode(goleft)
+        goright_ref[q] = encode(goright)
 
 
 def forward_body(
@@ -191,7 +205,7 @@
     got_ref, blur_ref, bx_ref, by_ref, bz_ref,
     mid_ref, up_ref, down_ref, goleft_ref, goright_ref, obs_ref, count_ref,
     rz_ref, ry_ref, tiles_ref, names_ref, wide_ref, label_ref, head_ref, next_ref, times_ref,
-    sems,
+    many_ref, plane_ref, sems,
 ):
     v = pl.program_id(0)
     sources = got_ref.shape[0]
@@ -212,22 +226,33 @@
             head_ref[i] = 0
             times_ref[i] = 0
 
+        head_ref[VIEWS * CZ] = 0
+        times_ref[VIEWS * CZ] = 0
+        for w in range(VIEWS):
+            many_ref[w] = 0
+
         names.wait()
         wide_ref[...] = names_ref[...].astype(jnp.float32)[:, 0, :].astype(jnp.int32)
         labels = pltpu.make_async_copy(wide_ref, label_ref, sems.at[2])
         labels.start()
         labels.wait()
 
-        @pl.loop(0, sources)
+        @pl.loop(0, sources, unroll=2)
         def _(i):
             for r in range(SLOTS):
-                label = label_ref[i, r]
-
-                @pl.when(label >= 0)
+                name = label_ref[i, r]
+                label = jnp.where(name < 0, VIEWS * CZ, name)
+                times = times_ref[label]
+                next_ref[i * SLOTS + r] = head_ref[label]
+                head_ref[label] = i * SLOTS + r
+                times_ref[label] = times + 1
+
+                @pl.when((times == 1) & (name >= 0))
                 def _():
-                    next_ref[i * SLOTS + r] = head_ref[label]
-                    head_ref[label] = i * SLOTS + r
-                    times_ref[label] = times_ref[label] + 1
+                    view = label // CZ
+                    many = many_ref[view]
+                    plane_ref[view * CZ + many] = label
+                    many_ref[view] = many + 1
 
         tiles.wait()
 
@@ -243,19 +268,17 @@
         )
         obs_ref[0, z] = jnp.where(times > 0, tile(first), jnp.zeros((), jnp.bfloat16))
 
-    @pl.loop(0, CZ)
-    def _(z):
-        times = times_ref[v * CZ + z]
-
-        @pl.when(times > 1)
-        def _():
-            def add(_, carry):
-                at, total = carry
-                return next_ref[at], total + tile(at).astype(jnp.float32)
-
-            first = head_ref[v * CZ + z]
-            total = jnp.zeros((SIDE, SIDE), jnp.float32)
-            obs_ref[0, z] = lax.fori_loop(0, times, add, (first, total))[1].astype(jnp.bfloat16)
+    @pl.loop(0, many_ref[v])
+    def _(i):
+        plane = plane_ref[v * CZ + i]
+
+        def add(_, carry):
+            at, total = carry
+            return next_ref[at], total + tile(at).astype(jnp.float32)
+
+        total = jnp.zeros((SIDE, SIDE), jnp.float32)
+        total = lax.fori_loop(0, times_ref[plane], add, (head_ref[plane], total))[1]
+        obs_ref[0, plane - v * CZ] = total.astype(jnp.bfloat16)
 
     @pl.loop(0, SIDE // RIM, unroll=UZ)
     def _(i):
@@ -320,8 +343,9 @@
 FRONT_SPECS = [once(2 * SIDE, VIEWS * SIDE), per_view(SIDE, EXT), per_view(*Z_BAND)]
 BACK_SPECS = [once(VIEWS * SIDE, 2 * SIDE), per_view(EXT, SIDE), per_view(*Z_BAND)]
 PART_SPECS = [whole(*CORE), whole(*ROWS), whole(*ROWS), whole(*STRIP), whole(*STRIP)]
-PARTS = tuple(
-    jax.ShapeDtypeStruct(shape, jnp.float32) for shape in (CORE, ROWS, ROWS, STRIP, STRIP)
+PARTS = tuple(jax.ShapeDtypeStruct(shape, jnp.float32) for shape in (CORE, ROWS, ROWS)) + (
+    jax.ShapeDtypeStruct(STRIP, jnp.int16),
+    jax.ShapeDtypeStruct(STRIP, jnp.int16),
 )
 FRONT_SCRATCH = [
     pltpu.VMEM((UX, ZPER, EXT, 2 * SIDE), jnp.bfloat16),
@@ -365,8 +389,10 @@
             pltpu.VMEM((sources, HALF_TILE, SIDE), jnp.bfloat16),
             pltpu.VMEM((sources, SIDE), jnp.int32),
             pltpu.SMEM((sources, SIDE), jnp.int32),
-            pltpu.SMEM((VIEWS * CZ,), jnp.int32),
+            pltpu.SMEM((VIEWS * CZ + 1,), jnp.int32),
             pltpu.SMEM((sources * SLOTS,), jnp.int32),
+            pltpu.SMEM((VIEWS * CZ + 1,), jnp.int32),
+            pltpu.SMEM((VIEWS,), jnp.int32),
             pltpu.SMEM((VIEWS * CZ,), jnp.int32),
             pltpu.SemaphoreType.DMA((3,)),
         ],
@@ -393,38 +419,34 @@
 
 
 def beside(q, g, rows, left_ref, right_ref):
-    low = pltpu.roll(left_ref[q, rows], (SIDE - RIM * g) % SIDE, 1)
-    high = pltpu.roll(right_ref[q, rows], (2 * SIDE - RIM - RIM * g) % SIDE, 1)
+    low = pltpu.roll(decode(left_ref[q, rows]), (SIDE - RIM * g) % SIDE, 1)
+    high = pltpu.roll(decode(right_ref[q, rows]), (2 * SIDE - RIM - RIM * g) % SIDE, 1)
     lane = lanes(low.shape)
     return jnp.where(lane < RIM, low, jnp.where(lane >= SIDE - RIM, high, 0.0))
 
 
-def in_two(values):
-    high = values.astype(jnp.bfloat16)
-    return high, (values - high.astype(jnp.float32)).astype(jnp.bfloat16)
-
-
 def join_x_body(first_ref, last_ref, up_ref, down_ref, left_ref, right_ref, *outs):
+    goup_ref, godown_ref = outs[:2]
+
     @pl.loop(0, ZPER, unroll=True)
     def _(q):
         for g in range(GROUPS):
             z = g * ZPER + q
             head = up_ref[z] + beside(q, g, slice(0, RIM), left_ref, right_ref)
             tail = down_ref[z] + beside(q, g, slice(SIDE + RIM, EXT), left_ref, right_ref)
-            outs[0][z], outs[1][z] = head, tail
+            goup_ref[z], godown_ref[z] = encode(head), encode(tail)
             if len(outs) > 2:
+                outs[2][z], outs[3][z] = head, tail
                 own = first_ref[z] + beside(q, g, slice(RIM, 2 * RIM), left_ref, right_ref)
-                outs[2][z], outs[2][CZ + z] = in_two(head)
-                outs[2][2 * CZ + z] = own.astype(jnp.bfloat16)
+                goup_ref[CZ + z] = encode(own)
                 own = last_ref[z] + beside(q, g, slice(SIDE, SIDE + RIM), left_ref, right_ref)
-                outs[3][z], outs[3][CZ + z] = in_two(tail)
-                outs[3][2 * CZ + z] = own.astype(jnp.bfloat16)
+                godown_ref[CZ + z] = encode(own)
 
 
 def join_x(mid, up, down, from_left, from_right, more):
     rows = jax.ShapeDtypeStruct(ROWS, jnp.float32)
-    message = jax.ShapeDtypeStruct((3 * CZ, RIM, SIDE), jnp.bfloat16)
-    out_shape = (rows, rows) + ((message, message) if more else ())
+    message = jax.ShapeDtypeStruct(((1 + more) * CZ, RIM, SIDE), jnp.int16)
+    out_shape = (message, message) + ((rows, rows) if more else ())
     return pl.pallas_call(
         join_x_body,
         out_shape=out_shape,
@@ -458,7 +480,8 @@
         for g in range(GROUPS):
             z = g * ZPER + q
             out_ref[z] = joined(
-                est_ref, mid_ref, left_ref, right_ref, q, g, above_ref[z], below_ref[z]
+                est_ref, mid_ref, left_ref, right_ref, q, g,
+                decode(above_ref[z]), decode(below_ref[z]),
             )
 
 
@@ -487,9 +510,6 @@
     up_ref, down_ref, top_ref, bot_ref,
     out_ref, newtop_ref, newbot_ref, goleft_ref, goright_ref,
 ):
-    def whole_of(ref, z):
-        return ref[z].astype(jnp.float32) + ref[CZ + z].astype(jnp.float32)
-
     @pl.loop(0, ZPER, unroll=2)
     def _(q):
         planes = []
@@ -497,13 +517,13 @@
             z = g * ZPER + q
             now = joined(
                 est_ref, mid_ref, left_ref, right_ref, q, g,
-                whole_of(above_ref, z), whole_of(below_ref, z),
+                decode(above_ref[z]), decode(below_ref[z]),
             )
             out_ref[z] = now
-            total = above_ref[2 * CZ + z].astype(jnp.float32) + up_ref[z]
+            total = decode(above_ref[CZ + z]) + up_ref[z]
             newtop = top_ref[z].astype(jnp.float32) * total / VIEWS
             newtop_ref[z] = newtop.astype(jnp.bfloat16)
-            total = below_ref[2 * CZ + z].astype(jnp.float32) + down_ref[z]
+            total = decode(below_ref[CZ + z]) + down_ref[z]
             newbot = bot_ref[z].astype(jnp.float32) * total / VIEWS
             newbot_ref[z] = newbot.astype(jnp.bfloat16)
             planes.append(jnp.concatenate([newtop, now, newbot], axis=0))
@@ -537,7 +557,7 @@
             pl.BlockSpec(ROWS, lambda i: (0, SIDE // RIM - 1, 0)),
         ],
         out_specs=[whole(*ROWS), whole(*ROWS)],
-        compiler_params=room(8),
+        compiler_params=room(56),
         name="rims",
     )(est, est)
 
@@ -606,6 +626,7 @@
     one = jnp.where(first < count * 256, first % 256, -1)
     two = jnp.where(last > first, last % 256, -1)
     labels = jnp.where(lanes((devices, HALF_TILE, SIDE)) == 0, one, two).astype(jnp.bfloat16)
+    labels, top, bot = lax.optimization_barrier((labels, top, bot))
     low, high = edges(estimate, top, bot)
     left, right = shift(high, "gx", 1), shift(low, "gx", -1)
     packed = pack(dest, tiles, labels)
@@ -620,11 +641,11 @@
         sides = shift(goright, "gx", 1), shift(goleft, "gx", -1)
         sent = join_x(mid, up, down, *sides, more)
         if not more:
-            up, down = sent
+            goup, godown = sent
             return last_join(
-                estimate, mid, *sides, shift(down, "gy", 1), shift(up, "gy", -1)
+                estimate, mid, *sides, shift(godown, "gy", 1), shift(goup, "gy", -1)
             )
-        up, down, goup, godown = sent
+        goup, godown, up, down = sent
         estimate, top, bot, low, high = next_join(
             estimate, mid, *sides, shift(godown, "gy", 1), shift(goup, "gy", -1), up, down, top, bot
         )

time: 269 us -> 253 us (0.941)
  waiting for transfers between devices: 124 us -> 111 us
  starting transfers between devices: 67.3 us -> 64.4 us
    ppermute x14, waiting for transfers between devices: 42.7 us -> 30.4 us  [shift(): return lax.ppermute(values, axis, pairs)]
    ppermute x14, starting transfers between devices: 56.1 us -> 53.2 us  [shift(): return lax.ppermute(values, axis, pairs)]
    unnamed x44 -> x42, local copies, waits for them, and re-layouts: 9.01 us -> 7.43 us
  transfers between devices with their start and end apart: 15 -> 15, of which waited for: 13 -> 11; matrix products, arithmetic and copies ran while one was open for 4% -> 4% of each run, Pallas kernels for 5% -> 5%
where the time goes in v2:
time: 253 us
  waiting for transfers between devices  111 us (44%)
  starting transfers between devices  64.4 us (25%)
  Pallas kernels  59.3 us (23%)
  local copies, waits for them, and re-layouts  10.2 us (4%)
  matrix products  5.46 us (2%)
    all_to_all x1, waiting for transfers between devices, local(): got = lax.all_to_all(packed, axes, split_axis=0, concat_axis=0, tiled=True)  80.8 us
    ppermute x14, starting transfers between devices, shift(): return lax.ppermute(values, axis, pairs)  53.2 us
    ppermute x14, waiting for transfers between devices, shift(): return lax.ppermute(values, axis, pairs)  30.4 us
    pallas_call x1, Pallas kernels, backward(): pl.pallas_call(backward_body, out_shape=PARTS + (jax.ShapeDtypeStruct((VI...  22.1 us
    pallas_call x1, Pallas kernels, iterate(): pl.pallas_call(step_body, out_shape=PARTS, grid=(VIEWS,), in_specs=[once(...  16.1 us
    all_to_all x1, starting transfers between devices, local(): got = lax.all_to_all(packed, axes, split_axis=0, concat_axis=0, tiled=True)  11.1 us
    pallas_call x1, Pallas kernels, forward(): pl.pallas_call(forward_body, out_shape=jax.ShapeDtypeStruct((VIEWS,) + BL...  8.11 us
    unnamed x42, local copies, waits for them, and re-layouts  7.43 us
  transfers between devices with their start and end apart: 15, of which 11 were waited for; matrix products, arithmetic and copies ran while one was open for 4% of the time, Pallas kernels for 5%

profile of v2, /device:TPU:15, one launch (start us, length us, event | category | flops | bytes accessed | tf_op | source)
XLA Modules:
  0.0 252.9 jit_solution(7319153669522058792)
XLA Ops:
  0.0 1.9 rims.1
  1.9 4.4 %collective-permute-start = (bf16[32,16,128]{2,1,0:T(8,128)(2,1)}, bf16[32,16,128]{2,1,0:T(8,128)(2,1)S(1)}, u32[]{:S(2)}, u32[]{:S(2)}) collective-permute-start(bf16[32,16,128]{2,1,0:T(8,128)(2,1)} %get-tuple-element.38), channel_id=1, source_target_pairs={{0,16},{16,32},{32,48},{48,64},{64,80},{80,96},{96,112},{1,17},{17... | collective-permute-start | bytes 393224 | tf_op jit(solution)/shard_map/ppermute | solution.py:29
  6.3 2.4 collective-permute-start.1
  8.8 0.1 select_reduce_fusion.1
  8.9 1.0 select_convert_fusion.labels_ref
  9.9 4.7 %collective-permute-done.1.bot_ref = bf16[32,16,128]{2,1,0:T(8,128)(2,1)S(1)} collective-permute-done((bf16[32,16,128]{2,1,0:T(8,128)(2,1)}, bf16[32,16,128]{2,1,0:T(8,128)(2,1)S(1)}, u32[]{:S(2)}, u32[]{:S(2)}) %collective-permute-start.1) | collective-permute-done | bytes 131104 | tf_op jit(solution)/shard_map/ppermute | solution.py:29
  14.6 0.8 edges.1
  15.4 0.6 copy-done.8
  16.1 4.5 %collective-permute-start.2 = (bf16[4,160,128]{2,1,0:T(8,128)(2,1)S(1)}, bf16[4,160,128]{2,1,0:T(8,128)(2,1)S(1)}, u32[]{:S(2)}, u32[]{:S(2)}) collective-permute-start(bf16[4,160,128]{2,1,0:T(8,128)(2,1)S(1)} %get-tuple-element.43), channel_id=1, source_target_pairs={{0,1},{1,2},{2,3},{3,4},{4,5},{5,6},{6,7},{7,8},{8,9},{9,10},{10,1... | collective-permute-start | bytes 491528 | tf_op jit(solution)/shard_map/ppermute | solution.py:29
  20.6 1.9 collective-permute-start.3
  22.5 5.1 %pack.1 = bf16[128,264,128]{2,1,0:T(8,128)(2,1)} custom-call(s32[128]{0:T(128)} %bitcast.23, bf16[128,128,128]{2,1,0:T(8,128)(2,1)} %tiles_ref.1, bf16[128,8,128]{2,1,0:T(8,128)(2,1)} %select_convert_fusion.labels_ref), custom_call_target="tpu_custom_call" | custom-call | tf_op jit(solution)/shard_map/pack/pallas_call | solution.py:64
  27.6 0.0 copy-start.18
  27.7 0.7 copy-done.14
  28.3 0.7 copy-done.16
  29.0 11.1 %all-to-all-start = ((bf16[128,264,128]{2,1,0:T(8,128)(2,1)}), bf16[128,264,128]{2,1,0:T(8,128)(2,1)}, u32[]{:S(2)}, u32[]{:S(2)}) async-start(bf16[128,264,128]{2,1,0:T(8,128)(2,1)} %pack.1), calls=%async_computation | async-start | bytes 17301504 | tf_op jit(solution)/shard_map/all_to_all | solution.py:634
  40.1 0.1 reduce_sum.9
  40.2 0.1 copy.31
  40.3 0.1 fusion.15
  40.4 0.1 subtract_add_fusion.4
  40.5 0.5 fusion.6
  41.0 1.0 copy.34.wy_ref
  42.0 0.1 subtract_add_fusion.3
  42.1 0.5 fusion.7
  42.7 0.1 pad_add_fusion
  42.8 0.1 subtract_add_fusion.2
  42.9 0.8 fusion.14
  43.7 0.3 copy.33
  44.0 0.9 copy.36.wx_ref
  44.9 0.8 fusion.12
  45.7 0.1 copy.37
  45.8 0.1 compare_select_fusion
  46.0 1.4 fusion.1
  47.4 0.2 copy.47.bz_ref
  47.6 1.4 fusion
  49.0 0.2 copy.48.wz_ref
  49.3 8.1 %forward.1.blur_ref = f32[6,8,256,256]{3,2,1,0:T(8,128)S(1)} custom-call(f32[32,128,128]{2,1,0:T(8,128)S(1)} %copy-done, bf16[32,16,128]{2,1,0:T(8,128)(2,1)S(1)} %copy-done.9, bf16[32,16,128]{2,1,0:T(8,128)(2,1)S(1)} %copy-done.12, bf16[4,160,128]{2,1,0:T(8,128)(2,1)S(1)} %copy-done.15, bf16[4,160,128]{2,1,0:T(8,128)(2,1)S(1)} %copy-done.17, ...), custom_call_target="tpu_custom_call" | custom-call | tf_op jit(solution)/shard_map/forward/pallas_call | solution.py:362
  57.4 4.5 %copy-done.1 = f32[6,8,256,256]{3,2,1,0:T(8,128)} copy-done((f32[6,8,256,256]{3,2,1,0:T(8,128)}, f32[6,8,256,256]{3,2,1,0:T(8,128)S(1)}, u32[]{:S(2)}) %copy-start.1) | copy-done | bytes 12582936
  61.9 0.9 copy-done.2
  62.8 80.8 %all-to-all-done.got_ref = bf16[128,264,128]{2,1,0:T(8,128)(2,1)} async-done(((bf16[128,264,128]{2,1,0:T(8,128)(2,1)}), bf16[128,264,128]{2,1,0:T(8,128)(2,1)}, u32[]{:S(2)}, u32[]{:S(2)}) %all-to-all-start) | async-done | bytes 8650784 | tf_op jit(solution)/shard_map/all_to_all | solution.py:634
  143.6 22.1 %backward.1 = (f32[32,128,128]{2,1,0:T(8,128)S(1)}, f32[32,16,128]{2,1,0:T(8,128)S(1)}, f32[32,16,128]{2,1,0:T(8,128)S(1)}, s16[4,160,128]{2,1,0:T(8,128)(2,1)S(...) custom-call(bf16[128,264,128]{2,1,0:T(8,128)(2,1)} %all-to-all-done.got_ref, ...), custom_call_target="tpu_custom_call" | custom-call | tf_op jit(solution)/shard_map/backward/pallas_call | solution.py:376
  165.7 13.8 %collective-permute-start.4 = (s16[4,160,128]{2,1,0:T(8,128)(2,1)S(1)}, s16[4,160,128]{2,1,0:T(8,128)(2,1)S(1)}, u32[]{:S(2)}, u32[]{:S(2)}) collective-permute-start(s16[4,160,128]{2,1,0:T(8,128)(2,1)S(1)} %get-tuple-element.49), channel_id=1, source_target_pairs={{0,1},{1,2},{2,3},{3,4},{4,5},{5,6},{6,7},{7,8},{8,9},{9,10},{10,1... | collective-permute-start | bytes 491528 | tf_op jit(solution)/shard_map/ppermute | solution.py:29
  179.6 1.9 collective-permute-start.5
  181.5 0.3 collective-permute-done.4.left_ref
  181.8 5.3 %collective-permute-done.5.right_ref = s16[4,160,128]{2,1,0:T(8,128)(2,1)S(1)} collective-permute-done((s16[4,160,128]{2,1,0:T(8,128)(2,1)S(1)}, s16[4,160,128]{2,1,0:T(8,128)(2,1)S(1)}, u32[]{:S(2)}, u32[]{:S(2)}) %collective-permute-start.5) | collective-permute-done | bytes 163872 | tf_op jit(solution)/shard_map/ppermute | solution.py:29
  187.1 0.7 join_x.2
  187.8 1.9 collective-permute-start.6
  189.8 5.1 %collective-permute-start.7 = (s16[64,16,128]{2,1,0:T(8,128)(2,1)S(1)}, s16[64,16,128]{2,1,0:T(8,128)(2,1)S(1)}, u32[]{:S(2)}, u32[]{:S(2)}) collective-permute-start(s16[64,16,128]{2,1,0:T(8,128)(2,1)S(1)} %get-tuple-element.54), channel_id=1, source_target_pairs={{16,0},{32,16},{48,32},{64,48},{80,64},{96,80},{112,96},{17,1},{33... | collective-permute-start | bytes 786440 | tf_op jit(solution)/shard_map/ppermute | solution.py:29
  194.8 1.6 collective-permute-done.6.above_ref
  196.4 2.8 %collective-permute-done.7.below_ref = s16[64,16,128]{2,1,0:T(8,128)(2,1)S(1)} collective-permute-done((s16[64,16,128]{2,1,0:T(8,128)(2,1)S(1)}, s16[64,16,128]{2,1,0:T(8,128)(2,1)S(1)}, u32[]{:S(2)}, u32[]{:S(2)}) %collective-permute-start.7) | collective-permute-done | bytes 262176 | tf_op jit(solution)/shard_map/ppermute | solution.py:29
  199.3 1.7 next_join.1
  201.0 4.2 %collective-permute-start.8 = (bf16[4,160,128]{2,1,0:T(8,128)(2,1)S(1)}, bf16[4,160,128]{2,1,0:T(8,128)(2,1)S(1)}, u32[]{:S(2)}, u32[]{:S(2)}) collective-permute-start(bf16[4,160,128]{2,1,0:T(8,128)(2,1)S(1)} %get-tuple-element.60), channel_id=1, source_target_pairs={{0,1},{1,2},{2,3},{3,4},{4,5},{5,6},{6,7},{7,8},{8,9},{9,10},{10,1... | collective-permute-start | bytes 491528 | tf_op jit(solution)/shard_map/ppermute | solution.py:29
  205.3 1.9 collective-permute-start.9
  207.2 1.8 collective-permute-done.8.left_ref
  208.9 3.8 %collective-permute-done.9.right_ref = bf16[4,160,128]{2,1,0:T(8,128)(2,1)S(1)} collective-permute-done((bf16[4,160,128]{2,1,0:T(8,128)(2,1)S(1)}, bf16[4,160,128]{2,1,0:T(8,128)(2,1)S(1)}, u32[]{:S(2)}, u32[]{:S(2)}) %collective-permute-start.9) | collective-permute-done | bytes 163872 | tf_op jit(solution)/shard_map/ppermute | solution.py:29
  212.8 16.1 %iterate.1 = (f32[32,128,128]{2,1,0:T(8,128)S(1)}, f32[32,16,128]{2,1,0:T(8,128)S(1)}, f32[32,16,128]{2,1,0:T(8,128)S(1)}, s16[4,160,128]{2,1,0:T(8,128)(2,1)S(1)}, s16[4,160,128]{2,1,0:T(8,128)(2,1)S(1)}) custom-call(f32[32,128,128]{2,1,0:T(8,128)S(1)} %get-tuple-element.57.est_ref, bf16[32,16,128]{2,1,0:T(8,128)(2,1)S(1)} %get-tuple-element.58.top_ref, ...), custom_call_target="tpu_custom_call" | custom-call | tf_op jit(solution)/shard_map/iterate/pallas_call | solution.py:405
  228.9 1.9 collective-permute-start.10
  230.8 2.4 collective-permute-start.11
  233.3 5.1 %collective-permute-done.11.right_ref = s16[4,160,128]{2,1,0:T(8,128)(2,1)S(1)} collective-permute-done((s16[4,160,128]{2,1,0:T(8,128)(2,1)S(1)}, s16[4,160,128]{2,1,0:T(8,128)(2,1)S(1)}, u32[]{:S(2)}, u32[]{:S(2)}) %collective-permute-start.11) | collective-permute-done | bytes 163872 | tf_op jit(solution)/shard_map/ppermute | solution.py:29
  238.4 0.4 join_x.3
  238.7 3.6 %collective-permute-start.12 = (s16[32,16,128]{2,1,0:T(8,128)(2,1)S(1)}, s16[32,16,128]{2,1,0:T(8,128)(2,1)S(1)}, u32[]{:S(2)}, u32[]{:S(2)}) collective-permute-start(s16[32,16,128]{2,1,0:T(8,128)(2,1)S(1)} %get-tuple-element.69), channel_id=1, source_target_pairs={{0,16},{16,32},{32,48},{48,64},{64,80},{80,96},{96,112},{1,17},{17... | collective-permute-start | bytes 393224 | tf_op jit(solution)/shard_map/ppermute | solution.py:29
  242.4 3.2 %collective-permute-start.13 = (s16[32,16,128]{2,1,0:T(8,128)(2,1)S(1)}, s16[32,16,128]{2,1,0:T(8,128)(2,1)S(1)}, u32[]{:S(2)}, u32[]{:S(2)}) collective-permute-start(s16[32,16,128]{2,1,0:T(8,128)(2,1)S(1)} %get-tuple-element.70), channel_id=1, source_target_pairs={{16,0},{32,16},{48,32},{64,48},{80,64},{96,80},{112,96},{17,1},{33... | collective-permute-start | bytes 393224 | tf_op jit(solution)/shard_map/ppermute | solution.py:29
  245.5 0.4 collective-permute-done.12.above_ref
  246.0 4.5 %collective-permute-done.13.below_ref = s16[32,16,128]{2,1,0:T(8,128)(2,1)S(1)} collective-permute-done((s16[32,16,128]{2,1,0:T(8,128)(2,1)S(1)}, s16[32,16,128]{2,1,0:T(8,128)(2,1)S(1)}, u32[]{:S(2)}, u32[]{:S(2)}) %collective-permute-start.13) | collective-permute-done | bytes 131104 | tf_op jit(solution)/shard_map/ppermute | solution.py:29
  250.5 2.4 last_join.1
  (50 shorter events, 0.2 us)
Async XLA Ops:
  0.0 14.6 %copy-start = (f32[32,128,128]{2,1,0:T(8,128)S(1)}, f32[32,128,128]{2,1,0:T(8,128)}, u32[]{:S(2)}) copy-start(f32[32,128,128]{2,1,0:T(8,128)} %est_ref.5) | copy-start | bytes 6291460
  0.0 8.7 %copy-start.20 = (s32[128]{0:T(128)S(1)}, s32[128]{0:T(128)}, u32[]{:S(2)}) copy-start(s32[128]{0:T(128)} %param.7) | copy-start | bytes 1540
  0.0 8.7 %copy-start.19 = (s32[128,1]{0,1:T(1,128)S(1)}, s32[128,1]{0,1:T(1,128)}, u32[]{:S(2)}) copy-start(s32[128,1]{0,1:T(1,128)} %param.6) | copy-start | bytes 1540
  1.9 8.0 %collective-permute-start = (bf16[32,16,128]{2,1,0:T(8,128)(2,1)}, bf16[32,16,128]{2,1,0:T(8,128)(2,1)S(1)}, u32[]{:S(2)}, u32[]{:S(2)}) collective-permute-start(bf16[32,16,128]{2,1,0:T(8,128)(2,1)} %get-tuple-element.38), channel_id=1, source_target_pairs={{0,16},{16,32},{32,48},{48,64},{64,80},{80,96},{96,112},{1,17},{17... | collective-permute-start | bytes 393224 | tf_op jit(solution)/shard_map/ppermute | solution.py:29
  6.3 8.3 %collective-permute-start.1 = (bf16[32,16,128]{2,1,0:T(8,128)(2,1)}, bf16[32,16,128]{2,1,0:T(8,128)(2,1)S(1)}, u32[]{:S(2)}, u32[]{:S(2)}) collective-permute-start(bf16[32,16,128]{2,1,0:T(8,128)(2,1)} %get-tuple-element.39), channel_id=1, source_target_pairs={{16,0},{32,16},{48,32},{64,48},{80,64},{96,80},{112,96},{17,1},{33... | collective-permute-start | bytes 393224 | tf_op jit(solution)/shard_map/ppermute | solution.py:29
  14.6 0.8 copy-start.11
  15.4 0.7 copy-start.8
  16.1 11.6 %collective-permute-start.2 = (bf16[4,160,128]{2,1,0:T(8,128)(2,1)S(1)}, bf16[4,160,128]{2,1,0:T(8,128)(2,1)S(1)}, u32[]{:S(2)}, u32[]{:S(2)}) collective-permute-start(bf16[4,160,128]{2,1,0:T(8,128)(2,1)S(1)} %get-tuple-element.43), channel_id=1, source_target_pairs={{0,1},{1,2},{2,3},{3,4},{4,5},{5,6},{6,7},{7,8},{8,9},{9,10},{10,1... | collective-permute-start | bytes 491528 | tf_op jit(solution)/shard_map/ppermute | solution.py:29
  20.6 7.7 %collective-permute-start.3 = (bf16[4,160,128]{2,1,0:T(8,128)(2,1)S(1)}, bf16[4,160,128]{2,1,0:T(8,128)(2,1)S(1)}, u32[]{:S(2)}, u32[]{:S(2)}) collective-permute-start(bf16[4,160,128]{2,1,0:T(8,128)(2,1)S(1)} %get-tuple-element.44), channel_id=1, source_target_pairs={{1,0},{2,1},{3,2},{4,3},{5,4},{6,5},{7,6},{8,7},{9,8},{10,9},{11,1... | collective-permute-start | bytes 491528 | tf_op jit(solution)/shard_map/ppermute | solution.py:29
  27.6 12.5 %copy-start.18 = (f32[6,3,31]{2,1,0:T(4,128)S(1)}, f32[6,3,31]{2,1,0:T(4,128)}, u32[]{:S(2)}) copy-start(f32[6,3,31]{2,1,0:T(4,128)} %param.8) | copy-start | bytes 6700
  27.7 0.7 copy-start.14
  28.3 0.7 copy-start.16
  29.0 114.6 %all-to-all-start = ((bf16[128,264,128]{2,1,0:T(8,128)(2,1)}), bf16[128,264,128]{2,1,0:T(8,128)(2,1)}, u32[]{:S(2)}, u32[]{:S(2)}) async-start(bf16[128,264,128]{2,1,0:T(8,128)(2,1)} %pack.1), calls=%async_computation | async-start | bytes 17301504 | tf_op jit(solution)/shard_map/all_to_all | solution.py:634
  45.9 3.3 %copy-start.4 = (bf16[256,768]{1,0:T(8,128)(2,1)S(1)}, bf16[256,768]{1,0:T(8,128)(2,1)}, u32[]{:S(2)}) copy-start(bf16[256,768]{1,0:T(8,128)(2,1)} %copy.36.wx_ref) | copy-start | bytes 1179652
  46.0 3.3 %copy-start.6 = (bf16[6,128,160]{2,1,0:T(8,128)(2,1)S(1)}, bf16[6,128,160]{2,1,0:T(8,128)(2,1)}, u32[]{:S(2)}) copy-start(bf16[6,128,160]{2,1,0:T(8,128)(2,1)} %copy.34.wy_ref) | copy-start | bytes 737284
  46.0 3.3 %copy-start.9 = (bf16[32,16,128]{2,1,0:T(8,128)(2,1)S(1)}, bf16[32,16,128]{2,1,0:T(8,128)(2,1)}, u32[]{:S(2)}) copy-start(bf16[32,16,128]{2,1,0:T(8,128)(2,1)} %copy-done.8) | copy-start | bytes 393220
  46.0 3.3 %copy-start.12 = (bf16[32,16,128]{2,1,0:T(8,128)(2,1)S(1)}, bf16[32,16,128]{2,1,0:T(8,128)(2,1)}, u32[]{:S(2)}) copy-start(bf16[32,16,128]{2,1,0:T(8,128)(2,1)} %copy-done.11) | copy-start | bytes 393220
  46.0 3.3 %copy-start.15 = (bf16[4,160,128]{2,1,0:T(8,128)(2,1)S(1)}, bf16[4,160,128]{2,1,0:T(8,128)(2,1)}, u32[]{:S(2)}) copy-start(bf16[4,160,128]{2,1,0:T(8,128)(2,1)} %copy-done.14) | copy-start | bytes 491524
  46.0 3.3 %copy-start.17 = (bf16[4,160,128]{2,1,0:T(8,128)(2,1)S(1)}, bf16[4,160,128]{2,1,0:T(8,128)(2,1)}, u32[]{:S(2)}) copy-start(bf16[4,160,128]{2,1,0:T(8,128)(2,1)} %copy-done.16) | copy-start | bytes 491524
  57.4 4.5 %copy-start.1 = (f32[6,8,256,256]{3,2,1,0:T(8,128)}, f32[6,8,256,256]{3,2,1,0:T(8,128)S(1)}, u32[]{:S(2)}) copy-start(f32[6,8,256,256]{3,2,1,0:T(8,128)S(1)} %forward.1.blur_ref) | copy-start | bytes 37748740
  61.9 0.9 copy-start.2
  165.7 33.6 %copy-start.10 = (bf16[32,16,128]{2,1,0:T(8,128)(2,1)S(1)}, bf16[32,16,128]{2,1,0:T(8,128)(2,1)}, u32[]{:S(2)}) copy-start(bf16[32,16,128]{2,1,0:T(8,128)(2,1)} %copy-done.8) | copy-start | bytes 393220
  165.7 33.5 %copy-start.13 = (bf16[32,16,128]{2,1,0:T(8,128)(2,1)S(1)}, bf16[32,16,128]{2,1,0:T(8,128)(2,1)}, u32[]{:S(2)}) copy-start(bf16[32,16,128]{2,1,0:T(8,128)(2,1)} %copy-done.11) | copy-start | bytes 393220
  165.7 16.1 %collective-permute-start.4 = (s16[4,160,128]{2,1,0:T(8,128)(2,1)S(1)}, s16[4,160,128]{2,1,0:T(8,128)(2,1)S(1)}, u32[]{:S(2)}, u32[]{:S(2)}) collective-permute-start(s16[4,160,128]{2,1,0:T(8,128)(2,1)S(1)} %get-tuple-element.49), channel_id=1, source_target_pairs={{0,1},{1,2},{2,3},{3,4},{4,5},{5,6},{6,7},{7,8},{8,9},{9,10},{10,1... | collective-permute-start | bytes 491528 | tf_op jit(solution)/shard_map/ppermute | solution.py:29
  179.6 7.5 %collective-permute-start.5 = (s16[4,160,128]{2,1,0:T(8,128)(2,1)S(1)}, s16[4,160,128]{2,1,0:T(8,128)(2,1)S(1)}, u32[]{:S(2)}, u32[]{:S(2)}) collective-permute-start(s16[4,160,128]{2,1,0:T(8,128)(2,1)S(1)} %get-tuple-element.50), channel_id=1, source_target_pairs={{1,0},{2,1},{3,2},{4,3},{5,4},{6,5},{7,6},{8,7},{9,8},{10,9},{11,1... | collective-permute-start | bytes 491528 | tf_op jit(solution)/shard_map/ppermute | solution.py:29
  187.1 25.7 %copy-start.3 = (bf16[6,256,256]{2,1,0:T(8,128)(2,1)S(1)}, bf16[6,256,256]{2,1,0:T(8,128)(2,1)}, u32[]{:S(2)}) copy-start(bf16[6,256,256]{2,1,0:T(8,128)(2,1)} %copy-done.2) | copy-start | bytes 2359300
  187.1 25.7 %copy-start.5 = (bf16[256,768]{1,0:T(8,128)(2,1)S(1)}, bf16[256,768]{1,0:T(8,128)(2,1)}, u32[]{:S(2)}) copy-start(bf16[256,768]{1,0:T(8,128)(2,1)} %copy.36.wx_ref) | copy-start | bytes 1179652
  187.1 25.7 %copy-start.7 = (bf16[6,128,160]{2,1,0:T(8,128)(2,1)S(1)}, bf16[6,128,160]{2,1,0:T(8,128)(2,1)}, u32[]{:S(2)}) copy-start(bf16[6,128,160]{2,1,0:T(8,128)(2,1)} %copy.34.wy_ref) | copy-start | bytes 737284
  187.8 8.6 %collective-permute-start.6 = (s16[64,16,128]{2,1,0:T(8,128)(2,1)S(1)}, s16[64,16,128]{2,1,0:T(8,128)(2,1)S(1)}, u32[]{:S(2)}, u32[]{:S(2)}) collective-permute-start(s16[64,16,128]{2,1,0:T(8,128)(2,1)S(1)} %get-tuple-element.53), channel_id=1, source_target_pairs={{0,16},{16,32},{32,48},{48,64},{64,80},{80,96},{96,112},{1,17},{17... | collective-permute-start | bytes 786440 | tf_op jit(solution)/shard_map/ppermute | solution.py:29
  189.8 9.5 %collective-permute-start.7 = (s16[64,16,128]{2,1,0:T(8,128)(2,1)S(1)}, s16[64,16,128]{2,1,0:T(8,128)(2,1)S(1)}, u32[]{:S(2)}, u32[]{:S(2)}) collective-permute-start(s16[64,16,128]{2,1,0:T(8,128)(2,1)S(1)} %get-tuple-element.54), channel_id=1, source_target_pairs={{16,0},{32,16},{48,32},{64,48},{80,64},{96,80},{112,96},{17,1},{33... | collective-permute-start | bytes 786440 | tf_op jit(solution)/shard_map/ppermute | solution.py:29
  201.0 7.9 %collective-permute-start.8 = (bf16[4,160,128]{2,1,0:T(8,128)(2,1)S(1)}, bf16[4,160,128]{2,1,0:T(8,128)(2,1)S(1)}, u32[]{:S(2)}, u32[]{:S(2)}) collective-permute-start(bf16[4,160,128]{2,1,0:T(8,128)(2,1)S(1)} %get-tuple-element.60), channel_id=1, source_target_pairs={{0,1},{1,2},{2,3},{3,4},{4,5},{5,6},{6,7},{7,8},{8,9},{9,10},{10,1... | collective-permute-start | bytes 491528 | tf_op jit(solution)/shard_map/ppermute | solution.py:29
  205.3 7.5 %collective-permute-start.9 = (bf16[4,160,128]{2,1,0:T(8,128)(2,1)S(1)}, bf16[4,160,128]{2,1,0:T(8,128)(2,1)S(1)}, u32[]{:S(2)}, u32[]{:S(2)}) collective-permute-start(bf16[4,160,128]{2,1,0:T(8,128)(2,1)S(1)} %get-tuple-element.61), channel_id=1, source_target_pairs={{1,0},{2,1},{3,2},{4,3},{5,4},{6,5},{7,6},{8,7},{9,8},{10,9},{11,1... | collective-permute-start | bytes 491528 | tf_op jit(solution)/shard_map/ppermute | solution.py:29
  228.9 4.3 %collective-permute-start.10 = (s16[4,160,128]{2,1,0:T(8,128)(2,1)S(1)}, s16[4,160,128]{2,1,0:T(8,128)(2,1)S(1)}, u32[]{:S(2)}, u32[]{:S(2)}) collective-permute-start(s16[4,160,128]{2,1,0:T(8,128)(2,1)S(1)} %get-tuple-element.65), channel_id=1, source_target_pairs={{0,1},{1,2},{2,3},{3,4},{4,5},{5,6},{6,7},{7,8},{8,9},{9,10},{10,1... | collective-permute-start | bytes 491528 | tf_op jit(solution)/shard_map/ppermute | solution.py:29
  230.8 7.5 %collective-permute-start.11 = (s16[4,160,128]{2,1,0:T(8,128)(2,1)S(1)}, s16[4,160,128]{2,1,0:T(8,128)(2,1)S(1)}, u32[]{:S(2)}, u32[]{:S(2)}) collective-permute-start(s16[4,160,128]{2,1,0:T(8,128)(2,1)S(1)} %get-tuple-element.66), channel_id=1, source_target_pairs={{1,0},{2,1},{3,2},{4,3},{5,4},{6,5},{7,6},{8,7},{9,8},{10,9},{11,1... | collective-permute-start | bytes 491528 | tf_op jit(solution)/shard_map/ppermute | solution.py:29
  238.7 7.2 %collective-permute-start.12 = (s16[32,16,128]{2,1,0:T(8,128)(2,1)S(1)}, s16[32,16,128]{2,1,0:T(8,128)(2,1)S(1)}, u32[]{:S(2)}, u32[]{:S(2)}) collective-permute-start(s16[32,16,128]{2,1,0:T(8,128)(2,1)S(1)} %get-tuple-element.69), channel_id=1, source_target_pairs={{0,16},{16,32},{32,48},{48,64},{64,80},{80,96},{96,112},{1,17},{17... | collective-permute-start | bytes 393224 | tf_op jit(solution)/shard_map/ppermute | solution.py:29
  242.4 8.1 %collective-permute-start.13 = (s16[32,16,128]{2,1,0:T(8,128)(2,1)S(1)}, s16[32,16,128]{2,1,0:T(8,128)(2,1)S(1)}, u32[]{:S(2)}, u32[]{:S(2)}) collective-permute-start(s16[32,16,128]{2,1,0:T(8,128)(2,1)S(1)} %get-tuple-element.70), channel_id=1, source_target_pairs={{16,0},{32,16},{48,32},{64,48},{80,64},{96,80},{112,96},{17,1},{33... | collective-permute-start | bytes 393224 | tf_op jit(solution)/shard_map/ppermute | solution.py:29

commit v3 on v2

--- a/solution.py
+++ b/solution.py
@@ -18,7 +18,7 @@
 ZPER = CZ // GROUPS
 SLOTS = 2
 HALF_TILE = 8
-UX, UY, UZ, UB, UE = 2, 16, 8, 16, 2
+UX, UY, UZ, UB, UE = 4, 16, 8, 16, 4
 def room(mebibytes):
     return pltpu.CompilerParams(vmem_limit_bytes=mebibytes << 20)
 
@@ -228,38 +228,36 @@
 
         head_ref[VIEWS * CZ] = 0
         times_ref[VIEWS * CZ] = 0
-        for w in range(VIEWS):
+        for w in range(VIEWS + 1):
             many_ref[w] = 0
 
         names.wait()
-        wide_ref[...] = names_ref[...].astype(jnp.float32)[:, 0, :].astype(jnp.int32)
+        wide_ref[...] = jnp.sum(names_ref[...].astype(jnp.float32), axis=0).astype(jnp.int32)
         labels = pltpu.make_async_copy(wide_ref, label_ref, sems.at[2])
         labels.start()
         labels.wait()
 
-        @pl.loop(0, sources, unroll=2)
+        @pl.loop(0, sources, unroll=8)
         def _(i):
             for r in range(SLOTS):
-                name = label_ref[i, r]
+                name = label_ref[r, i] - 1
                 label = jnp.where(name < 0, VIEWS * CZ, name)
                 times = times_ref[label]
                 next_ref[i * SLOTS + r] = head_ref[label]
                 head_ref[label] = i * SLOTS + r
                 times_ref[label] = times + 1
-
-                @pl.when((times == 1) & (name >= 0))
-                def _():
-                    view = label // CZ
-                    many = many_ref[view]
-                    plane_ref[view * CZ + many] = label
-                    many_ref[view] = many + 1
+                view = label // CZ
+                many = many_ref[view]
+                plane_ref[view * (CZ + 1) + many] = label
+                second = (times == 1) & (name >= 0)
+                many_ref[view] = many + second.astype(jnp.int32)
 
         tiles.wait()
 
     def tile(i):
         return tiles_ref[i // SLOTS, pl.ds(pl.multiple_of(i % SLOTS * SIDE, SIDE), SIDE)]
 
-    @pl.loop(0, CZ, unroll=4)
+    @pl.loop(0, CZ, unroll=16)
     def _(z):
         first = head_ref[v * CZ + z]
         times = times_ref[v * CZ + z]
@@ -270,7 +268,7 @@
 
     @pl.loop(0, many_ref[v])
     def _(i):
-        plane = plane_ref[v * CZ + i]
+        plane = plane_ref[v * (CZ + 1) + i]
 
         def add(_, carry):
             at, total = carry
@@ -387,13 +385,13 @@
         + [
             pltpu.VMEM((sources, SLOTS * SIDE, SIDE), jnp.bfloat16),
             pltpu.VMEM((sources, HALF_TILE, SIDE), jnp.bfloat16),
-            pltpu.VMEM((sources, SIDE), jnp.int32),
-            pltpu.SMEM((sources, SIDE), jnp.int32),
+            pltpu.VMEM((HALF_TILE, SIDE), jnp.int32),
+            pltpu.SMEM((HALF_TILE, SIDE), jnp.int32),
             pltpu.SMEM((VIEWS * CZ + 1,), jnp.int32),
             pltpu.SMEM((sources * SLOTS,), jnp.int32),
             pltpu.SMEM((VIEWS * CZ + 1,), jnp.int32),
-            pltpu.SMEM((VIEWS,), jnp.int32),
-            pltpu.SMEM((VIEWS * CZ,), jnp.int32),
+            pltpu.SMEM((VIEWS + 1,), jnp.int32),
+            pltpu.SMEM(((VIEWS + 1) * (CZ + 1),), jnp.int32),
             pltpu.SemaphoreType.DMA((3,)),
         ],
         compiler_params=room(38),
@@ -623,9 +621,13 @@
     hit = dest[None, :] == jnp.arange(devices)[:, None]
     first = jnp.min(jnp.where(hit, order, count * 256), axis=1)[:, None, None]
     last = jnp.max(jnp.where(hit, order, -1), axis=1)[:, None, None]
-    one = jnp.where(first < count * 256, first % 256, -1)
-    two = jnp.where(last > first, last % 256, -1)
-    labels = jnp.where(lanes((devices, HALF_TILE, SIDE)) == 0, one, two).astype(jnp.bfloat16)
+    one = jnp.where(first < count * 256, first % 256 + 1, 0)
+    two = jnp.where(last > first, last % 256 + 1, 0)
+    shape = (devices, HALF_TILE, SIDE)
+    row = lax.broadcasted_iota(jnp.int32, shape, 1)
+    mine = lanes(shape) == lax.axis_index(axes)
+    labels = jnp.where(row == 0, one, jnp.where(row == 1, two, 0))
+    labels = jnp.where(mine, labels, 0).astype(jnp.bfloat16)
     labels, top, bot = lax.optimization_barrier((labels, top, bot))
     low, high = edges(estimate, top, bot)
     left, right = shift(high, "gx", 1), shift(low, "gx", -1)

time: 253 us -> 250 us (0.988)
  no operation moved by 1% of the time
where the time goes in v3:
time: 250 us
  waiting for transfers between devices  111 us (44%)
  starting transfers between devices  64.4 us (26%)
  Pallas kernels  56.8 us (23%)
  local copies, waits for them, and re-layouts  9.52 us (4%)
  matrix products  5.46 us (2%)
    all_to_all x1, waiting for transfers between devices, local(): got = lax.all_to_all(packed, axes, split_axis=0, concat_axis=0, tiled=True)  81.1 us
    ppermute x14, starting transfers between devices, shift(): return lax.ppermute(values, axis, pairs)  53.3 us
    ppermute x14, waiting for transfers between devices, shift(): return lax.ppermute(values, axis, pairs)  30.3 us
    pallas_call x1, Pallas kernels, backward(): pl.pallas_call(backward_body, out_shape=PARTS + (jax.ShapeDtypeStruct((VI...  20.4 us
    pallas_call x1, Pallas kernels, iterate(): pl.pallas_call(step_body, out_shape=PARTS, grid=(VIEWS,), in_specs=[once(...  15.6 us
    all_to_all x1, starting transfers between devices, local(): got = lax.all_to_all(packed, axes, split_axis=0, concat_axis=0, tiled=True)  11.1 us
    pallas_call x1, Pallas kernels, forward(): pl.pallas_call(forward_body, out_shape=jax.ShapeDtypeStruct((VIEWS,) + BL...  7.87 us
    unnamed x42, local copies, waits for them, and re-layouts  6.78 us
  transfers between devices with their start and end apart: 15, of which 11 were waited for; matrix products, arithmetic and copies ran while one was open for 4% of the time, Pallas kernels for 5%

profile of v3, /device:TPU:15, one launch (start us, length us, event | category | flops | bytes accessed | tf_op | source)
XLA Modules:
  0.0 249.9 jit_solution(2498569046816144611)
XLA Ops:
  0.0 1.9 rims.1
  1.9 4.4 %collective-permute-start = (bf16[32,16,128]{2,1,0:T(8,128)(2,1)}, bf16[32,16,128]{2,1,0:T(8,128)(2,1)S(1)}, u32[]{:S(2)}, u32[]{:S(2)}) collective-permute-start(bf16[32,16,128]{2,1,0:T(8,128)(2,1)} %get-tuple-element.38), channel_id=1, source_target_pairs={{0,16},{16,32},{32,48},{48,64},{64,80},{80,96},{96,112},{1,17},{17... | collective-permute-start | bytes 393224 | tf_op jit(solution)/shard_map/ppermute | solution.py:29
  6.3 2.4 collective-permute-start.1
  8.8 0.1 select_reduce_fusion.1
  8.9 1.0 select_convert_fusion.labels_ref
  10.0 4.7 %collective-permute-done.1.bot_ref = bf16[32,16,128]{2,1,0:T(8,128)(2,1)S(1)} collective-permute-done((bf16[32,16,128]{2,1,0:T(8,128)(2,1)}, bf16[32,16,128]{2,1,0:T(8,128)(2,1)S(1)}, u32[]{:S(2)}, u32[]{:S(2)}) %collective-permute-start.1) | collective-permute-done | bytes 131104 | tf_op jit(solution)/shard_map/ppermute | solution.py:29
  14.6 0.7 edges.1
  15.4 4.6 %collective-permute-start.2 = (bf16[4,160,128]{2,1,0:T(8,128)(2,1)S(1)}, bf16[4,160,128]{2,1,0:T(8,128)(2,1)S(1)}, u32[]{:S(2)}, u32[]{:S(2)}) collective-permute-start(bf16[4,160,128]{2,1,0:T(8,128)(2,1)S(1)} %get-tuple-element.43), channel_id=1, source_target_pairs={{0,1},{1,2},{2,3},{3,4},{4,5},{5,6},{6,7},{7,8},{8,9},{9,10},{10,1... | collective-permute-start | bytes 491528 | tf_op jit(solution)/shard_map/ppermute | solution.py:29
  20.0 1.9 collective-permute-start.3
  21.9 5.1 %pack.1 = bf16[128,264,128]{2,1,0:T(8,128)(2,1)} custom-call(s32[128]{0:T(128)} %bitcast.23, bf16[128,128,128]{2,1,0:T(8,128)(2,1)} %tiles_ref.1, bf16[128,8,128]{2,1,0:T(8,128)(2,1)} %select_convert_fusion.labels_ref), custom_call_target="tpu_custom_call" | custom-call | tf_op jit(solution)/shard_map/pack/pallas_call | solution.py:64
  27.0 0.0 copy-start.18
  27.0 0.7 copy-done.14
  27.7 0.7 copy-done.16
  28.4 11.1 %all-to-all-start = ((bf16[128,264,128]{2,1,0:T(8,128)(2,1)}), bf16[128,264,128]{2,1,0:T(8,128)(2,1)}, u32[]{:S(2)}, u32[]{:S(2)}) async-start(bf16[128,264,128]{2,1,0:T(8,128)(2,1)} %pack.1), calls=%async_computation | async-start | bytes 17301504 | tf_op jit(solution)/shard_map/all_to_all | solution.py:636
  39.5 0.1 reduce_sum.9
  39.6 0.1 copy.31
  39.7 0.1 fusion.15
  39.7 0.1 subtract_add_fusion.4
  39.8 0.5 fusion.6
  40.4 1.0 copy.34.wy_ref
  41.3 0.1 subtract_add_fusion.3
  41.4 0.5 fusion.7
  42.0 0.1 pad_add_fusion
  42.1 0.1 subtract_add_fusion.2
  42.2 0.8 fusion.14
  43.0 0.3 copy.33
  43.3 0.9 copy.36.wx_ref
  44.2 0.8 fusion.12
  45.0 0.1 copy.37
  45.1 0.1 compare_select_fusion
  45.3 0.0 copy-start.15
  45.3 1.4 fusion.1
  46.7 0.2 copy.47.bz_ref
  46.9 1.4 fusion
  48.3 0.2 copy.48.wz_ref
  48.6 7.9 %forward.1.blur_ref = f32[6,8,256,256]{3,2,1,0:T(8,128)S(1)} custom-call(f32[32,128,128]{2,1,0:T(8,128)S(1)} %copy-done, bf16[32,16,128]{2,1,0:T(8,128)(2,1)S(1)} %copy-done.9, bf16[32,16,128]{2,1,0:T(8,128)(2,1)S(1)} %copy-done.12, bf16[4,160,128]{2,1,0:T(8,128)(2,1)S(1)} %copy-done.15, bf16[4,160,128]{2,1,0:T(8,128)(2,1)S(1)} %copy-done.17, ...), custom_call_target="tpu_custom_call" | custom-call | tf_op jit(solution)/shard_map/forward/pallas_call | solution.py:360
  56.5 4.5 %copy-done.1 = f32[6,8,256,256]{3,2,1,0:T(8,128)} copy-done((f32[6,8,256,256]{3,2,1,0:T(8,128)}, f32[6,8,256,256]{3,2,1,0:T(8,128)S(1)}, u32[]{:S(2)}) %copy-start.1) | copy-done | bytes 12582936
  61.0 0.9 copy-done.2
  61.8 81.1 %all-to-all-done.got_ref = bf16[128,264,128]{2,1,0:T(8,128)(2,1)} async-done(((bf16[128,264,128]{2,1,0:T(8,128)(2,1)}), bf16[128,264,128]{2,1,0:T(8,128)(2,1)}, u32[]{:S(2)}, u32[]{:S(2)}) %all-to-all-start) | async-done | bytes 8650784 | tf_op jit(solution)/shard_map/all_to_all | solution.py:636
  142.9 20.4 %backward.1 = (f32[32,128,128]{2,1,0:T(8,128)S(1)}, f32[32,16,128]{2,1,0:T(8,128)S(1)}, f32[32,16,128]{2,1,0:T(8,128)S(1)}, s16[4,160,128]{2,1,0:T(8,128)(2,1)S(...) custom-call(bf16[128,264,128]{2,1,0:T(8,128)(2,1)} %all-to-all-done.got_ref, ...), custom_call_target="tpu_custom_call" | custom-call | tf_op jit(solution)/shard_map/backward/pallas_call | solution.py:374
  163.3 14.1 %collective-permute-start.4 = (s16[4,160,128]{2,1,0:T(8,128)(2,1)S(1)}, s16[4,160,128]{2,1,0:T(8,128)(2,1)S(1)}, u32[]{:S(2)}, u32[]{:S(2)}) collective-permute-start(s16[4,160,128]{2,1,0:T(8,128)(2,1)S(1)} %get-tuple-element.49), channel_id=1, source_target_pairs={{0,1},{1,2},{2,3},{3,4},{4,5},{5,6},{6,7},{7,8},{8,9},{9,10},{10,1... | collective-permute-start | bytes 491528 | tf_op jit(solution)/shard_map/ppermute | solution.py:29
  177.4 1.9 collective-permute-start.5
  179.3 0.3 collective-permute-done.4.left_ref
  179.6 5.3 %collective-permute-done.5.right_ref = s16[4,160,128]{2,1,0:T(8,128)(2,1)S(1)} collective-permute-done((s16[4,160,128]{2,1,0:T(8,128)(2,1)S(1)}, s16[4,160,128]{2,1,0:T(8,128)(2,1)S(1)}, u32[]{:S(2)}, u32[]{:S(2)}) %collective-permute-start.5) | collective-permute-done | bytes 163872 | tf_op jit(solution)/shard_map/ppermute | solution.py:29
  184.9 0.7 join_x.2
  185.6 1.9 collective-permute-start.6
  187.6 4.9 %collective-permute-start.7 = (s16[64,16,128]{2,1,0:T(8,128)(2,1)S(1)}, s16[64,16,128]{2,1,0:T(8,128)(2,1)S(1)}, u32[]{:S(2)}, u32[]{:S(2)}) collective-permute-start(s16[64,16,128]{2,1,0:T(8,128)(2,1)S(1)} %get-tuple-element.54), channel_id=1, source_target_pairs={{16,0},{32,16},{48,32},{64,48},{80,64},{96,80},{112,96},{17,1},{33... | collective-permute-start | bytes 786440 | tf_op jit(solution)/shard_map/ppermute | solution.py:29
  192.5 1.8 collective-permute-done.6.above_ref
  194.3 2.8 %collective-permute-done.7.below_ref = s16[64,16,128]{2,1,0:T(8,128)(2,1)S(1)} collective-permute-done((s16[64,16,128]{2,1,0:T(8,128)(2,1)S(1)}, s16[64,16,128]{2,1,0:T(8,128)(2,1)S(1)}, u32[]{:S(2)}, u32[]{:S(2)}) %collective-permute-start.7) | collective-permute-done | bytes 262176 | tf_op jit(solution)/shard_map/ppermute | solution.py:29
  197.1 1.7 next_join.1
  198.8 4.2 %collective-permute-start.8 = (bf16[4,160,128]{2,1,0:T(8,128)(2,1)S(1)}, bf16[4,160,128]{2,1,0:T(8,128)(2,1)S(1)}, u32[]{:S(2)}, u32[]{:S(2)}) collective-permute-start(bf16[4,160,128]{2,1,0:T(8,128)(2,1)S(1)} %get-tuple-element.60), channel_id=1, source_target_pairs={{0,1},{1,2},{2,3},{3,4},{4,5},{5,6},{6,7},{7,8},{8,9},{9,10},{10,1... | collective-permute-start | bytes 491528 | tf_op jit(solution)/shard_map/ppermute | solution.py:29
  203.0 1.9 collective-permute-start.9
  204.9 1.8 collective-permute-done.8.left_ref
  206.7 3.8 %collective-permute-done.9.right_ref = bf16[4,160,128]{2,1,0:T(8,128)(2,1)S(1)} collective-permute-done((bf16[4,160,128]{2,1,0:T(8,128)(2,1)S(1)}, bf16[4,160,128]{2,1,0:T(8,128)(2,1)S(1)}, u32[]{:S(2)}, u32[]{:S(2)}) %collective-permute-start.9) | collective-permute-done | bytes 163872 | tf_op jit(solution)/shard_map/ppermute | solution.py:29
  210.6 15.6 %iterate.1 = (f32[32,128,128]{2,1,0:T(8,128)S(1)}, f32[32,16,128]{2,1,0:T(8,128)S(1)}, f32[32,16,128]{2,1,0:T(8,128)S(1)}, s16[4,160,128]{2,1,0:T(8,128)(2,1)S(1)}, s16[4,160,128]{2,1,0:T(8,128)(2,1)S(1)}) custom-call(f32[32,128,128]{2,1,0:T(8,128)S(1)} %get-tuple-element.57.est_ref, bf16[32,16,128]{2,1,0:T(8,128)(2,1)S(1)} %get-tuple-element.58.top_ref, ...), custom_call_target="tpu_custom_call" | custom-call | tf_op jit(solution)/shard_map/iterate/pallas_call | solution.py:403
  226.1 1.9 collective-permute-start.10
  228.1 2.4 collective-permute-start.11
  230.5 5.1 %collective-permute-done.11.right_ref = s16[4,160,128]{2,1,0:T(8,128)(2,1)S(1)} collective-permute-done((s16[4,160,128]{2,1,0:T(8,128)(2,1)S(1)}, s16[4,160,128]{2,1,0:T(8,128)(2,1)S(1)}, u32[]{:S(2)}, u32[]{:S(2)}) %collective-permute-start.11) | collective-permute-done | bytes 163872 | tf_op jit(solution)/shard_map/ppermute | solution.py:29
  235.6 0.4 join_x.3
  236.0 3.3 %collective-permute-start.12 = (s16[32,16,128]{2,1,0:T(8,128)(2,1)S(1)}, s16[32,16,128]{2,1,0:T(8,128)(2,1)S(1)}, u32[]{:S(2)}, u32[]{:S(2)}) collective-permute-start(s16[32,16,128]{2,1,0:T(8,128)(2,1)S(1)} %get-tuple-element.69), channel_id=1, source_target_pairs={{0,16},{16,32},{32,48},{48,64},{64,80},{80,96},{96,112},{1,17},{17... | collective-permute-start | bytes 393224 | tf_op jit(solution)/shard_map/ppermute | solution.py:29
  239.3 3.4 %collective-permute-start.13 = (s16[32,16,128]{2,1,0:T(8,128)(2,1)S(1)}, s16[32,16,128]{2,1,0:T(8,128)(2,1)S(1)}, u32[]{:S(2)}, u32[]{:S(2)}) collective-permute-start(s16[32,16,128]{2,1,0:T(8,128)(2,1)S(1)} %get-tuple-element.70), channel_id=1, source_target_pairs={{16,0},{32,16},{48,32},{64,48},{80,64},{96,80},{112,96},{17,1},{33... | collective-permute-start | bytes 393224 | tf_op jit(solution)/shard_map/ppermute | solution.py:29
  242.8 0.4 collective-permute-done.12.above_ref
  243.2 4.3 %collective-permute-done.13.below_ref = s16[32,16,128]{2,1,0:T(8,128)(2,1)S(1)} collective-permute-done((s16[32,16,128]{2,1,0:T(8,128)(2,1)S(1)}, s16[32,16,128]{2,1,0:T(8,128)(2,1)S(1)}, u32[]{:S(2)}, u32[]{:S(2)}) %collective-permute-start.13) | collective-permute-done | bytes 131104 | tf_op jit(solution)/shard_map/ppermute | solution.py:29
  247.4 2.4 last_join.1
  (51 shorter events, 0.2 us)
Async XLA Ops:
  0.0 14.6 %copy-start = (f32[32,128,128]{2,1,0:T(8,128)S(1)}, f32[32,128,128]{2,1,0:T(8,128)}, u32[]{:S(2)}) copy-start(f32[32,128,128]{2,1,0:T(8,128)} %est_ref.5) | copy-start | bytes 6291460
  0.0 8.7 %copy-start.20 = (s32[128]{0:T(128)S(1)}, s32[128]{0:T(128)}, u32[]{:S(2)}) copy-start(s32[128]{0:T(128)} %param.7) | copy-start | bytes 1540
  0.0 8.8 %copy-start.19 = (s32[128,1]{0,1:T(1,128)S(1)}, s32[128,1]{0,1:T(1,128)}, u32[]{:S(2)}) copy-start(s32[128,1]{0,1:T(1,128)} %param.6) | copy-start | bytes 1540
  1.9 8.0 %collective-permute-start = (bf16[32,16,128]{2,1,0:T(8,128)(2,1)}, bf16[32,16,128]{2,1,0:T(8,128)(2,1)S(1)}, u32[]{:S(2)}, u32[]{:S(2)}) collective-permute-start(bf16[32,16,128]{2,1,0:T(8,128)(2,1)} %get-tuple-element.38), channel_id=1, source_target_pairs={{0,16},{16,32},{32,48},{48,64},{64,80},{80,96},{96,112},{1,17},{17... | collective-permute-start | bytes 393224 | tf_op jit(solution)/shard_map/ppermute | solution.py:29
  6.3 8.3 %collective-permute-start.1 = (bf16[32,16,128]{2,1,0:T(8,128)(2,1)}, bf16[32,16,128]{2,1,0:T(8,128)(2,1)S(1)}, u32[]{:S(2)}, u32[]{:S(2)}) collective-permute-start(bf16[32,16,128]{2,1,0:T(8,128)(2,1)} %get-tuple-element.39), channel_id=1, source_target_pairs={{16,0},{32,16},{48,32},{64,48},{80,64},{96,80},{112,96},{17,1},{33... | collective-permute-start | bytes 393224 | tf_op jit(solution)/shard_map/ppermute | solution.py:29
  10.0 17.0 %copy-start.8 = (bf16[32,16,128]{2,1,0:T(8,128)(2,1)}, bf16[32,16,128]{2,1,0:T(8,128)(2,1)S(1)}, u32[]{:S(2)}) copy-start(bf16[32,16,128]{2,1,0:T(8,128)(2,1)S(1)} %collective-permute-done.top_ref) | copy-start | bytes 393220
  14.6 12.4 %copy-start.11 = (bf16[32,16,128]{2,1,0:T(8,128)(2,1)}, bf16[32,16,128]{2,1,0:T(8,128)(2,1)S(1)}, u32[]{:S(2)}) copy-start(bf16[32,16,128]{2,1,0:T(8,128)(2,1)S(1)} %collective-permute-done.1.bot_ref) | copy-start | bytes 393220
  15.4 11.6 %collective-permute-start.2 = (bf16[4,160,128]{2,1,0:T(8,128)(2,1)S(1)}, bf16[4,160,128]{2,1,0:T(8,128)(2,1)S(1)}, u32[]{:S(2)}, u32[]{:S(2)}) collective-permute-start(bf16[4,160,128]{2,1,0:T(8,128)(2,1)S(1)} %get-tuple-element.43), channel_id=1, source_target_pairs={{0,1},{1,2},{2,3},{3,4},{4,5},{5,6},{6,7},{7,8},{8,9},{9,10},{10,1... | collective-permute-start | bytes 491528 | tf_op jit(solution)/shard_map/ppermute | solution.py:29
  20.0 7.7 %collective-permute-start.3 = (bf16[4,160,128]{2,1,0:T(8,128)(2,1)S(1)}, bf16[4,160,128]{2,1,0:T(8,128)(2,1)S(1)}, u32[]{:S(2)}, u32[]{:S(2)}) collective-permute-start(bf16[4,160,128]{2,1,0:T(8,128)(2,1)S(1)} %get-tuple-element.44), channel_id=1, source_target_pairs={{1,0},{2,1},{3,2},{4,3},{5,4},{6,5},{7,6},{8,7},{9,8},{10,9},{11,1... | collective-permute-start | bytes 491528 | tf_op jit(solution)/shard_map/ppermute | solution.py:29
  27.0 12.5 %copy-start.18 = (f32[6,3,31]{2,1,0:T(4,128)S(1)}, f32[6,3,31]{2,1,0:T(4,128)}, u32[]{:S(2)}) copy-start(f32[6,3,31]{2,1,0:T(4,128)} %param.8) | copy-start | bytes 6700
  27.0 0.7 copy-start.14
  27.7 0.7 copy-start.16
  28.4 114.5 %all-to-all-start = ((bf16[128,264,128]{2,1,0:T(8,128)(2,1)}), bf16[128,264,128]{2,1,0:T(8,128)(2,1)}, u32[]{:S(2)}, u32[]{:S(2)}) async-start(bf16[128,264,128]{2,1,0:T(8,128)(2,1)} %pack.1), calls=%async_computation | async-start | bytes 17301504 | tf_op jit(solution)/shard_map/all_to_all | solution.py:636
  45.3 3.3 %copy-start.4 = (bf16[256,768]{1,0:T(8,128)(2,1)S(1)}, bf16[256,768]{1,0:T(8,128)(2,1)}, u32[]{:S(2)}) copy-start(bf16[256,768]{1,0:T(8,128)(2,1)} %copy.36.wx_ref) | copy-start | bytes 1179652
  45.3 3.3 %copy-start.6 = (bf16[6,128,160]{2,1,0:T(8,128)(2,1)S(1)}, bf16[6,128,160]{2,1,0:T(8,128)(2,1)}, u32[]{:S(2)}) copy-start(bf16[6,128,160]{2,1,0:T(8,128)(2,1)} %copy.34.wy_ref) | copy-start | bytes 737284
  45.3 3.3 %copy-start.9 = (bf16[32,16,128]{2,1,0:T(8,128)(2,1)S(1)}, bf16[32,16,128]{2,1,0:T(8,128)(2,1)}, u32[]{:S(2)}) copy-start(bf16[32,16,128]{2,1,0:T(8,128)(2,1)} %copy-done.8) | copy-start | bytes 393220
  45.3 3.3 %copy-start.12 = (bf16[32,16,128]{2,1,0:T(8,128)(2,1)S(1)}, bf16[32,16,128]{2,1,0:T(8,128)(2,1)}, u32[]{:S(2)}) copy-start(bf16[32,16,128]{2,1,0:T(8,128)(2,1)} %copy-done.11) | copy-start | bytes 393220
  45.3 3.3 %copy-start.15 = (bf16[4,160,128]{2,1,0:T(8,128)(2,1)S(1)}, bf16[4,160,128]{2,1,0:T(8,128)(2,1)}, u32[]{:S(2)}) copy-start(bf16[4,160,128]{2,1,0:T(8,128)(2,1)} %copy-done.14) | copy-start | bytes 491524
  45.3 3.3 %copy-start.17 = (bf16[4,160,128]{2,1,0:T(8,128)(2,1)S(1)}, bf16[4,160,128]{2,1,0:T(8,128)(2,1)}, u32[]{:S(2)}) copy-start(bf16[4,160,128]{2,1,0:T(8,128)(2,1)} %copy-done.16) | copy-start | bytes 491524
  56.4 4.5 %copy-start.1 = (f32[6,8,256,256]{3,2,1,0:T(8,128)}, f32[6,8,256,256]{3,2,1,0:T(8,128)S(1)}, u32[]{:S(2)}) copy-start(f32[6,8,256,256]{3,2,1,0:T(8,128)S(1)} %forward.1.blur_ref) | copy-start | bytes 37748740
  61.0 0.9 copy-start.2
  163.3 33.8 %copy-start.10 = (bf16[32,16,128]{2,1,0:T(8,128)(2,1)S(1)}, bf16[32,16,128]{2,1,0:T(8,128)(2,1)}, u32[]{:S(2)}) copy-start(bf16[32,16,128]{2,1,0:T(8,128)(2,1)} %copy-done.8) | copy-start | bytes 393220
  163.3 33.8 %copy-start.13 = (bf16[32,16,128]{2,1,0:T(8,128)(2,1)S(1)}, bf16[32,16,128]{2,1,0:T(8,128)(2,1)}, u32[]{:S(2)}) copy-start(bf16[32,16,128]{2,1,0:T(8,128)(2,1)} %copy-done.11) | copy-start | bytes 393220
  163.3 16.3 %collective-permute-start.4 = (s16[4,160,128]{2,1,0:T(8,128)(2,1)S(1)}, s16[4,160,128]{2,1,0:T(8,128)(2,1)S(1)}, u32[]{:S(2)}, u32[]{:S(2)}) collective-permute-start(s16[4,160,128]{2,1,0:T(8,128)(2,1)S(1)} %get-tuple-element.49), channel_id=1, source_target_pairs={{0,1},{1,2},{2,3},{3,4},{4,5},{5,6},{6,7},{7,8},{8,9},{9,10},{10,1... | collective-permute-start | bytes 491528 | tf_op jit(solution)/shard_map/ppermute | solution.py:29
  177.4 7.5 %collective-permute-start.5 = (s16[4,160,128]{2,1,0:T(8,128)(2,1)S(1)}, s16[4,160,128]{2,1,0:T(8,128)(2,1)S(1)}, u32[]{:S(2)}, u32[]{:S(2)}) collective-permute-start(s16[4,160,128]{2,1,0:T(8,128)(2,1)S(1)} %get-tuple-element.50), channel_id=1, source_target_pairs={{1,0},{2,1},{3,2},{4,3},{5,4},{6,5},{7,6},{8,7},{9,8},{10,9},{11,1... | collective-permute-start | bytes 491528 | tf_op jit(solution)/shard_map/ppermute | solution.py:29
  184.9 25.6 %copy-start.3 = (bf16[6,256,256]{2,1,0:T(8,128)(2,1)S(1)}, bf16[6,256,256]{2,1,0:T(8,128)(2,1)}, u32[]{:S(2)}) copy-start(bf16[6,256,256]{2,1,0:T(8,128)(2,1)} %copy-done.2) | copy-start | bytes 2359300
  184.9 25.6 %copy-start.5 = (bf16[256,768]{1,0:T(8,128)(2,1)S(1)}, bf16[256,768]{1,0:T(8,128)(2,1)}, u32[]{:S(2)}) copy-start(bf16[256,768]{1,0:T(8,128)(2,1)} %copy.36.wx_ref) | copy-start | bytes 1179652
  184.9 25.6 %copy-start.7 = (bf16[6,128,160]{2,1,0:T(8,128)(2,1)S(1)}, bf16[6,128,160]{2,1,0:T(8,128)(2,1)}, u32[]{:S(2)}) copy-start(bf16[6,128,160]{2,1,0:T(8,128)(2,1)} %copy.34.wy_ref) | copy-start | bytes 737284
  185.6 8.6 %collective-permute-start.6 = (s16[64,16,128]{2,1,0:T(8,128)(2,1)S(1)}, s16[64,16,128]{2,1,0:T(8,128)(2,1)S(1)}, u32[]{:S(2)}, u32[]{:S(2)}) collective-permute-start(s16[64,16,128]{2,1,0:T(8,128)(2,1)S(1)} %get-tuple-element.53), channel_id=1, source_target_pairs={{0,16},{16,32},{32,48},{48,64},{64,80},{80,96},{96,112},{1,17},{17... | collective-permute-start | bytes 786440 | tf_op jit(solution)/shard_map/ppermute | solution.py:29
  187.6 9.5 %collective-permute-start.7 = (s16[64,16,128]{2,1,0:T(8,128)(2,1)S(1)}, s16[64,16,128]{2,1,0:T(8,128)(2,1)S(1)}, u32[]{:S(2)}, u32[]{:S(2)}) collective-permute-start(s16[64,16,128]{2,1,0:T(8,128)(2,1)S(1)} %get-tuple-element.54), channel_id=1, source_target_pairs={{16,0},{32,16},{48,32},{64,48},{80,64},{96,80},{112,96},{17,1},{33... | collective-permute-start | bytes 786440 | tf_op jit(solution)/shard_map/ppermute | solution.py:29
  198.8 7.9 %collective-permute-start.8 = (bf16[4,160,128]{2,1,0:T(8,128)(2,1)S(1)}, bf16[4,160,128]{2,1,0:T(8,128)(2,1)S(1)}, u32[]{:S(2)}, u32[]{:S(2)}) collective-permute-start(bf16[4,160,128]{2,1,0:T(8,128)(2,1)S(1)} %get-tuple-element.60), channel_id=1, source_target_pairs={{0,1},{1,2},{2,3},{3,4},{4,5},{5,6},{6,7},{7,8},{8,9},{9,10},{10,1... | collective-permute-start | bytes 491528 | tf_op jit(solution)/shard_map/ppermute | solution.py:29
  203.0 7.5 %collective-permute-start.9 = (bf16[4,160,128]{2,1,0:T(8,128)(2,1)S(1)}, bf16[4,160,128]{2,1,0:T(8,128)(2,1)S(1)}, u32[]{:S(2)}, u32[]{:S(2)}) collective-permute-start(bf16[4,160,128]{2,1,0:T(8,128)(2,1)S(1)} %get-tuple-element.61), channel_id=1, source_target_pairs={{1,0},{2,1},{3,2},{4,3},{5,4},{6,5},{7,6},{8,7},{9,8},{10,9},{11,1... | collective-permute-start | bytes 491528 | tf_op jit(solution)/shard_map/ppermute | solution.py:29
  226.1 4.3 %collective-permute-start.10 = (s16[4,160,128]{2,1,0:T(8,128)(2,1)S(1)}, s16[4,160,128]{2,1,0:T(8,128)(2,1)S(1)}, u32[]{:S(2)}, u32[]{:S(2)}) collective-permute-start(s16[4,160,128]{2,1,0:T(8,128)(2,1)S(1)} %get-tuple-element.65), channel_id=1, source_target_pairs={{0,1},{1,2},{2,3},{3,4},{4,5},{5,6},{6,7},{7,8},{8,9},{9,10},{10,1... | collective-permute-start | bytes 491528 | tf_op jit(solution)/shard_map/ppermute | solution.py:29
  228.1 7.5 %collective-permute-start.11 = (s16[4,160,128]{2,1,0:T(8,128)(2,1)S(1)}, s16[4,160,128]{2,1,0:T(8,128)(2,1)S(1)}, u32[]{:S(2)}, u32[]{:S(2)}) collective-permute-start(s16[4,160,128]{2,1,0:T(8,128)(2,1)S(1)} %get-tuple-element.66), channel_id=1, source_target_pairs={{1,0},{2,1},{3,2},{4,3},{5,4},{6,5},{7,6},{8,7},{9,8},{10,9},{11,1... | collective-permute-start | bytes 491528 | tf_op jit(solution)/shard_map/ppermute | solution.py:29
  236.0 7.2 %collective-permute-start.12 = (s16[32,16,128]{2,1,0:T(8,128)(2,1)S(1)}, s16[32,16,128]{2,1,0:T(8,128)(2,1)S(1)}, u32[]{:S(2)}, u32[]{:S(2)}) collective-permute-start(s16[32,16,128]{2,1,0:T(8,128)(2,1)S(1)} %get-tuple-element.69), channel_id=1, source_target_pairs={{0,16},{16,32},{32,48},{48,64},{64,80},{80,96},{96,112},{1,17},{17... | collective-permute-start | bytes 393224 | tf_op jit(solution)/shard_map/ppermute | solution.py:29
  239.3 8.1 %collective-permute-start.13 = (s16[32,16,128]{2,1,0:T(8,128)(2,1)S(1)}, s16[32,16,128]{2,1,0:T(8,128)(2,1)S(1)}, u32[]{:S(2)}, u32[]{:S(2)}) collective-permute-start(s16[32,16,128]{2,1,0:T(8,128)(2,1)S(1)} %get-tuple-element.70), channel_id=1, source_target_pairs={{16,0},{32,16},{48,32},{64,48},{80,64},{96,80},{112,96},{17,1},{33... | collective-permute-start | bytes 393224 | tf_op jit(solution)/shard_map/ppermute | solution.py:29

commit v4 on v3

--- a/solution.py
+++ b/solution.py
@@ -33,26 +33,40 @@
     return lax.broadcasted_iota(jnp.int32, shape, len(shape) - 1)
 
 
-def pack_body(dest_ref, tiles_ref, labels_ref, out_ref, seen_ref, tile_sem, label_sem):
+def pack_body(
+    dest_ref, tiles_ref, labels_ref, out_ref, held_ref, seen_ref, load_sems, tile_sem, label_sem
+):
+    devices = out_ref.shape[0]
+    pieces = load_sems.shape[0]
     count = tiles_ref.shape[0]
-    devices = out_ref.shape[0]
+    piece = count // pieces
+    loads = []
+    for p in range(pieces):
+        part = pl.ds(p * piece, piece)
+        loads.append(
+            pltpu.make_async_copy(tiles_ref.at[part], held_ref.at[part], load_sems.at[p])
+        )
+        loads[-1].start()
     named = pltpu.make_async_copy(
         labels_ref, out_ref.at[:, pl.ds(SLOTS * SIDE, HALF_TILE)], label_sem
     )
     named.start()
 
-    @pl.loop(0, devices)
+    @pl.loop(0, devices, unroll=8)
     def _(i):
         seen_ref[i] = 0
 
-    @pl.loop(0, count)
-    def _(i):
-        target = dest_ref[i]
-        rank = seen_ref[target]
-        seen_ref[target] = rank + 1
-        pltpu.make_async_copy(
-            tiles_ref.at[i], out_ref.at[target, pl.ds(rank * SIDE, SIDE)], tile_sem
-        ).start()
+    for p in range(pieces):
+        loads[p].wait()
+
+        @pl.loop(p * piece, (p + 1) * piece, unroll=4)
+        def _(i):
+            target = dest_ref[i]
+            rank = seen_ref[target]
+            seen_ref[target] = rank + 1
+            pltpu.make_async_copy(
+                held_ref.at[i], out_ref.at[target, pl.ds(rank * SIDE, SIDE)], tile_sem
+            ).start()
 
     every = out_ref.at[pl.ds(0, count // SLOTS), pl.ds(0, SLOTS * SIDE)]
     pltpu.make_async_copy(every, every, tile_sem).wait()
@@ -66,12 +80,14 @@
         out_shape=jax.ShapeDtypeStruct((devices, SLOTS * SIDE + HALF_TILE, SIDE), tiles.dtype),
         in_specs=[
             pl.BlockSpec(memory_space=pltpu.SMEM),
-            pl.BlockSpec(memory_space=pltpu.VMEM),
+            pl.BlockSpec(memory_space=pl.ANY),
             pl.BlockSpec(memory_space=pltpu.VMEM),
         ],
         out_specs=pl.BlockSpec(memory_space=pltpu.HBM),
         scratch_shapes=[
+            pltpu.VMEM(tiles.shape, tiles.dtype),
             pltpu.SMEM((devices,), jnp.int32),
+            pltpu.SemaphoreType.DMA((4,)),
             pltpu.SemaphoreType.DMA(()),
             pltpu.SemaphoreType.DMA(()),
         ],

time: 250 us -> 250 us (level)
  transfers between devices with their start and end apart: 15 -> 15, of which waited for: 11 -> 12; matrix products, arithmetic and copies ran while one was open for 4% -> 4% of each run, Pallas kernels for 5% -> 5%
where the time goes in v4:
time: 250 us
  waiting for transfers between devices  112 us (45%)
  starting transfers between devices  64 us (26%)
  Pallas kernels  56 us (22%)
  local copies, waits for them, and re-layouts  9.52 us (4%)
  matrix products  5.46 us (2%)
    all_to_all x1, waiting for transfers between devices, local(): got = lax.all_to_all(packed, axes, split_axis=0, concat_axis=0, tiled=True)  81.1 us
    ppermute x14, starting transfers between devices, shift(): return lax.ppermute(values, axis, pairs)  53.4 us
    ppermute x14, waiting for transfers between devices, shift(): return lax.ppermute(values, axis, pairs)  31.1 us
    pallas_call x1, Pallas kernels, backward(): pl.pallas_call(backward_body, out_shape=PARTS + (jax.ShapeDtypeStruct((VI...  20.3 us
    pallas_call x1, Pallas kernels, iterate(): pl.pallas_call(step_body, out_shape=PARTS, grid=(VIEWS,), in_specs=[once(...  15.6 us
    all_to_all x1, starting transfers between devices, local(): got = lax.all_to_all(packed, axes, split_axis=0, concat_axis=0, tiled=True)  10.6 us
    pallas_call x1, Pallas kernels, forward(): pl.pallas_call(forward_body, out_shape=jax.ShapeDtypeStruct((VIEWS,) + BL...  7.87 us
    unnamed x42, local copies, waits for them, and re-layouts  6.78 us
  transfers between devices with their start and end apart: 15, of which 12 were waited for; matrix products, arithmetic and copies ran while one was open for 4% of the time, Pallas kernels for 5%

profile of v4, /device:TPU:15, one launch (start us, length us, event | category | flops | bytes accessed | tf_op | source)
XLA Modules:
  0.0 249.5 jit_solution(16666748234897312212)
XLA Ops:
  0.0 1.9 rims.1
  1.9 4.4 %collective-permute-start = (bf16[32,16,128]{2,1,0:T(8,128)(2,1)}, bf16[32,16,128]{2,1,0:T(8,128)(2,1)S(1)}, u32[]{:S(2)}, u32[]{:S(2)}) collective-permute-start(bf16[32,16,128]{2,1,0:T(8,128)(2,1)} %get-tuple-element.38), channel_id=1, source_target_pairs={{0,16},{16,32},{32,48},{48,64},{64,80},{80,96},{96,112},{1,17},{17... | collective-permute-start | bytes 393224 | tf_op jit(solution)/shard_map/ppermute | solution.py:29
  6.3 2.4 collective-permute-start.1
  8.8 0.1 select_reduce_fusion.1
  8.9 1.0 select_convert_fusion.labels_ref
  10.0 4.7 %collective-permute-done.1.bot_ref = bf16[32,16,128]{2,1,0:T(8,128)(2,1)S(1)} collective-permute-done((bf16[32,16,128]{2,1,0:T(8,128)(2,1)}, bf16[32,16,128]{2,1,0:T(8,128)(2,1)S(1)}, u32[]{:S(2)}, u32[]{:S(2)}) %collective-permute-start.1) | collective-permute-done | bytes 131104 | tf_op jit(solution)/shard_map/ppermute | solution.py:29
  14.6 0.7 edges.1
  15.4 4.6 %collective-permute-start.2 = (bf16[4,160,128]{2,1,0:T(8,128)(2,1)S(1)}, bf16[4,160,128]{2,1,0:T(8,128)(2,1)S(1)}, u32[]{:S(2)}, u32[]{:S(2)}) collective-permute-start(bf16[4,160,128]{2,1,0:T(8,128)(2,1)S(1)} %get-tuple-element.43), channel_id=1, source_target_pairs={{0,1},{1,2},{2,3},{3,4},{4,5},{5,6},{6,7},{7,8},{8,9},{9,10},{10,1... | collective-permute-start | bytes 491528 | tf_op jit(solution)/shard_map/ppermute | solution.py:29
  20.0 1.9 collective-permute-start.3
  21.9 4.4 %pack.1 = bf16[128,264,128]{2,1,0:T(8,128)(2,1)} custom-call(s32[128]{0:T(128)} %bitcast.23, bf16[128,128,128]{2,1,0:T(8,128)(2,1)} %tiles_ref.1, bf16[128,8,128]{2,1,0:T(8,128)(2,1)} %select_convert_fusion.labels_ref), custom_call_target="tpu_custom_call" | custom-call | tf_op jit(solution)/shard_map/pack/pallas_call | solution.py:78
  26.3 0.0 copy-start.14
  26.3 0.7 copy-done.14
  27.0 0.5 collective-permute-done.3.right_ref
  27.5 0.7 copy-done.16
  28.2 10.6 %all-to-all-start = ((bf16[128,264,128]{2,1,0:T(8,128)(2,1)}), bf16[128,264,128]{2,1,0:T(8,128)(2,1)}, u32[]{:S(2)}, u32[]{:S(2)}) async-start(bf16[128,264,128]{2,1,0:T(8,128)(2,1)} %pack.1), calls=%async_computation | async-start | bytes 17301504 | tf_op jit(solution)/shard_map/all_to_all | solution.py:652
  38.8 0.1 reduce_sum.9
  38.9 0.1 copy.31
  39.0 0.1 fusion.15
  39.1 0.1 subtract_add_fusion.4
  39.2 0.5 fusion.6
  39.7 1.0 copy.34.wy_ref
  40.7 0.1 subtract_add_fusion.3
  40.8 0.5 fusion.7
  41.4 0.1 pad_add_fusion
  41.5 0.1 subtract_add_fusion.2
  41.6 0.8 fusion.14
  42.3 0.3 copy.33
  42.6 0.9 copy.36.wx_ref
  43.6 0.8 fusion.12
  44.3 0.1 copy.37
  44.4 0.1 compare_select_fusion
  44.7 1.4 fusion.1
  46.1 0.2 copy.47.bz_ref
  46.2 1.4 fusion
  47.7 0.2 copy.48.wz_ref
  47.9 7.9 %forward.1.blur_ref = f32[6,8,256,256]{3,2,1,0:T(8,128)S(1)} custom-call(f32[32,128,128]{2,1,0:T(8,128)S(1)} %copy-done, bf16[32,16,128]{2,1,0:T(8,128)(2,1)S(1)} %copy-done.9, bf16[32,16,128]{2,1,0:T(8,128)(2,1)S(1)} %copy-done.12, bf16[4,160,128]{2,1,0:T(8,128)(2,1)S(1)} %copy-done.15, bf16[4,160,128]{2,1,0:T(8,128)(2,1)S(1)} %copy-done.17, ...), custom_call_target="tpu_custom_call" | custom-call | tf_op jit(solution)/shard_map/forward/pallas_call | solution.py:376
  55.8 4.5 %copy-done.1 = f32[6,8,256,256]{3,2,1,0:T(8,128)} copy-done((f32[6,8,256,256]{3,2,1,0:T(8,128)}, f32[6,8,256,256]{3,2,1,0:T(8,128)S(1)}, u32[]{:S(2)}) %copy-start.1) | copy-done | bytes 12582936
  60.3 0.9 copy-done.2
  61.2 81.1 %all-to-all-done.got_ref = bf16[128,264,128]{2,1,0:T(8,128)(2,1)} async-done(((bf16[128,264,128]{2,1,0:T(8,128)(2,1)}), bf16[128,264,128]{2,1,0:T(8,128)(2,1)}, u32[]{:S(2)}, u32[]{:S(2)}) %all-to-all-start) | async-done | bytes 8650784 | tf_op jit(solution)/shard_map/all_to_all | solution.py:652
  142.2 20.3 %backward.1 = (f32[32,128,128]{2,1,0:T(8,128)S(1)}, f32[32,16,128]{2,1,0:T(8,128)S(1)}, f32[32,16,128]{2,1,0:T(8,128)S(1)}, s16[4,160,128]{2,1,0:T(8,128)(2,1)S(...) custom-call(bf16[128,264,128]{2,1,0:T(8,128)(2,1)} %all-to-all-done.got_ref, ...), custom_call_target="tpu_custom_call" | custom-call | tf_op jit(solution)/shard_map/backward/pallas_call | solution.py:390
  162.6 14.1 %collective-permute-start.4 = (s16[4,160,128]{2,1,0:T(8,128)(2,1)S(1)}, s16[4,160,128]{2,1,0:T(8,128)(2,1)S(1)}, u32[]{:S(2)}, u32[]{:S(2)}) collective-permute-start(s16[4,160,128]{2,1,0:T(8,128)(2,1)S(1)} %get-tuple-element.49), channel_id=1, source_target_pairs={{0,1},{1,2},{2,3},{3,4},{4,5},{5,6},{6,7},{7,8},{8,9},{9,10},{10,1... | collective-permute-start | bytes 491528 | tf_op jit(solution)/shard_map/ppermute | solution.py:29
  176.7 1.9 collective-permute-start.5
  178.6 0.3 collective-permute-done.4.left_ref
  178.9 5.3 %collective-permute-done.5.right_ref = s16[4,160,128]{2,1,0:T(8,128)(2,1)S(1)} collective-permute-done((s16[4,160,128]{2,1,0:T(8,128)(2,1)S(1)}, s16[4,160,128]{2,1,0:T(8,128)(2,1)S(1)}, u32[]{:S(2)}, u32[]{:S(2)}) %collective-permute-start.5) | collective-permute-done | bytes 163872 | tf_op jit(solution)/shard_map/ppermute | solution.py:29
  184.2 0.7 join_x.2
  184.9 1.9 collective-permute-start.6
  186.9 4.9 %collective-permute-start.7 = (s16[64,16,128]{2,1,0:T(8,128)(2,1)S(1)}, s16[64,16,128]{2,1,0:T(8,128)(2,1)S(1)}, u32[]{:S(2)}, u32[]{:S(2)}) collective-permute-start(s16[64,16,128]{2,1,0:T(8,128)(2,1)S(1)} %get-tuple-element.54), channel_id=1, source_target_pairs={{16,0},{32,16},{48,32},{64,48},{80,64},{96,80},{112,96},{17,1},{33... | collective-permute-start | bytes 786440 | tf_op jit(solution)/shard_map/ppermute | solution.py:29
  191.8 1.8 collective-permute-done.6.above_ref
  193.6 2.8 %collective-permute-done.7.below_ref = s16[64,16,128]{2,1,0:T(8,128)(2,1)S(1)} collective-permute-done((s16[64,16,128]{2,1,0:T(8,128)(2,1)S(1)}, s16[64,16,128]{2,1,0:T(8,128)(2,1)S(1)}, u32[]{:S(2)}, u32[]{:S(2)}) %collective-permute-start.7) | collective-permute-done | bytes 262176 | tf_op jit(solution)/shard_map/ppermute | solution.py:29
  196.4 1.7 next_join.1
  198.1 4.3 %collective-permute-start.8 = (bf16[4,160,128]{2,1,0:T(8,128)(2,1)S(1)}, bf16[4,160,128]{2,1,0:T(8,128)(2,1)S(1)}, u32[]{:S(2)}, u32[]{:S(2)}) collective-permute-start(bf16[4,160,128]{2,1,0:T(8,128)(2,1)S(1)} %get-tuple-element.60), channel_id=1, source_target_pairs={{0,1},{1,2},{2,3},{3,4},{4,5},{5,6},{6,7},{7,8},{8,9},{9,10},{10,1... | collective-permute-start | bytes 491528 | tf_op jit(solution)/shard_map/ppermute | solution.py:29
  202.4 1.9 collective-permute-start.9
  204.3 1.8 collective-permute-done.8.left_ref
  206.1 3.8 %collective-permute-done.9.right_ref = bf16[4,160,128]{2,1,0:T(8,128)(2,1)S(1)} collective-permute-done((bf16[4,160,128]{2,1,0:T(8,128)(2,1)S(1)}, bf16[4,160,128]{2,1,0:T(8,128)(2,1)S(1)}, u32[]{:S(2)}, u32[]{:S(2)}) %collective-permute-start.9) | collective-permute-done | bytes 163872 | tf_op jit(solution)/shard_map/ppermute | solution.py:29
  210.0 15.6 %iterate.1 = (f32[32,128,128]{2,1,0:T(8,128)S(1)}, f32[32,16,128]{2,1,0:T(8,128)S(1)}, f32[32,16,128]{2,1,0:T(8,128)S(1)}, s16[4,160,128]{2,1,0:T(8,128)(2,1)S(1)}, s16[4,160,128]{2,1,0:T(8,128)(2,1)S(1)}) custom-call(f32[32,128,128]{2,1,0:T(8,128)S(1)} %get-tuple-element.57.est_ref, bf16[32,16,128]{2,1,0:T(8,128)(2,1)S(1)} %get-tuple-element.58.top_ref, ...), custom_call_target="tpu_custom_call" | custom-call | tf_op jit(solution)/shard_map/iterate/pallas_call | solution.py:419
  225.5 1.9 collective-permute-start.10
  227.5 2.4 collective-permute-start.11
  229.9 5.1 %collective-permute-done.11.right_ref = s16[4,160,128]{2,1,0:T(8,128)(2,1)S(1)} collective-permute-done((s16[4,160,128]{2,1,0:T(8,128)(2,1)S(1)}, s16[4,160,128]{2,1,0:T(8,128)(2,1)S(1)}, u32[]{:S(2)}, u32[]{:S(2)}) %collective-permute-start.11) | collective-permute-done | bytes 163872 | tf_op jit(solution)/shard_map/ppermute | solution.py:29
  235.0 0.4 join_x.3
  235.4 3.6 %collective-permute-start.12 = (s16[32,16,128]{2,1,0:T(8,128)(2,1)S(1)}, s16[32,16,128]{2,1,0:T(8,128)(2,1)S(1)}, u32[]{:S(2)}, u32[]{:S(2)}) collective-permute-start(s16[32,16,128]{2,1,0:T(8,128)(2,1)S(1)} %get-tuple-element.69), channel_id=1, source_target_pairs={{0,16},{16,32},{32,48},{48,64},{64,80},{80,96},{96,112},{1,17},{17... | collective-permute-start | bytes 393224 | tf_op jit(solution)/shard_map/ppermute | solution.py:29
  239.0 3.2 %collective-permute-start.13 = (s16[32,16,128]{2,1,0:T(8,128)(2,1)S(1)}, s16[32,16,128]{2,1,0:T(8,128)(2,1)S(1)}, u32[]{:S(2)}, u32[]{:S(2)}) collective-permute-start(s16[32,16,128]{2,1,0:T(8,128)(2,1)S(1)} %get-tuple-element.70), channel_id=1, source_target_pairs={{16,0},{32,16},{48,32},{64,48},{80,64},{96,80},{112,96},{17,1},{33... | collective-permute-start | bytes 393224 | tf_op jit(solution)/shard_map/ppermute | solution.py:29
  242.2 0.4 collective-permute-done.12.above_ref
  242.6 4.5 %collective-permute-done.13.below_ref = s16[32,16,128]{2,1,0:T(8,128)(2,1)S(1)} collective-permute-done((s16[32,16,128]{2,1,0:T(8,128)(2,1)S(1)}, s16[32,16,128]{2,1,0:T(8,128)(2,1)S(1)}, u32[]{:S(2)}, u32[]{:S(2)}) %collective-permute-start.13) | collective-permute-done | bytes 131104 | tf_op jit(solution)/shard_map/ppermute | solution.py:29
  247.1 2.4 last_join.1
  (51 shorter events, 0.2 us)
Async XLA Ops:
  0.0 14.6 %copy-start = (f32[32,128,128]{2,1,0:T(8,128)S(1)}, f32[32,128,128]{2,1,0:T(8,128)}, u32[]{:S(2)}) copy-start(f32[32,128,128]{2,1,0:T(8,128)} %est_ref.5) | copy-start | bytes 6291460
  0.0 8.7 %copy-start.20 = (s32[128]{0:T(128)S(1)}, s32[128]{0:T(128)}, u32[]{:S(2)}) copy-start(s32[128]{0:T(128)} %param.7) | copy-start | bytes 1540
  0.0 8.8 %copy-start.19 = (s32[128,1]{0,1:T(1,128)S(1)}, s32[128,1]{0,1:T(1,128)}, u32[]{:S(2)}) copy-start(s32[128,1]{0,1:T(1,128)} %param.6) | copy-start | bytes 1540
  1.9 8.0 %collective-permute-start = (bf16[32,16,128]{2,1,0:T(8,128)(2,1)}, bf16[32,16,128]{2,1,0:T(8,128)(2,1)S(1)}, u32[]{:S(2)}, u32[]{:S(2)}) collective-permute-start(bf16[32,16,128]{2,1,0:T(8,128)(2,1)} %get-tuple-element.38), channel_id=1, source_target_pairs={{0,16},{16,32},{32,48},{48,64},{64,80},{80,96},{96,112},{1,17},{17... | collective-permute-start | bytes 393224 | tf_op jit(solution)/shard_map/ppermute | solution.py:29
  6.3 8.3 %collective-permute-start.1 = (bf16[32,16,128]{2,1,0:T(8,128)(2,1)}, bf16[32,16,128]{2,1,0:T(8,128)(2,1)S(1)}, u32[]{:S(2)}, u32[]{:S(2)}) collective-permute-start(bf16[32,16,128]{2,1,0:T(8,128)(2,1)} %get-tuple-element.39), channel_id=1, source_target_pairs={{16,0},{32,16},{48,32},{64,48},{80,64},{96,80},{112,96},{17,1},{33... | collective-permute-start | bytes 393224 | tf_op jit(solution)/shard_map/ppermute | solution.py:29
  10.0 16.3 %copy-start.8 = (bf16[32,16,128]{2,1,0:T(8,128)(2,1)}, bf16[32,16,128]{2,1,0:T(8,128)(2,1)S(1)}, u32[]{:S(2)}) copy-start(bf16[32,16,128]{2,1,0:T(8,128)(2,1)S(1)} %collective-permute-done.top_ref) | copy-start | bytes 393220
  14.6 11.7 %copy-start.11 = (bf16[32,16,128]{2,1,0:T(8,128)(2,1)}, bf16[32,16,128]{2,1,0:T(8,128)(2,1)S(1)}, u32[]{:S(2)}) copy-start(bf16[32,16,128]{2,1,0:T(8,128)(2,1)S(1)} %collective-permute-done.1.bot_ref) | copy-start | bytes 393220
  15.4 10.9 %collective-permute-start.2 = (bf16[4,160,128]{2,1,0:T(8,128)(2,1)S(1)}, bf16[4,160,128]{2,1,0:T(8,128)(2,1)S(1)}, u32[]{:S(2)}, u32[]{:S(2)}) collective-permute-start(bf16[4,160,128]{2,1,0:T(8,128)(2,1)S(1)} %get-tuple-element.43), channel_id=1, source_target_pairs={{0,1},{1,2},{2,3},{3,4},{4,5},{5,6},{6,7},{7,8},{8,9},{9,10},{10,1... | collective-permute-start | bytes 491528 | tf_op jit(solution)/shard_map/ppermute | solution.py:29
  20.0 7.5 %collective-permute-start.3 = (bf16[4,160,128]{2,1,0:T(8,128)(2,1)S(1)}, bf16[4,160,128]{2,1,0:T(8,128)(2,1)S(1)}, u32[]{:S(2)}, u32[]{:S(2)}) collective-permute-start(bf16[4,160,128]{2,1,0:T(8,128)(2,1)S(1)} %get-tuple-element.44), channel_id=1, source_target_pairs={{1,0},{2,1},{3,2},{4,3},{5,4},{6,5},{7,6},{8,7},{9,8},{10,9},{11,1... | collective-permute-start | bytes 491528 | tf_op jit(solution)/shard_map/ppermute | solution.py:29
  26.3 12.5 %copy-start.18 = (f32[6,3,31]{2,1,0:T(4,128)S(1)}, f32[6,3,31]{2,1,0:T(4,128)}, u32[]{:S(2)}) copy-start(f32[6,3,31]{2,1,0:T(4,128)} %param.8) | copy-start | bytes 6700
  26.3 0.7 copy-start.14
  27.5 0.7 copy-start.16
  28.2 114.1 %all-to-all-start = ((bf16[128,264,128]{2,1,0:T(8,128)(2,1)}), bf16[128,264,128]{2,1,0:T(8,128)(2,1)}, u32[]{:S(2)}, u32[]{:S(2)}) async-start(bf16[128,264,128]{2,1,0:T(8,128)(2,1)} %pack.1), calls=%async_computation | async-start | bytes 17301504 | tf_op jit(solution)/shard_map/all_to_all | solution.py:652
  44.6 3.3 %copy-start.4 = (bf16[256,768]{1,0:T(8,128)(2,1)S(1)}, bf16[256,768]{1,0:T(8,128)(2,1)}, u32[]{:S(2)}) copy-start(bf16[256,768]{1,0:T(8,128)(2,1)} %copy.36.wx_ref) | copy-start | bytes 1179652
  44.6 3.3 %copy-start.6 = (bf16[6,128,160]{2,1,0:T(8,128)(2,1)S(1)}, bf16[6,128,160]{2,1,0:T(8,128)(2,1)}, u32[]{:S(2)}) copy-start(bf16[6,128,160]{2,1,0:T(8,128)(2,1)} %copy.34.wy_ref) | copy-start | bytes 737284
  44.6 3.3 %copy-start.9 = (bf16[32,16,128]{2,1,0:T(8,128)(2,1)S(1)}, bf16[32,16,128]{2,1,0:T(8,128)(2,1)}, u32[]{:S(2)}) copy-start(bf16[32,16,128]{2,1,0:T(8,128)(2,1)} %copy-done.8) | copy-start | bytes 393220
  44.6 3.3 %copy-start.12 = (bf16[32,16,128]{2,1,0:T(8,128)(2,1)S(1)}, bf16[32,16,128]{2,1,0:T(8,128)(2,1)}, u32[]{:S(2)}) copy-start(bf16[32,16,128]{2,1,0:T(8,128)(2,1)} %copy-done.11) | copy-start | bytes 393220
  44.6 3.3 %copy-start.15 = (bf16[4,160,128]{2,1,0:T(8,128)(2,1)S(1)}, bf16[4,160,128]{2,1,0:T(8,128)(2,1)}, u32[]{:S(2)}) copy-start(bf16[4,160,128]{2,1,0:T(8,128)(2,1)} %copy-done.14) | copy-start | bytes 491524
  44.6 3.3 %copy-start.17 = (bf16[4,160,128]{2,1,0:T(8,128)(2,1)S(1)}, bf16[4,160,128]{2,1,0:T(8,128)(2,1)}, u32[]{:S(2)}) copy-start(bf16[4,160,128]{2,1,0:T(8,128)(2,1)} %copy-done.16) | copy-start | bytes 491524
  55.8 4.5 %copy-start.1 = (f32[6,8,256,256]{3,2,1,0:T(8,128)}, f32[6,8,256,256]{3,2,1,0:T(8,128)S(1)}, u32[]{:S(2)}) copy-start(f32[6,8,256,256]{3,2,1,0:T(8,128)S(1)} %forward.1.blur_ref) | copy-start | bytes 37748740
  60.3 0.9 copy-start.2
  162.6 33.8 %copy-start.10 = (bf16[32,16,128]{2,1,0:T(8,128)(2,1)S(1)}, bf16[32,16,128]{2,1,0:T(8,128)(2,1)}, u32[]{:S(2)}) copy-start(bf16[32,16,128]{2,1,0:T(8,128)(2,1)} %copy-done.8) | copy-start | bytes 393220
  162.6 33.8 %copy-start.13 = (bf16[32,16,128]{2,1,0:T(8,128)(2,1)S(1)}, bf16[32,16,128]{2,1,0:T(8,128)(2,1)}, u32[]{:S(2)}) copy-start(bf16[32,16,128]{2,1,0:T(8,128)(2,1)} %copy-done.11) | copy-start | bytes 393220
  162.6 16.3 %collective-permute-start.4 = (s16[4,160,128]{2,1,0:T(8,128)(2,1)S(1)}, s16[4,160,128]{2,1,0:T(8,128)(2,1)S(1)}, u32[]{:S(2)}, u32[]{:S(2)}) collective-permute-start(s16[4,160,128]{2,1,0:T(8,128)(2,1)S(1)} %get-tuple-element.49), channel_id=1, source_target_pairs={{0,1},{1,2},{2,3},{3,4},{4,5},{5,6},{6,7},{7,8},{8,9},{9,10},{10,1... | collective-permute-start | bytes 491528 | tf_op jit(solution)/shard_map/ppermute | solution.py:29
  176.7 7.5 %collective-permute-start.5 = (s16[4,160,128]{2,1,0:T(8,128)(2,1)S(1)}, s16[4,160,128]{2,1,0:T(8,128)(2,1)S(1)}, u32[]{:S(2)}, u32[]{:S(2)}) collective-permute-start(s16[4,160,128]{2,1,0:T(8,128)(2,1)S(1)} %get-tuple-element.50), channel_id=1, source_target_pairs={{1,0},{2,1},{3,2},{4,3},{5,4},{6,5},{7,6},{8,7},{9,8},{10,9},{11,1... | collective-permute-start | bytes 491528 | tf_op jit(solution)/shard_map/ppermute | solution.py:29
  184.2 25.7 %copy-start.3 = (bf16[6,256,256]{2,1,0:T(8,128)(2,1)S(1)}, bf16[6,256,256]{2,1,0:T(8,128)(2,1)}, u32[]{:S(2)}) copy-start(bf16[6,256,256]{2,1,0:T(8,128)(2,1)} %copy-done.2) | copy-start | bytes 2359300
  184.2 25.7 %copy-start.5 = (bf16[256,768]{1,0:T(8,128)(2,1)S(1)}, bf16[256,768]{1,0:T(8,128)(2,1)}, u32[]{:S(2)}) copy-start(bf16[256,768]{1,0:T(8,128)(2,1)} %copy.36.wx_ref) | copy-start | bytes 1179652
  184.2 25.7 %copy-start.7 = (bf16[6,128,160]{2,1,0:T(8,128)(2,1)S(1)}, bf16[6,128,160]{2,1,0:T(8,128)(2,1)}, u32[]{:S(2)}) copy-start(bf16[6,128,160]{2,1,0:T(8,128)(2,1)} %copy.34.wy_ref) | copy-start | bytes 737284
  184.9 8.6 %collective-permute-start.6 = (s16[64,16,128]{2,1,0:T(8,128)(2,1)S(1)}, s16[64,16,128]{2,1,0:T(8,128)(2,1)S(1)}, u32[]{:S(2)}, u32[]{:S(2)}) collective-permute-start(s16[64,16,128]{2,1,0:T(8,128)(2,1)S(1)} %get-tuple-element.53), channel_id=1, source_target_pairs={{0,16},{16,32},{32,48},{48,64},{64,80},{80,96},{96,112},{1,17},{17... | collective-permute-start | bytes 786440 | tf_op jit(solution)/shard_map/ppermute | solution.py:29
  186.9 9.5 %collective-permute-start.7 = (s16[64,16,128]{2,1,0:T(8,128)(2,1)S(1)}, s16[64,16,128]{2,1,0:T(8,128)(2,1)S(1)}, u32[]{:S(2)}, u32[]{:S(2)}) collective-permute-start(s16[64,16,128]{2,1,0:T(8,128)(2,1)S(1)} %get-tuple-element.54), channel_id=1, source_target_pairs={{16,0},{32,16},{48,32},{64,48},{80,64},{96,80},{112,96},{17,1},{33... | collective-permute-start | bytes 786440 | tf_op jit(solution)/shard_map/ppermute | solution.py:29
  198.1 8.0 %collective-permute-start.8 = (bf16[4,160,128]{2,1,0:T(8,128)(2,1)S(1)}, bf16[4,160,128]{2,1,0:T(8,128)(2,1)S(1)}, u32[]{:S(2)}, u32[]{:S(2)}) collective-permute-start(bf16[4,160,128]{2,1,0:T(8,128)(2,1)S(1)} %get-tuple-element.60), channel_id=1, source_target_pairs={{0,1},{1,2},{2,3},{3,4},{4,5},{5,6},{6,7},{7,8},{8,9},{9,10},{10,1... | collective-permute-start | bytes 491528 | tf_op jit(solution)/shard_map/ppermute | solution.py:29
  202.4 7.5 %collective-permute-start.9 = (bf16[4,160,128]{2,1,0:T(8,128)(2,1)S(1)}, bf16[4,160,128]{2,1,0:T(8,128)(2,1)S(1)}, u32[]{:S(2)}, u32[]{:S(2)}) collective-permute-start(bf16[4,160,128]{2,1,0:T(8,128)(2,1)S(1)} %get-tuple-element.61), channel_id=1, source_target_pairs={{1,0},{2,1},{3,2},{4,3},{5,4},{6,5},{7,6},{8,7},{9,8},{10,9},{11,1... | collective-permute-start | bytes 491528 | tf_op jit(solution)/shard_map/ppermute | solution.py:29
  225.5 4.3 %collective-permute-start.10 = (s16[4,160,128]{2,1,0:T(8,128)(2,1)S(1)}, s16[4,160,128]{2,1,0:T(8,128)(2,1)S(1)}, u32[]{:S(2)}, u32[]{:S(2)}) collective-permute-start(s16[4,160,128]{2,1,0:T(8,128)(2,1)S(1)} %get-tuple-element.65), channel_id=1, source_target_pairs={{0,1},{1,2},{2,3},{3,4},{4,5},{5,6},{6,7},{7,8},{8,9},{9,10},{10,1... | collective-permute-start | bytes 491528 | tf_op jit(solution)/shard_map/ppermute | solution.py:29
  227.5 7.5 %collective-permute-start.11 = (s16[4,160,128]{2,1,0:T(8,128)(2,1)S(1)}, s16[4,160,128]{2,1,0:T(8,128)(2,1)S(1)}, u32[]{:S(2)}, u32[]{:S(2)}) collective-permute-start(s16[4,160,128]{2,1,0:T(8,128)(2,1)S(1)} %get-tuple-element.66), channel_id=1, source_target_pairs={{1,0},{2,1},{3,2},{4,3},{5,4},{6,5},{7,6},{8,7},{9,8},{10,9},{11,1... | collective-permute-start | bytes 491528 | tf_op jit(solution)/shard_map/ppermute | solution.py:29
  235.4 7.2 %collective-permute-start.12 = (s16[32,16,128]{2,1,0:T(8,128)(2,1)S(1)}, s16[32,16,128]{2,1,0:T(8,128)(2,1)S(1)}, u32[]{:S(2)}, u32[]{:S(2)}) collective-permute-start(s16[32,16,128]{2,1,0:T(8,128)(2,1)S(1)} %get-tuple-element.69), channel_id=1, source_target_pairs={{0,16},{16,32},{32,48},{48,64},{64,80},{80,96},{96,112},{1,17},{17... | collective-permute-start | bytes 393224 | tf_op jit(solution)/shard_map/ppermute | solution.py:29
  239.0 8.1 %collective-permute-start.13 = (s16[32,16,128]{2,1,0:T(8,128)(2,1)S(1)}, s16[32,16,128]{2,1,0:T(8,128)(2,1)S(1)}, u32[]{:S(2)}, u32[]{:S(2)}) collective-permute-start(s16[32,16,128]{2,1,0:T(8,128)(2,1)S(1)} %get-tuple-element.70), channel_id=1, source_target_pairs={{16,0},{32,16},{48,32},{64,48},{80,64},{96,80},{112,96},{17,1},{33... | collective-permute-start | bytes 393224 | tf_op jit(solution)/shard_map/ppermute | solution.py:29
